TPU v7x, 128 devices: a whole 4x4x4 slice. The times are simulated.
128 devices in a mesh: blk: 8 (over z, y_hi), grp: 16 (over y_lo, x, core).
Axes of the slice: x: 4, y: 4 (y_hi: 2, y_lo: 2; y = y_hi * 2 + y_lo), z: 4, core: 2. Of those that a mesh axis runs over, the one named last changes fastest.
Arguments:
- obj_query: bfloat16 [8192, 1536], P(('blk', 'grp')), may hold values from -64 to 64
- grad_out: bfloat16 [8192, 1536], P(('blk', 'grp')), may hold values from -256 to 256
- pattern_key: bfloat16 [8192, 1536], P('grp'), may hold values from -4.5 to 4.5
- pattern_value: bfloat16 [8192, 1536], P('grp'), may hold values from -6 to 6
- pencil_order: int32 [512], replicated, may hold values from 0 to 511, as said below
Outputs:
- query_grad: bfloat16 [8192, 1536], P(('blk', 'grp'))
- key_grad: bfloat16 [8192, 1536], P(('blk', 'grp'))
- value_grad: bfloat16 [8192, 1536], P(('blk', 'grp'))
Inputs may be any that keep to these rules, and one draw needn't show every extreme that they name: pencil_order is a permutation of 0 to 511. With c the number of devices along grp, block r of the encoder's layout lies on the device of index r // 4 of the axes blk+grp, and pencil_order[r] names a block of pattern rows g * 512 to (g + 1) * 512 - 1, where g is that device index mod c.
All inputs are finite; a program needn't handle non-finite values.
Results may differ from a plain program's by a relative error of at most 0.0051.
Values may be sent and summed in bfloat16 or wider, within the bound.
No kernel may reach another device: no remote copies, remote signals or barrier semaphores. Data moves between devices by JAX's collectives and lax.ppermute only.
A program may use at most 128 MiB of HBM per device.

v0:
```python
import math

import jax
import jax.numpy as jnp
from jax import lax
from jax.sharding import Mesh
from jax.sharding import PartitionSpec as P

H = 16
PENCIL = 16
GRP = ("grp_0", "grp_1", "grp_2")
BLK = ("blk_0", "blk_1")
BLK_GRP = ("blk_0", "blk_1", "grp_0", "grp_1", "grp_2")


def sent_together(arrays, axis, dim, along):
    widths = [a.shape[along] for a in arrays]
    both = jnp.concatenate(arrays, axis=along)
    result = lax.all_gather(both, axis, axis=dim, tiled=True)
    return tuple(jnp.split(result, [sum(widths[:k]) for k in range(1, len(widths))], axis=along))


def all_in_one(value, axis):
    leaves = jax.tree.leaves(value)
    turns = sorted(range(len(leaves)), key=lambda k: -leaves[k].size)
    width = (1, *leaves[turns[0]].shape)[-1]
    lines = [
        jnp.pad(leaves[k].reshape(-1), (0, -leaves[k].size % width)).reshape(-1, width)
        for k in turns
    ]
    both, at, found = (lax.all_gather(jnp.concatenate(lines), axis), 0, {})
    for k, line in zip(turns, lines):
        piece = both[:, at : at + len(line)].reshape(len(both), -1)
        found[k] = piece[:, : leaves[k].size].reshape(-1, *leaves[k].shape)
        at += len(line)
    numbers = iter(range(len(leaves)))
    return jax.tree.map(lambda _: found[next(numbers)], value)


def combined_by_axis(value, axes, combine):
    for axis in axes:
        pieces = all_in_one(value, axis)
        value = jax.tree.map(lambda part: part[0], pieces)
        for k in range(1, lax.axis_size(axis)):
            value = combine(value, jax.tree.map(lambda part: part[k], pieces))
    return value


def summed_rows(so_far, axes):
    for axis in axes:
        so_far = lax.psum_scatter(so_far, axis, scatter_dimension=0, tiled=True)
    return so_far


def split_heads(matrix):
    return matrix.reshape(matrix.shape[0], H, matrix.shape[1] // H)


def block_stats(part_query, part_grad, key_block, value_block):
    scaling = 1.0 / math.sqrt(key_block.shape[1] // H)
    scores = (
        jnp.einsum(
            "rhd,chd->hrc",
            split_heads(part_query),
            split_heads(key_block),
            preferred_element_type=jnp.float32,
        )
        * scaling
    )
    prob_grad = jnp.einsum(
        "rhd,chd->hrc",
        split_heads(part_grad),
        split_heads(value_block),
        preferred_element_type=jnp.float32,
    )
    highest = jnp.max(scores, axis=2)
    weights = jnp.exp(scores - highest[:, :, None])
    return (highest, jnp.sum(weights, axis=2), jnp.sum(weights * prob_grad, axis=2))


def join_stats(earlier, later):
    highest = jnp.maximum(earlier[0], later[0])
    before = jnp.exp(earlier[0] - highest)
    after = jnp.exp(later[0] - highest)
    return (highest, earlier[1] * before + later[1] * after, earlier[2] * before + later[2] * after)


def stats_of_rows(queries, grads, key_block, value_block):
    amount, features = queries.shape
    blocking = math.gcd(amount, 128)

    def one_block(couple):
        return block_stats(couple[0], couple[1], key_block, value_block)

    stacked = lax.map(
        one_block,
        (
            queries.reshape(amount // blocking, blocking, features),
            grads.reshape(amount // blocking, blocking, features),
        ),
    )
    return tuple((jnp.moveaxis(member, 0, 1).reshape(H, amount) for member in stacked))


def block_grads(part_query, part_grad, log_now, mean_now, key_block, value_block):
    features = key_block.shape[1]
    scaling = 1.0 / math.sqrt(features // H)
    query_heads = split_heads(part_query)
    grad_heads = split_heads(part_grad)
    key_heads = split_heads(key_block)
    value_heads = split_heads(value_block)
    scores = (
        jnp.einsum("rhd,chd->hrc", query_heads, key_heads, preferred_element_type=jnp.float32)
        * scaling
    )
    prob_grad = jnp.einsum(
        "rhd,chd->hrc", grad_heads, value_heads, preferred_element_type=jnp.float32
    )
    softmax = jnp.exp(scores - log_now[:, :, None])
    softmax_low = softmax.astype(jnp.bfloat16)
    score_grad = (scaling * softmax * (prob_grad - mean_now[:, :, None])).astype(jnp.bfloat16)
    query_term = jnp.einsum(
        "hrc,chd->rhd", score_grad, key_heads, preferred_element_type=jnp.float32
    ).reshape(part_query.shape[0], features)
    key_term = jnp.einsum(
        "hrc,rhd->chd", score_grad, query_heads, preferred_element_type=jnp.float32
    ).reshape(key_block.shape[0], features)
    value_term = jnp.einsum(
        "hrc,rhd->chd", softmax_low, grad_heads, preferred_element_type=jnp.float32
    ).reshape(key_block.shape[0], features)
    return (query_term, key_term, value_term)


def on_device(obj_query, grad_out, pattern_key, pattern_value, pencil_order):
    amount, features = obj_query.shape
    columns = pattern_key.shape[0]
    groups = lax.axis_size(GRP)
    position = lax.axis_index(GRP)
    group_rows = groups * amount
    all_query, all_grad = sent_together((obj_query, grad_out), GRP, 0, 1)
    partial_value = stats_of_rows(all_query, all_grad, pattern_key, pattern_value)
    highest, totals, weighted = combined_by_axis(partial_value, GRP, join_stats)
    log_totals = highest + jnp.log(totals)
    mean_grads = weighted / totals
    blocking = math.gcd(group_rows, 128)
    sweeps = group_rows // blocking

    def sweep(carried, segment):
        keys_acc, values_acc = carried
        query_term, key_term, value_term = block_grads(
            segment[0], segment[1], segment[2], segment[3], pattern_key, pattern_value
        )
        return ((keys_acc + key_term, values_acc + value_term), query_term)

    log_blocks = jnp.moveaxis(log_totals.reshape(H, sweeps, blocking), 1, 0)
    mean_blocks = jnp.moveaxis(mean_grads.reshape(H, sweeps, blocking), 1, 0)
    zeros_acc = jnp.zeros((columns, features), jnp.float32)
    segments = (
        all_query.reshape(sweeps, blocking, features),
        all_grad.reshape(sweeps, blocking, features),
        log_blocks,
        mean_blocks,
    )
    (keys_acc, values_acc), pieces = lax.scan(sweep, (zeros_acc, zeros_acc), segments)
    query_total = lax.psum_scatter(
        pieces.reshape(group_rows, features), GRP, scatter_dimension=0, tiled=True
    )
    device_rows = columns // lax.axis_size(BLK)
    spots = jnp.arange(columns, dtype=jnp.int32)
    target = (spots // device_rows * groups + position) * device_rows + spots % device_rows
    source = (
        jnp.take(pencil_order, target // PENCIL) * PENCIL + target % PENCIL - position * columns
    )
    combined = summed_rows(
        jnp.concatenate(
            [jnp.take(keys_acc, source, axis=0), jnp.take(values_acc, source, axis=0)], axis=1
        ),
        BLK,
    )
    key_grad = combined[:, :features].astype(jnp.bfloat16)
    value_grad = combined[:, features:].astype(jnp.bfloat16)
    return (query_total.astype(jnp.bfloat16), key_grad, value_grad)


def solution(mesh):
    split = Mesh(mesh.devices.reshape(4, 2, 2, 4, 2), ("blk_0", "blk_1", "grp_0", "grp_1", "grp_2"))
    placed = (P(BLK_GRP, None), P(BLK_GRP, None), P(GRP, None), P(GRP, None), P())
    return jax.shard_map(
        on_device,
        mesh=split,
        in_specs=placed,
        out_specs=(P(BLK_GRP, None), P(BLK_GRP, None), P(BLK_GRP, None)),
        check_vma=False,
    )
```

profile of v0, /device:TPU:1, one launch (start us, length us, event | category | flops | bytes accessed | tf_op | source)
XLA Modules:
  0.0 520.2 jit_solution(6838633641931952430)
XLA Ops:
  12.7 3.5 gather_fusion
  16.3 39.4 %all-gather.5.cloned.1.call-done = bf16[1024,3072]{1,0:T(8,128)(2,1)} async-done(((bf16[64,3072]{1,0:T(8,128)(2,1)}), bf16[1024,3072]{1,0:T(8,128)(2,1)}) %all-gather.5.cloned.1.call-update) | async-done | bytes 6291472 | tf_op jit(solution)/shard_map/all_gather | solution.py:19
  55.6 5.9 %fusion.60 = (bf16[1024,1536]{1,0:T(8,128)(2,1)}, bf16[1024,1536]{1,0:T(8,128)(2,1)}) fusion(bf16[1024,3072]{1,0:T(8,128)(2,1)} %all-gather.5.cloned.1.call-done), kind=kLoop, calls=%fused_computation.152 | loop fusion | bytes 12582912 | tf_op jit(solution)/shard_map/split | solution.py:20
  61.5 4.7 copy.17
  66.3 4.6 copy.22
  70.9 46.8 %while.29 = (s32[]{:T(128)}, f32[8,16,128]{2,1,0:T(8,128)S(1)}, f32[8,16,128]{2,1,0:T(8,128)S(1)}, f32[8,16,128]{2,1,0:T(8,128)S(1)}, bf16[8,128,1536]{1,2,0:T(8...) while((s32[]{:T(128)}, f32[8,16,128]{2,1,0:T(8,128)S(1)}, ...), condition=%wide.region_4.5_spmd, body=%wide.region_0.4_spmd.sunk | while | flops 412084224 | bytes 18178164 | solution.py:95
  117.8 6.8 %all-gather = f32[96,1024]{1,0:T(8,128)S(1)} all-gather(f32[48,1024]{1,0:T(8,128)S(1)} %pad_maximum_fusion.2), channel_id=2, replica_groups=mesh['blk_0'=4,'blk_1'=2,'grp_0'=2,'grp_1'=4,'grp_2'=2] {'grp_0'}, dimensions={0}, use_global_device_ids=true | all-gather | bytes 589824 | tf_op jit(solution)/shard_map/all_gather | solution.py:31
  124.7 12.2 %all-gather.1 = f32[192,1024]{1,0:T(8,128)S(1)} all-gather(f32[48,1024]{1,0:T(8,128)S(1)} %pad_maximum_fusion.3), channel_id=3, replica_groups=mesh['blk_0'=4,'blk_1'=2,'grp_0'=2,'grp_1'=4,'grp_2'=2] {'grp_1'}, dimensions={0}, use_global_device_ids=true | all-gather | bytes 983040 | tf_op jit(solution)/shard_map/all_gather | solution.py:31
  137.0 4.3 all-gather.2
  141.6 178.2 %while.30 = (s32[]{:T(128)}, f32[512,1536]{0,1:T(8,128)}, f32[512,1536]{0,1:T(8,128)}, f32[8,128,1536]{2,1,0:T(8,128)}, bf16[8,128,1536]{1,2,0:T(8,128)(2,1)}, /...) while((s32[]{:T(128)}, f32[512,1536]{0,1:T(8,128)}, ...), condition=%wide.region_6.7_spmd.clone, body=%wide.region_5.6_spmd.clone.sunk | while | flops 1019215872 | bytes 97837504 | solution.py:164
  155.9 4.7 bitcast_add_fusion.3
  175.8 7.4 %bitcast_add_fusion.3 = (f32[512,1536]{0,1:T(8,128)}, f32[512,1536]{0,1:T(8,128)}) fusion(f32[16,96,512]{2,1,0:T(8,128)S(1)} %copy-done.4, f32[512,1536]{0,1:T(8,128)} %get-tuple-element.404, pred[]{:T(512)S(6)} %compare.28, f32[16,96,512]{2,1,0:T(8,128)S(1)} %fusion.117, f32[512,1536]{0,1:T(8,128)} %get-tuple-element.403), kind=kLoop, calls=%fused_computation.15.clone.1 | loop fusion | flops 3145728 | bytes 18874368 | tf_op jit(solution)/shard_map/while/body/eval_jaxpr/add | solution.py:153
  198.4 7.4 %bitcast_add_fusion.3 = (f32[512,1536]{0,1:T(8,128)}, f32[512,1536]{0,1:T(8,128)}) fusion(f32[16,96,512]{2,1,0:T(8,128)S(1)} %copy-done.4, f32[512,1536]{0,1:T(8,128)} %get-tuple-element.404, pred[]{:T(512)S(6)} %compare.28, f32[16,96,512]{2,1,0:T(8,128)S(1)} %fusion.117, f32[512,1536]{0,1:T(8,128)} %get-tuple-element.403), kind=kLoop, calls=%fused_computation.15.clone.1 | loop fusion | flops 3145728 | bytes 18874368 | tf_op jit(solution)/shard_map/while/body/eval_jaxpr/add | solution.py:153
  221.0 7.4 %bitcast_add_fusion.3 = (f32[512,1536]{0,1:T(8,128)}, f32[512,1536]{0,1:T(8,128)}) fusion(f32[16,96,512]{2,1,0:T(8,128)S(1)} %copy-done.4, f32[512,1536]{0,1:T(8,128)} %get-tuple-element.404, pred[]{:T(512)S(6)} %compare.28, f32[16,96,512]{2,1,0:T(8,128)S(1)} %fusion.117, f32[512,1536]{0,1:T(8,128)} %get-tuple-element.403), kind=kLoop, calls=%fused_computation.15.clone.1 | loop fusion | flops 3145728 | bytes 18874368 | tf_op jit(solution)/shard_map/while/body/eval_jaxpr/add | solution.py:153
  243.6 7.4 %bitcast_add_fusion.3 = (f32[512,1536]{0,1:T(8,128)}, f32[512,1536]{0,1:T(8,128)}) fusion(f32[16,96,512]{2,1,0:T(8,128)S(1)} %copy-done.4, f32[512,1536]{0,1:T(8,128)} %get-tuple-element.404, pred[]{:T(512)S(6)} %compare.28, f32[16,96,512]{2,1,0:T(8,128)S(1)} %fusion.117, f32[512,1536]{0,1:T(8,128)} %get-tuple-element.403), kind=kLoop, calls=%fused_computation.15.clone.1 | loop fusion | flops 3145728 | bytes 18874368 | tf_op jit(solution)/shard_map/while/body/eval_jaxpr/add | solution.py:153
  266.2 7.4 %bitcast_add_fusion.3 = (f32[512,1536]{0,1:T(8,128)}, f32[512,1536]{0,1:T(8,128)}) fusion(f32[16,96,512]{2,1,0:T(8,128)S(1)} %copy-done.4, f32[512,1536]{0,1:T(8,128)} %get-tuple-element.404, pred[]{:T(512)S(6)} %compare.28, f32[16,96,512]{2,1,0:T(8,128)S(1)} %fusion.117, f32[512,1536]{0,1:T(8,128)} %get-tuple-element.403), kind=kLoop, calls=%fused_computation.15.clone.1 | loop fusion | flops 3145728 | bytes 18874368 | tf_op jit(solution)/shard_map/while/body/eval_jaxpr/add | solution.py:153
  288.9 7.4 %bitcast_add_fusion.3 = (f32[512,1536]{0,1:T(8,128)}, f32[512,1536]{0,1:T(8,128)}) fusion(f32[16,96,512]{2,1,0:T(8,128)S(1)} %copy-done.4, f32[512,1536]{0,1:T(8,128)} %get-tuple-element.404, pred[]{:T(512)S(6)} %compare.28, f32[16,96,512]{2,1,0:T(8,128)S(1)} %fusion.117, f32[512,1536]{0,1:T(8,128)} %get-tuple-element.403), kind=kLoop, calls=%fused_computation.15.clone.1 | loop fusion | flops 3145728 | bytes 18874368 | tf_op jit(solution)/shard_map/while/body/eval_jaxpr/add | solution.py:153
  311.5 7.4 %bitcast_add_fusion.3 = (f32[512,1536]{0,1:T(8,128)}, f32[512,1536]{0,1:T(8,128)}) fusion(f32[16,96,512]{2,1,0:T(8,128)S(1)} %copy-done.4, f32[512,1536]{0,1:T(8,128)} %get-tuple-element.404, pred[]{:T(512)S(6)} %compare.28, f32[16,96,512]{2,1,0:T(8,128)S(1)} %fusion.117, f32[512,1536]{0,1:T(8,128)} %get-tuple-element.403), kind=kLoop, calls=%fused_computation.15.clone.1 | loop fusion | flops 3145728 | bytes 18874368 | tf_op jit(solution)/shard_map/while/body/eval_jaxpr/add | solution.py:153
  319.8 3.6 copy.29
  325.8 6.5 %gather_fusion.1 = f32[512,1536]{1,0:T(8,128)} fusion(f32[512,1536]{1,0:T(8,128)} %copy.29, s32[1024]{0:T(1024)S(1)} %pad_clamp_fusion), kind=kCustom, calls=%fused_computation.clone | custom fusion | bytes 6293504 | tf_op jit(solution)/shard_map/jit(_take)/gather | solution.py:176
  335.4 3.7 broadcast_select_fusion.1
  343.0 64.4 %reduce-scatter.6.cloned.1.call-done = f32[128,3072]{1,0:T(8,128)} async-done(((f32[512,3072]{1,0:T(8,128)}), f32[128,3072]{1,0:T(8,128)}) %reduce-scatter.6.cloned.1.call-update) | async-done | bytes 1572880 | tf_op jit(solution)/shard_map/reduce_scatter | solution.py:51
  407.5 69.3 %reduce-scatter.4.cloned.1.call-done = f32[64,1536]{1,0:T(8,128)} async-done(((f32[1024,1536]{1,0:T(8,128)}), f32[64,1536]{1,0:T(8,128)}) %reduce-scatter.4.cloned.1.call-update) | async-done | bytes 393232 | tf_op jit(solution)/shard_map/reduce_scatter | solution.py:165
  478.5 33.2 %reduce-scatter.8.cloned.1.call-done = f32[64,3072]{1,0:T(8,128)} async-done(((f32[128,3072]{1,0:T(8,128)}), f32[64,3072]{1,0:T(8,128)}) %reduce-scatter.8.cloned.1.call-update) | async-done | bytes 786448 | tf_op jit(solution)/shard_map/reduce_scatter | solution.py:51
  (352 shorter events, 186.3 us)
Async XLA Ops:
  7.2 48.5 %all-gather.5.cloned.1.call-start = ((), (), s32[]{:S(2)}) async-start(), calls=%async_computation.3 | async-start | bytes 6684672 | tf_op jit(solution)/shard_map/all_gather | solution.py:19
  9.1 398.4 %reduce-scatter.6.cloned.1.call-start = ((), (), s32[]{:S(2)}) async-start(), calls=%async_computation.5 | async-start | bytes 7864320 | tf_op jit(solution)/shard_map/reduce_scatter | solution.py:51
  175.8 8.4 %copy-start.3 = (bf16[512,1536]{0,1:T(8,128)(2,1)S(1)}, bf16[512,1536]{0,1:T(8,128)(2,1)}, u32[]{:S(2)}) copy-start(bf16[512,1536]{0,1:T(8,128)(2,1)} %copy-done.2) | copy-start | bytes 4718596 | tf_op jit(solution)/shard_map/while
  175.8 8.4 %copy-start.6 = (bf16[512,1536]{0,1:T(8,128)(2,1)S(1)}, bf16[512,1536]{0,1:T(8,128)(2,1)}, u32[]{:S(2)}) copy-start(bf16[512,1536]{0,1:T(8,128)(2,1)} %copy-done.5) | copy-start | bytes 4718596 | tf_op jit(solution)/shard_map/while
  175.8 8.4 %copy-start.9 = (f32[8,16,128]{2,0,1:T(8,128)S(1)}, f32[8,16,128]{2,0,1:T(8,128)}, u32[]{:S(2)}) copy-start(f32[8,16,128]{2,0,1:T(8,128)} %copy-done.8) | copy-start | bytes 196612 | tf_op jit(solution)/shard_map/while
  175.8 8.4 %copy-start.11 = (f32[8,16,128]{2,0,1:T(8,128)S(1)}, f32[8,16,128]{2,0,1:T(8,128)}, u32[]{:S(2)}) copy-start(f32[8,16,128]{2,0,1:T(8,128)} %copy-done.10) | copy-start | bytes 196612 | tf_op jit(solution)/shard_map/while
  243.6 8.3 %copy-start.3 = (bf16[512,1536]{0,1:T(8,128)(2,1)S(1)}, bf16[512,1536]{0,1:T(8,128)(2,1)}, u32[]{:S(2)}) copy-start(bf16[512,1536]{0,1:T(8,128)(2,1)} %copy-done.2) | copy-start | bytes 4718596 | tf_op jit(solution)/shard_map/while
  243.6 8.3 %copy-start.6 = (bf16[512,1536]{0,1:T(8,128)(2,1)S(1)}, bf16[512,1536]{0,1:T(8,128)(2,1)}, u32[]{:S(2)}) copy-start(bf16[512,1536]{0,1:T(8,128)(2,1)} %copy-done.5) | copy-start | bytes 4718596 | tf_op jit(solution)/shard_map/while
  243.6 8.3 %copy-start.9 = (f32[8,16,128]{2,0,1:T(8,128)S(1)}, f32[8,16,128]{2,0,1:T(8,128)}, u32[]{:S(2)}) copy-start(f32[8,16,128]{2,0,1:T(8,128)} %copy-done.8) | copy-start | bytes 196612 | tf_op jit(solution)/shard_map/while
  243.6 8.3 %copy-start.11 = (f32[8,16,128]{2,0,1:T(8,128)S(1)}, f32[8,16,128]{2,0,1:T(8,128)}, u32[]{:S(2)}) copy-start(f32[8,16,128]{2,0,1:T(8,128)} %copy-done.10) | copy-start | bytes 196612 | tf_op jit(solution)/shard_map/while
  266.2 8.3 %copy-start.3 = (bf16[512,1536]{0,1:T(8,128)(2,1)S(1)}, bf16[512,1536]{0,1:T(8,128)(2,1)}, u32[]{:S(2)}) copy-start(bf16[512,1536]{0,1:T(8,128)(2,1)} %copy-done.2) | copy-start | bytes 4718596 | tf_op jit(solution)/shard_map/while
  266.2 8.3 %copy-start.6 = (bf16[512,1536]{0,1:T(8,128)(2,1)S(1)}, bf16[512,1536]{0,1:T(8,128)(2,1)}, u32[]{:S(2)}) copy-start(bf16[512,1536]{0,1:T(8,128)(2,1)} %copy-done.5) | copy-start | bytes 4718596 | tf_op jit(solution)/shard_map/while
  266.2 8.3 %copy-start.9 = (f32[8,16,128]{2,0,1:T(8,128)S(1)}, f32[8,16,128]{2,0,1:T(8,128)}, u32[]{:S(2)}) copy-start(f32[8,16,128]{2,0,1:T(8,128)} %copy-done.8) | copy-start | bytes 196612 | tf_op jit(solution)/shard_map/while
  288.8 8.3 %copy-start.3 = (bf16[512,1536]{0,1:T(8,128)(2,1)S(1)}, bf16[512,1536]{0,1:T(8,128)(2,1)}, u32[]{:S(2)}) copy-start(bf16[512,1536]{0,1:T(8,128)(2,1)} %copy-done.2) | copy-start | bytes 4718596 | tf_op jit(solution)/shard_map/while
  288.8 8.3 %copy-start.6 = (bf16[512,1536]{0,1:T(8,128)(2,1)S(1)}, bf16[512,1536]{0,1:T(8,128)(2,1)}, u32[]{:S(2)}) copy-start(bf16[512,1536]{0,1:T(8,128)(2,1)} %copy-done.5) | copy-start | bytes 4718596 | tf_op jit(solution)/shard_map/while
  288.8 8.3 %copy-start.9 = (f32[8,16,128]{2,0,1:T(8,128)S(1)}, f32[8,16,128]{2,0,1:T(8,128)}, u32[]{:S(2)}) copy-start(f32[8,16,128]{2,0,1:T(8,128)} %copy-done.8) | copy-start | bytes 196612 | tf_op jit(solution)/shard_map/while
  288.8 8.3 %copy-start.11 = (f32[8,16,128]{2,0,1:T(8,128)S(1)}, f32[8,16,128]{2,0,1:T(8,128)}, u32[]{:S(2)}) copy-start(f32[8,16,128]{2,0,1:T(8,128)} %copy-done.10) | copy-start | bytes 196612 | tf_op jit(solution)/shard_map/while
  311.5 8.3 %copy-start.3 = (bf16[512,1536]{0,1:T(8,128)(2,1)S(1)}, bf16[512,1536]{0,1:T(8,128)(2,1)}, u32[]{:S(2)}) copy-start(bf16[512,1536]{0,1:T(8,128)(2,1)} %copy-done.2) | copy-start | bytes 4718596 | tf_op jit(solution)/shard_map/while
  311.5 8.3 %copy-start.6 = (bf16[512,1536]{0,1:T(8,128)(2,1)S(1)}, bf16[512,1536]{0,1:T(8,128)(2,1)}, u32[]{:S(2)}) copy-start(bf16[512,1536]{0,1:T(8,128)(2,1)} %copy-done.5) | copy-start | bytes 4718596 | tf_op jit(solution)/shard_map/while
  311.5 8.3 %copy-start.9 = (f32[8,16,128]{2,0,1:T(8,128)S(1)}, f32[8,16,128]{2,0,1:T(8,128)}, u32[]{:S(2)}) copy-start(f32[8,16,128]{2,0,1:T(8,128)} %copy-done.8) | copy-start | bytes 196612 | tf_op jit(solution)/shard_map/while
  311.5 8.3 %copy-start.11 = (f32[8,16,128]{2,0,1:T(8,128)S(1)}, f32[8,16,128]{2,0,1:T(8,128)}, u32[]{:S(2)}) copy-start(f32[8,16,128]{2,0,1:T(8,128)} %copy-done.10) | copy-start | bytes 196612 | tf_op jit(solution)/shard_map/while
  342.2 134.6 %reduce-scatter.4.cloned.1.call-start = ((), (), s32[]{:S(2)}) async-start(), calls=%async_computation.4 | async-start | bytes 6684672 | tf_op jit(solution)/shard_map/reduce_scatter | solution.py:165
  343.0 170.7 %copy-start.1 = (s32[512]{0:T(512)S(1)}, s32[512]{0:T(512)}, u32[]{:S(2)}) copy-start(s32[512]{0:T(512)} %param.15) | copy-start | bytes 6148
  343.0 168.7 %reduce-scatter.8.cloned.1.call-start = ((), (), s32[]{:S(2)}) async-start(), calls=%async_computation.6 | async-start | bytes 2359296 | tf_op jit(solution)/shard_map/reduce_scatter | solution.py:51
  (62 other events, 236.4 us)
Sparse Core Ops, SparseCore 0:
  9.7 45.9 all-gather.4
  342.4 65.0 reduce-scatter.5
  409.9 66.8 reduce-scatter.3
  479.0 32.5 reduce-scatter.7
where the time goes:
time: 523 us; the launch traced here: 520 us
  waiting for transfers between devices  207 us (40%)
  local copies, waits for them, and re-layouts  103 us (20%)
  matrix products  92.7 us (18%)
  other arithmetic  78.6 us (15%)
  blocking collectives  23.3 us (4%)
  between operations  14.1 us (3%)
    reduce_scatter x2, waiting for transfers between devices, summed_rows(): so_far = lax.psum_scatter(so_far, axis, scatter_dimension=0, tiled=True)  97.6 us
    reduce_scatter x1, waiting for transfers between devices, on_device(): lax.psum_scatter(pieces.reshape(group_rows, features), GRP, scatter_dimen...  69.3 us
    add x8, other arithmetic, sweep(): return ((keys_acc + key_term, values_acc + value_term), query_term)  56.2 us
    all_gather x1, waiting for transfers between devices, sent_together(): result = lax.all_gather(both, axis, axis=dim, tiled=True)  39.4 us
    dynamic_slice x32, local copies, waits for them, and re-layouts, stats_of_rows(): lax.map(one_block, (queries.reshape(amount // blocking, blocking, feature...  35.3 us
    dot_general x8, matrix products, block_grads(): jnp.einsum('rhd,chd->hrc', grad_heads, value_heads, preferred_element_typ...  23.9 us
    all_gather x3, blocking collectives, all_in_one(): both, at, found = (lax.all_gather(jnp.concatenate(lines), axis), 0, {})  23.3 us
    dot_general x8, matrix products, block_grads(): jnp.einsum('hrc,rhd->chd', softmax_low, grad_heads, preferred_element_typ...  21.4 us
  transfers between devices with their start and end apart: 4, of which 4 were waited for; matrix products, arithmetic and copies ran while one was open for 2% of the time, Pallas kernels for 0%

commit v1 on v0

v1 whole, which is shorter than its diff:
```python
import functools
import math

import jax
import jax.numpy as jnp
from jax import lax
from jax.experimental import pallas as pl
from jax.experimental.pallas import tpu as pltpu
from jax.sharding import Mesh
from jax.sharding import PartitionSpec as P

D = 1536
H = 16
HD = D // H
PENCIL = 16
PD = 64
HALF = PD // 2
WIDE = 4 * HD
N_Z = 4
N_Y = 2
N_G = 16
GRP = ("grp_0", "grp_1", "grp_2")
BLK_GRP = ("blk_0", "blk_1", "grp_0", "grp_1", "grp_2")
SCALE = 1.0 / math.sqrt(HD)
C2 = SCALE * math.log2(math.e)
TQ = 256
TK = 512
NEG = -1e30
F32 = jnp.float32
BF16 = jnp.bfloat16
CONTRACT_LAST = (((1,), (1,)), ((), ()))
CONTRACT_FIRST = (((0,), (0,)), ((), ()))


def mm(a, b, dims=(((1,), (0,)), ((), ()))):
    return lax.dot_general(a, b, dims, preferred_element_type=F32)


def pack_kernel(order_ref, place_ref, q_ref, g_ref, k_ref, v_ref, out_ref):
    y = place_ref[0]
    g = place_ref[1]
    for zt in range(N_Z):
        for part in range(PD // PENCIL):
            target = ((zt * N_Y + y) * N_G + g) * (PD // PENCIL) + part
            start = pl.multiple_of((order_ref[target] - g * (N_Z * N_Y * PD // PENCIL)) * PENCIL, PENCIL)
            keys = k_ref[pl.ds(start, PENCIL), :]
            values = v_ref[pl.ds(start, PENCIL), :]
            row = zt * HALF + part % 2 * PENCIL
            lane = part // 2 * 2 * HD
            for h in range(H):
                out_ref[h, row : row + PENCIL, lane : lane + HD] = keys[:, h * HD : (h + 1) * HD]
                out_ref[h, row : row + PENCIL, lane + HD : lane + 2 * HD] = values[:, h * HD : (h + 1) * HD]
    base = N_Z * HALF
    for half in range(2):
        lane = half * 2 * HD
        queries = q_ref[half * HALF : (half + 1) * HALF, :]
        grads = g_ref[half * HALF : (half + 1) * HALF, :]
        for h in range(H):
            out_ref[h, base : base + HALF, lane : lane + HD] = queries[:, h * HD : (h + 1) * HD]
            out_ref[h, base : base + HALF, lane + HD : lane + 2 * HD] = grads[:, h * HD : (h + 1) * HD]


def pack(order, place, obj_query, grad_out, pattern_key, pattern_value):
    vmem = pl.BlockSpec(memory_space=pltpu.VMEM)
    return pl.pallas_call(
        pack_kernel,
        out_shape=jax.ShapeDtypeStruct((H, N_Z * HALF + HALF, WIDE), BF16),
        in_specs=[pl.BlockSpec(memory_space=pltpu.SMEM), pl.BlockSpec(memory_space=pltpu.SMEM), vmem, vmem, vmem, vmem],
        out_specs=vmem,
        name="pack",
    )(order, place, obj_query, grad_out, pattern_key, pattern_value)


PK = N_G * N_Z * HALF
PQ = N_G * HALF


def unpack_keys(kv_ref, k_s, v_s):
    for half in range(2):
        for src in range(N_G):
            rows = slice(half * PK + src * N_Z * HALF, half * PK + (src + 1) * N_Z * HALF)
            lane = half * 2 * HD
            k_s[rows, :] = kv_ref[src, : N_Z * HALF, lane : lane + HD]
            v_s[rows, :] = kv_ref[src, : N_Z * HALF, lane + HD : lane + 2 * HD]


def unpack_queries(q_ref, q_s, g_s, base):
    for half in range(2):
        for src in range(N_G):
            rows = slice(base + half * PQ + src * HALF, base + half * PQ + (src + 1) * HALF)
            lane = half * 2 * HD
            q_s[rows, :] = q_ref[src, :, lane : lane + HD]
            g_s[rows, :] = q_ref[src, :, lane + HD : lane + 2 * HD]


def stats_kernel(q_ref, kv_ref, st_ref, q_s, g_s, k_s, v_s):
    unpack_keys(kv_ref, k_s, v_s)
    unpack_queries(q_ref, q_s, g_s, 0)

    def one_tile(t, _):
        q0 = pl.multiple_of(t * TQ, TQ)
        qt = q_s[pl.ds(q0, TQ), :]
        gt = g_s[pl.ds(q0, TQ), :]

        def one_chunk(j, carry):
            m, l, w = carry
            k0 = pl.multiple_of(j * TK, TK)
            s = mm(k_s[pl.ds(k0, TK), :], qt, CONTRACT_LAST).reshape(TK // 8, 8, TQ)
            d = mm(v_s[pl.ds(k0, TK), :], gt, CONTRACT_LAST).reshape(TK // 8, 8, TQ)
            top = jnp.maximum(m, jnp.max(s, axis=0))
            fade = jnp.exp2((m - top) * C2)
            e = jnp.exp2((s - top[None]) * C2)
            return top, l * fade + jnp.sum(e, axis=0), w * fade + jnp.sum(e * d, axis=0)

        zero = jnp.zeros((8, TQ), F32)
        m, l, w = lax.fori_loop(0, 2 * PK // TK, one_chunk, (jnp.full((8, TQ), NEG, F32), zero, zero), unroll=2)
        top = jnp.max(m, axis=0, keepdims=True)
        fade = jnp.exp2((m - top) * C2)
        st_ref[0:1, pl.ds(q0, TQ)] = top
        st_ref[1:2, pl.ds(q0, TQ)] = jnp.sum(l * fade, axis=0, keepdims=True)
        st_ref[2:3, pl.ds(q0, TQ)] = jnp.sum(w * fade, axis=0, keepdims=True)
        return 0

    lax.fori_loop(0, 2 * PQ // TQ, one_tile, 0)
    st_ref[3:8, :] = jnp.zeros((5, 2 * PQ), F32)


def stats(q, kv):
    vmem = pl.BlockSpec(memory_space=pltpu.VMEM)
    return pl.pallas_call(
        stats_kernel,
        out_shape=jax.ShapeDtypeStruct((8, 2 * PQ), F32),
        in_specs=[vmem, vmem],
        out_specs=vmem,
        scratch_shapes=[pltpu.VMEM((2 * PQ, HD), BF16)] * 2 + [pltpu.VMEM((2 * PK, HD), BF16)] * 2,
        name="stats",
    )(q, kv)


def joined(mine, theirs):
    top = jnp.maximum(mine[0:1], theirs[0:1])
    a = jnp.exp2((mine[0:1] - top) * C2)
    b = jnp.exp2((theirs[0:1] - top) * C2)
    total = mine[1:2] * a + theirs[1:2] * b
    return top * C2 + jnp.log2(total), (mine[2:3] * a + theirs[2:3] * b) / total


def grads_kernel(
    place_ref, qa_ref, qb_ref, kv_ref, sa_ref, sb_ref, ta_ref, tb_ref, dq_ref, dkv_ref,
    q_s, g_s, k_s, v_s, dq_s, dk_s, dv_s, log_s, mean_s,
):
    unpack_keys(kv_ref, k_s, v_s)
    unpack_queries(qa_ref, q_s, g_s, 0)
    unpack_queries(qb_ref, q_s, g_s, 2 * PQ)
    for n, (mine, theirs) in enumerate(((sa_ref, tb_ref), (sb_ref, ta_ref))):
        log_now, mean_now = joined(mine, theirs)
        log_s[:, n * 2 * PQ : (n + 1) * 2 * PQ] = jnp.broadcast_to(log_now, (8, 2 * PQ))
        mean_s[:, n * 2 * PQ : (n + 1) * 2 * PQ] = jnp.broadcast_to(mean_now, (8, 2 * PQ))
    dq_s[...] = jnp.zeros_like(dq_s)

    def one_chunk(j, _):
        k0 = pl.multiple_of(j * TK, TK)
        kc = k_s[pl.ds(k0, TK), :]
        vc = v_s[pl.ds(k0, TK), :]

        def one_tile(t, carry):
            dk, dv = carry
            q0 = pl.multiple_of(t * TQ, TQ)
            qt = q_s[pl.ds(q0, TQ), :]
            gt = g_s[pl.ds(q0, TQ), :]
            s = mm(kc, qt, CONTRACT_LAST).reshape(TK // 8, 8, TQ)
            d = mm(vc, gt, CONTRACT_LAST).reshape(TK // 8, 8, TQ)
            p = jnp.exp2(s * C2 - log_s[:, pl.ds(q0, TQ)][None])
            sg = ((d - mean_s[:, pl.ds(q0, TQ)][None]) * (p * SCALE)).astype(BF16).reshape(TK, TQ)
            p = p.astype(BF16).reshape(TK, TQ)
            dq_s[pl.ds(q0, TQ), :] += mm(sg, kc, CONTRACT_FIRST)
            return dk + mm(sg, qt), dv + mm(p, gt)

        zero = jnp.zeros((TK, HD), F32)
        dk, dv = lax.fori_loop(0, 4 * PQ // TQ, one_tile, (zero, zero), unroll=2)
        dk_s[pl.ds(k0, TK), :] = dk.astype(BF16)
        dv_s[pl.ds(k0, TK), :] = dv.astype(BF16)
        return 0

    lax.fori_loop(0, 2 * PK // TK, one_chunk, 0)
    for half in range(2):
        lane = half * 2 * HD
        for src in range(N_G):
            for zt in range(N_Z):
                r0 = half * PK + (src * N_Z + zt) * HALF
                dkv_ref[zt, src, :, lane : lane + HD] = dk_s[r0 : r0 + HALF, :]
                dkv_ref[zt, src, :, lane + HD : lane + 2 * HD] = dv_s[r0 : r0 + HALF, :]
    y = place_ref[0]
    for n, where in enumerate((y, 1 - y)):
        for src in range(N_G):
            for quarter in range(4):
                r0 = n * 2 * PQ + quarter // 2 * PQ + src * HALF + quarter % 2 * PENCIL
                dq_ref[where, src, :, quarter * HD : (quarter + 1) * HD] = dq_s[r0 : r0 + PENCIL, :].astype(BF16)


def grads(place, qa, qb, kv, sa, sb, ta, tb):
    vmem = pl.BlockSpec(memory_space=pltpu.VMEM)
    return pl.pallas_call(
        grads_kernel,
        out_shape=(
            jax.ShapeDtypeStruct((N_Y, N_G, PENCIL, WIDE), BF16),
            jax.ShapeDtypeStruct((N_Z, N_G, HALF, WIDE), BF16),
        ),
        in_specs=[pl.BlockSpec(memory_space=pltpu.SMEM)] + [vmem] * 7,
        out_specs=(vmem, vmem),
        scratch_shapes=[pltpu.VMEM((4 * PQ, HD), BF16)] * 2
        + [pltpu.VMEM((2 * PK, HD), BF16)] * 2
        + [pltpu.VMEM((4 * PQ, HD), F32)]
        + [pltpu.VMEM((2 * PK, HD), BF16)] * 2
        + [pltpu.VMEM((8, 4 * PQ), F32)] * 2,
        name="grads",
    )(place, qa, qb, kv, sa, sb, ta, tb)


def keys_out_kernel(got_ref, key_ref, value_ref):
    for h in range(H):
        total = got_ref[0, h].astype(F32)
        for z in range(1, N_Z):
            total = total + got_ref[z, h].astype(F32)
        total = total.astype(BF16)
        for half in range(2):
            lane = half * 2 * HD
            rows = slice(half * HALF, (half + 1) * HALF)
            key_ref[rows, h * HD : (h + 1) * HD] = total[:, lane : lane + HD]
            value_ref[rows, h * HD : (h + 1) * HD] = total[:, lane + HD : lane + 2 * HD]


def queries_out_kernel(got_ref, query_ref):
    for h in range(H):
        total = (got_ref[0, h].astype(F32) + got_ref[1, h].astype(F32)).astype(BF16)
        for quarter in range(4):
            rows = slice(quarter * PENCIL, (quarter + 1) * PENCIL)
            query_ref[rows, h * HD : (h + 1) * HD] = total[:, quarter * HD : (quarter + 1) * HD]


def placed_out(kernel, got, outs, name):
    vmem = pl.BlockSpec(memory_space=pltpu.VMEM)
    return pl.pallas_call(
        kernel,
        out_shape=[jax.ShapeDtypeStruct((PD, D), BF16)] * outs,
        in_specs=[vmem],
        out_specs=[vmem] * outs,
        name=name,
    )(got)


def on_device(obj_query, grad_out, pattern_key, pattern_value, pencil_order):
    place = jnp.stack([lax.axis_index("blk_1"), lax.axis_index(GRP)]).astype(jnp.int32)
    swap = functools.partial(lax.ppermute, axis_name="blk_1", perm=((0, 1), (1, 0)))
    sent = pack(pencil_order, place, obj_query, grad_out, pattern_key, pattern_value)
    got = lax.all_to_all(sent, GRP, 0, 0, tiled=True)
    qa = got[:, N_Z * HALF :, :]
    qb = swap(qa)
    sa = stats(qa, got)
    ta = swap(sa)
    sb = stats(qb, got)
    tb = swap(sb)
    dq, dkv = grads(place, qa, qb, got, sa, sb, ta, tb)
    dkv = lax.all_to_all(dkv.reshape(N_Z * N_G, HALF, WIDE), ("blk_0", *GRP), 0, 0, tiled=True)
    dq = lax.all_to_all(dq.reshape(N_Y * N_G, PENCIL, WIDE), ("blk_1", *GRP), 0, 0, tiled=True)
    key_grad, value_grad = placed_out(keys_out_kernel, dkv.reshape(N_Z, N_G, HALF, WIDE), 2, "keys_out")
    (query_grad,) = placed_out(queries_out_kernel, dq.reshape(N_Y, N_G, PENCIL, WIDE), 1, "queries_out")
    return query_grad, key_grad, value_grad


def solution(mesh):
    split = Mesh(mesh.devices.reshape(4, 2, 2, 4, 2), BLK_GRP)
    return jax.shard_map(
        on_device,
        mesh=split,
        in_specs=(P(BLK_GRP, None), P(BLK_GRP, None), P(GRP, None), P(GRP, None), P()),
        out_specs=(P(BLK_GRP, None), P(BLK_GRP, None), P(BLK_GRP, None)),
        check_vma=False,
    )
```

time: 523 us -> 181 us (0.35)
  waiting for transfers between devices: 207 us -> 24.4 us
  local copies, waits for them, and re-layouts: 103 us -> 2.59 us
  matrix products: 92.7 us -> 0 us
  Pallas kernels: 0 us -> 90.3 us
  other arithmetic: 78.6 us -> 0.65 us
  blocking collectives: 23.3 us -> 48.8 us
  between operations: 14.1 us -> 0.67 us
  starting transfers between devices: 0.16 us -> 12.7 us
    reduce_scatter x3 -> x0, waiting for transfers between devices: 167 us -> none  [the longest x2 97.6 us: summed_rows(): so_far = lax.psum_scatter(so_far, axis, scatter_dimension=0, tiled=True)]
    dot_general x56 -> x0, matrix products: 92.7 us -> none  [the longest x8 23.9 us: block_grads(): jnp.einsum('rhd,chd->hrc', grad_heads, value_heads, preferred_element_typ...]
    pallas_call x0 -> x6, Pallas kernels: none -> 90.3 us  [the longest x1 45.6 us: grads(): pl.pallas_call(grads_kernel, out_shape=(jax.ShapeDtypeStruct((N_Y, N_G, P...]
    add x12 -> x0, other arithmetic: 56.4 us -> none  [the longest x8 56.2 us: sweep(): return ((keys_acc + key_term, values_acc + value_term), query_term)]
    all_to_all x0 -> x2, blocking collectives: none -> 48.8 us  [the longest x1 31.8 us: on_device(): got = lax.all_to_all(sent, GRP, 0, 0, tiled=True)]
    all_gather x1 -> x0, waiting for transfers between devices: 39.4 us -> none  [sent_together(): result = lax.all_gather(both, axis, axis=dim, tiled=True)]
    dynamic_slice x48 -> x0, local copies, waits for them, and re-layouts: 35.5 us -> none  [the longest x32 35.3 us: stats_of_rows(): lax.map(one_block, (queries.reshape(amount // blocking, blocking, feature...]
    while x164 -> x0, local copies, waits for them, and re-layouts: 23.4 us -> none
  transfers between devices with their start and end apart: 4 -> 4, of which waited for: 4 -> 2; matrix products, arithmetic and copies ran while one was open for 2% -> 0% of each run, Pallas kernels for 0% -> 16%
where the time goes in v1:
time: 181 us; the launch traced here: 180 us
  Pallas kernels  90.3 us (50%)
  blocking collectives  48.8 us (27%)
  waiting for transfers between devices  24.4 us (13%)
  starting transfers between devices  12.7 us (7%)
  local copies, waits for them, and re-layouts  2.59 us (1%)
    pallas_call x1, Pallas kernels, grads(): pl.pallas_call(grads_kernel, out_shape=(jax.ShapeDtypeStruct((N_Y, N_G, P...  45.6 us
    all_to_all x1, blocking collectives, on_device(): got = lax.all_to_all(sent, GRP, 0, 0, tiled=True)  31.8 us
    pallas_call x2, Pallas kernels, stats(): pl.pallas_call(stats_kernel, out_shape=jax.ShapeDtypeStruct((8, 2 * PQ),...  26.6 us
    all_to_all x1, waiting for transfers between devices, on_device(): lax.all_to_all(dkv.reshape(N_Z * N_G, HALF, WIDE), ('blk_0', *GRP), 0, 0,...  21.6 us
    all_to_all x1, blocking collectives, on_device(): lax.all_to_all(dq.reshape(N_Y * N_G, PENCIL, WIDE), ('blk_1', *GRP), 0, 0...  17 us
    pallas_call x1, Pallas kernels, pack(): pl.pallas_call(pack_kernel, out_shape=jax.ShapeDtypeStruct((H, N_Z * HALF...  13.9 us
    all_to_all x1, starting transfers between devices, on_device(): lax.all_to_all(dkv.reshape(N_Z * N_G, HALF, WIDE), ('blk_0', *GRP), 0, 0,...  7.03 us
    pallas_call x2, Pallas kernels, placed_out(): pl.pallas_call(kernel, out_shape=[jax.ShapeDtypeStruct((PD, D), BF16)] *...  4.3 us
  transfers between devices with their start and end apart: 4, of which 2 were waited for; matrix products, arithmetic and copies ran while one was open for 0% of the time, Pallas kernels for 16%

profile of v1, /device:TPU:1, one launch (start us, length us, event | category | flops | bytes accessed | tf_op | source)
XLA Modules:
  0.0 180.2 jit_solution(16977469659254224194)
XLA Ops:
  0.6 0.7 pad_add_fusion.place_ref
  1.3 13.9 %pack.1 = bf16[16,160,384]{2,1,0:T(8,128)(2,1)} custom-call(s32[512]{0:T(512)} %order_ref.1, s32[2]{0:T(128)} %pad_add_fusion.place_ref, bf16[64,1536]{1,0:T(8,128)(2,1)} %q_ref.1, bf16[64,1536]{1,0:T(8,128)(2,1)} %g_ref.1, bf16[512,1536]{1,0:T(8,128)(2,1)} %k_ref.1, bf16[512,1536]{1,0:T(8,128)(2,1)} %v_ref.1), custom_call_target="tpu_custom_call" | custom-call | tf_op jit(solution)/shard_map/pack/pallas_call | solution.py:65
  15.2 31.8 %all_to_all.15.kv_ref = bf16[16,160,384]{2,1,0:T(8,128)(2,1)S(1)} all-to-all(bf16[16,160,384]{2,1,0:T(8,128)(2,1)} %pack.1), channel_id=1, replica_groups=mesh['blk_0'=4,'blk_1'=2,'grp_0'=2,'grp_1'=4,'grp_2'=2] {'grp_0','grp_1'..., dimensions={0} | all-to-all | bytes 3932160 | tf_op jit(solution)/shard_map/all_to_all | solution.py:256
  47.1 0.0 copy-start.2
  47.1 2.7 %collective-permute-start = (bf16[16,32,384]{2,1,0:T(8,128)(2,1)S(1)}, bf16[16,32,384]{2,1,0:T(8,128)(2,1)S(1)}, u32[]{:S(2)}, u32[]{:S(2)}) collective-permute-start(bf16[16,32,384]{2,1,0:T(8,128)(2,1)S(1)} %slice.4.q_ref.qa_ref), channel_id=1, source_target_pairs={{0,16},{16,0},{1,17},{17,1},{2,18},{18,2},{3,19},{19,3},{4,20},{20... | collective-permute-start | bytes 1179656 | tf_op jit(solution)/shard_map/ppermute | solution.py:258
  49.8 0.0 copy-done
  49.8 0.0 copy-done.2
  49.8 13.3 %stats.2.sa_ref = f32[8,1024]{1,0:T(8,128)} custom-call(bf16[16,32,384]{2,1,0:T(8,128)(2,1)} %copy-done.2, bf16[16,160,384]{2,1,0:T(8,128)(2,1)} %copy-done), custom_call_target="tpu_custom_call" | custom-call | tf_op jit(solution)/shard_map/stats/pallas_call | solution.py:130
  63.1 1.3 collective-permute-start.1
  64.4 0.0 collective-permute-done.q_ref.qb_ref
  64.4 0.7 copy-done.3
  65.1 13.3 %stats.3.sb_ref = f32[8,1024]{1,0:T(8,128)} custom-call(bf16[16,32,384]{2,1,0:T(8,128)(2,1)} %copy-done.3, bf16[16,160,384]{2,1,0:T(8,128)(2,1)} %copy-done), custom_call_target="tpu_custom_call" | custom-call | tf_op jit(solution)/shard_map/stats/pallas_call | solution.py:130
  78.4 1.7 collective-permute-start.2
  80.1 0.0 collective-permute-done.1.ta_ref
  80.1 2.8 %collective-permute-done.2.tb_ref = f32[8,1024]{1,0:T(8,128)S(1)} collective-permute-done((f32[8,1024]{1,0:T(8,128)}, f32[8,1024]{1,0:T(8,128)S(1)}, u32[]{:S(2)}, u32[]{:S(2)}) %collective-permute-start.2) | collective-permute-done | bytes 32800 | tf_op jit(solution)/shard_map/ppermute | solution.py:262
  82.9 0.0 copy-done.4
  82.9 0.6 copy-done.5
  83.5 45.6 %grads.1 = (bf16[2,16,16,384]{3,2,1,0:T(8,128)(2,1)}, bf16[4,16,32,384]{3,2,1,0:T(8,128)(2,1)}) custom-call(s32[2]{0:T(128)} %pad_add_fusion.place_ref, bf16[16,32,384]{2,1,0:T(8,128)(2,1)} %copy-done.2, bf16[16,32,384]{2,1,0:T(8,128)(2,1)} %copy-done.3, bf16[16,160,384]{2,1,0:T(8,128)(2,1)} %copy-done, f32[8,1024]{1,0:T(8,128)} %stats.2.sa_ref, ...), custom_call_target="tpu_custom_call" | custom-call | tf_op jit(solution)/shard_map/grads/pallas_call | solution.py:203
  129.1 17.0 %all_to_all.16 = bf16[32,16,384]{2,1,0:T(8,128)(2,1)} all-to-all(bf16[32,16,384]{2,1,0:T(8,128)(2,1)} %bitcast.9), channel_id=1, replica_groups=mesh['blk_0'=4,'blk_1'=2,'grp_0'=2,'grp_1'=4,'grp_2'=2] {'blk_1','grp_0'..., dimensions={0} | all-to-all | bytes 786432 | tf_op jit(solution)/shard_map/all_to_all | solution.py:265
  146.1 7.0 %all-to-all-start.2 = ((bf16[64,32,384]{2,1,0:T(8,128)(2,1)}), bf16[64,32,384]{2,1,0:T(8,128)(2,1)S(1)}, u32[]{:S(2)}, u32[]{:S(2)}) async-start(bf16[64,32,384]{2,1,0:T(8,128)(2,1)} %bitcast.7), calls=%async_computation.2 | async-start | bytes 3145728 | tf_op jit(solution)/shard_map/all_to_all | solution.py:264
  153.1 1.8 %queries_out.1 = bf16[64,1536]{1,0:T(8,128)(2,1)} custom-call(bf16[2,16,16,384]{3,2,1,0:T(8,128)(2,1)} %bitcast.8), custom_call_target="tpu_custom_call" | custom-call | tf_op jit(solution)/shard_map/queries_out/pallas_call | solution.py:243
  154.9 21.6 %all-to-all-done.2 = bf16[64,32,384]{2,1,0:T(8,128)(2,1)S(1)} async-done(((bf16[64,32,384]{2,1,0:T(8,128)(2,1)}), bf16[64,32,384]{2,1,0:T(8,128)(2,1)S(1)}, u32[]{:S(2)}, u32[]{:S(2)}) %all-to-all-start.2) | async-done | bytes 1572896 | tf_op jit(solution)/shard_map/all_to_all | solution.py:264
  176.6 1.2 copy-done.1
  177.7 2.5 %keys_out.1 = (bf16[64,1536]{1,0:T(8,128)(2,1)}, bf16[64,1536]{1,0:T(8,128)(2,1)}) custom-call(bf16[4,16,32,384]{3,2,1,0:T(8,128)(2,1)} %bitcast.6), custom_call_target="tpu_custom_call" | custom-call | tf_op jit(solution)/shard_map/keys_out/pallas_call | solution.py:243
  (6 shorter events, 0.0 us)
Async XLA Ops:
  47.0 2.8 %copy-start = (bf16[16,160,384]{2,1,0:T(8,128)(2,1)}, bf16[16,160,384]{2,1,0:T(8,128)(2,1)S(1)}, u32[]{:S(2)}) copy-start(bf16[16,160,384]{2,1,0:T(8,128)(2,1)S(1)} %all_to_all.15.kv_ref) | copy-start | bytes 5898244
  47.1 2.7 %copy-start.2 = (bf16[16,32,384]{2,1,0:T(8,128)(2,1)}, bf16[16,32,384]{2,1,0:T(8,128)(2,1)S(1)}, u32[]{:S(2)}) copy-start(bf16[16,32,384]{2,1,0:T(8,128)(2,1)S(1)} %slice.4.q_ref.qa_ref) | copy-start | bytes 1179652
  47.1 17.3 %collective-permute-start = (bf16[16,32,384]{2,1,0:T(8,128)(2,1)S(1)}, bf16[16,32,384]{2,1,0:T(8,128)(2,1)S(1)}, u32[]{:S(2)}, u32[]{:S(2)}) collective-permute-start(bf16[16,32,384]{2,1,0:T(8,128)(2,1)S(1)} %slice.4.q_ref.qa_ref), channel_id=1, source_target_pairs={{0,16},{16,0},{1,17},{17,1},{2,18},{18,2},{3,19},{19,3},{4,20},{20... | collective-permute-start | bytes 1179656 | tf_op jit(solution)/shard_map/ppermute | solution.py:258
  63.1 17.0 %collective-permute-start.1 = (f32[8,1024]{1,0:T(8,128)}, f32[8,1024]{1,0:T(8,128)S(1)}, u32[]{:S(2)}, u32[]{:S(2)}) collective-permute-start(f32[8,1024]{1,0:T(8,128)} %stats.2.sa_ref), channel_id=1, source_target_pairs={{0,16},{16,0},{1,17},{17,1},{2,18},{18,2},{3,19},{19,3},{4,20},{20... | collective-permute-start | bytes 98312 | tf_op jit(solution)/shard_map/ppermute | solution.py:260
  64.4 0.7 copy-start.3
  78.4 4.5 %collective-permute-start.2 = (f32[8,1024]{1,0:T(8,128)}, f32[8,1024]{1,0:T(8,128)S(1)}, u32[]{:S(2)}, u32[]{:S(2)}) collective-permute-start(f32[8,1024]{1,0:T(8,128)} %stats.3.sb_ref), channel_id=1, source_target_pairs={{0,16},{16,0},{1,17},{17,1},{2,18},{18,2},{3,19},{19,3},{4,20},{20... | collective-permute-start | bytes 98312 | tf_op jit(solution)/shard_map/ppermute | solution.py:262
  80.1 2.8 %copy-start.4 = (f32[8,1024]{1,0:T(8,128)}, f32[8,1024]{1,0:T(8,128)S(1)}, u32[]{:S(2)}) copy-start(f32[8,1024]{1,0:T(8,128)S(1)} %collective-permute-done.1.ta_ref) | copy-start | bytes 98308
  82.9 0.6 copy-start.5
  146.1 30.5 %all-to-all-start.2 = ((bf16[64,32,384]{2,1,0:T(8,128)(2,1)}), bf16[64,32,384]{2,1,0:T(8,128)(2,1)S(1)}, u32[]{:S(2)}, u32[]{:S(2)}) async-start(bf16[64,32,384]{2,1,0:T(8,128)(2,1)} %bitcast.7), calls=%async_computation.2 | async-start | bytes 3145728 | tf_op jit(solution)/shard_map/all_to_all | solution.py:264
  176.6 1.2 copy-start.1

commit v2 on v1

v2 whole, which is shorter than its diff:
```python
import functools
import math

import jax
import jax.numpy as jnp
from jax import lax
from jax.experimental import pallas as pl
from jax.experimental.pallas import tpu as pltpu
from jax.sharding import Mesh
from jax.sharding import PartitionSpec as P


D = 1536
H = 16
HD = D // H
PENCIL = 16
PD = 64
HALF = PD // 2
WIDE = 4 * HD
N_Z = 4
N_Y = 2
N_G = 16
GRP = ("grp_0", "grp_1", "grp_2")
BLK_GRP = ("blk_0", "blk_1", "grp_0", "grp_1", "grp_2")
SCALE = 1.0 / math.sqrt(HD)
C2 = SCALE * math.log2(math.e)
TQ = 1024
TK = 512
GUN = 1
STQ = 1024
STK = 2048
SUB = 64
SUN = 1
CHUNKS = 2
NEG = -1e30
F32 = jnp.float32
BF16 = jnp.bfloat16
CONTRACT_LAST = (((1,), (1,)), ((), ()))
CONTRACT_FIRST = (((0,), (0,)), ((), ()))


def mm(a, b, dims=(((1,), (0,)), ((), ()))):
    return lax.dot_general(a, b, dims, preferred_element_type=F32)


KR = N_Z * HALF
SR = KR + HALF
PK = N_G * KR
PQ = N_G * HALF
WINDOWS = ((0, 128, 0), (0, 256, HD), (128, 256, 2 * HD - 128), (256, 128, 3 * HD - 256))


def shift(rows, cols, src, dst):
    i = lax.broadcasted_iota(jnp.int32, (rows, cols), 0) - src
    j = lax.broadcasted_iota(jnp.int32, (rows, cols), 1) - dst
    return jnp.where((i == j) & (i >= 0) & (i < HD), 1.0, 0.0).astype(BF16)


def turned_shift(cols, src):
    i = lax.broadcasted_iota(jnp.int32, (128, cols), 0)
    j = lax.broadcasted_iota(jnp.int32, (128, cols), 1) - src
    return jnp.where((i == j) & (i < HD), 1.0, 0.0).astype(BF16)


def pack_four(parts):
    a, b, c, d = parts
    return (
        (a + b[:, :128]).astype(BF16),
        (b[:, 128:] + c[:, :128]).astype(BF16),
        (c[:, 128:] + d).astype(BF16),
    )


def pack_kernel(order_ref, place_ref, q_ref, g_ref, k_ref, v_ref, out_ref, ka_s, va_s, kb_s, vb_s):
    y = place_ref[0]
    g = place_ref[1]
    for zt in range(N_Z):
        for part in range(PD // PENCIL):
            target = ((zt * N_Y + y) * N_G + g) * (PD // PENCIL) + part
            start = pl.multiple_of((order_ref[target] - g * (N_Z * N_Y * PD // PENCIL)) * PENCIL, PENCIL)
            row = zt * HALF + part % 2 * PENCIL
            k_s, v_s = ((ka_s, va_s), (kb_s, vb_s))[part // 2]
            k_s[row : row + PENCIL, :] = k_ref[pl.ds(start, PENCIL), :]
            v_s[row : row + PENCIL, :] = v_ref[pl.ds(start, PENCIL), :]
    for half, (k_s, v_s) in enumerate(((ka_s, va_s), (kb_s, vb_s))):
        k_s[KR:SR, :] = q_ref[half * HALF : (half + 1) * HALF, :]
        v_s[KR:SR, :] = g_ref[half * HALF : (half + 1) * HALF, :]
    for turn in range(4):
        heads = range(turn, H, 4)
        offset = turn * HD % 128
        width = 128 if offset + HD <= 128 else 256
        parts = []
        for ref, (_, cols, dst) in zip((ka_s, va_s, kb_s, vb_s), WINDOWS):
            x = jnp.concatenate([ref[:, h * HD // 128 * 128 : h * HD // 128 * 128 + width] for h in heads], axis=0)
            parts.append(mm(x, shift(width, cols, offset, dst)))
        for n, piece in enumerate(pack_four(parts)):
            for k, h in enumerate(heads):
                out_ref[h, :, n * 128 : (n + 1) * 128] = piece[k * SR : (k + 1) * SR]


def pack(order, place, obj_query, grad_out, pattern_key, pattern_value):
    vmem = pl.BlockSpec(memory_space=pltpu.VMEM)
    return pl.pallas_call(
        pack_kernel,
        out_shape=jax.ShapeDtypeStruct((H, SR, WIDE), BF16),
        in_specs=[pl.BlockSpec(memory_space=pltpu.SMEM), pl.BlockSpec(memory_space=pltpu.SMEM), vmem, vmem, vmem, vmem],
        out_specs=vmem,
        scratch_shapes=[pltpu.VMEM((SR, D), BF16)] * 4,
        name="pack",
    )(order, place, obj_query, grad_out, pattern_key, pattern_value)


def unpack(read, rows, stores):
    for (start, width, offset), (ref, base) in zip(WINDOWS, stores):
        ref[base : base + rows, :] = mm(read(slice(start, start + width)), shift(width, 128, offset, 0)).astype(BF16)


def unpack_keys(kv_ref, k_s, v_s, chunk, chunks, t_s=None):
    rows = HALF // chunks
    for zt in range(N_Z):
        at = slice(zt * HALF + chunk * rows, zt * HALF + (chunk + 1) * rows)
        k_first, k_second = zt * N_G * rows, (N_Z + zt) * N_G * rows

        def read(lanes):
            return kv_ref[:, at, lanes].reshape(N_G * rows, lanes.stop - lanes.start)

        unpack(read, N_G * rows, ((k_s, k_first), (v_s, k_first), (k_s, k_second), (v_s, k_second)))
        if t_s is not None:
            for (start, width, offset), base in ((WINDOWS[0], k_first), (WINDOWS[2], k_second)):
                x = read(slice(start, start + width))
                t_s[:, base : base + N_G * rows] = mm(turned_shift(width, offset), x, CONTRACT_LAST)[:HD].astype(BF16)


def unpack_turned(read, rows, stores):
    for (start, width, offset), (ref, base) in zip(WINDOWS, stores):
        x = read(slice(start, start + width))
        ref[:, base : base + rows] = mm(turned_shift(width, offset), x, CONTRACT_LAST).astype(BF16)


def unpack_queries(q_ref, q_s, g_s, base):
    unpack_turned(
        lambda lanes: q_ref[:, :, lanes].reshape(PQ, lanes.stop - lanes.start),
        PQ,
        ((q_s, base), (g_s, base), (q_s, base + PQ), (g_s, base + PQ)),
    )


def unpack_query_rows(q_ref, q_s, g_s, base):
    unpack(
        lambda lanes: q_ref[:, :, lanes].reshape(PQ, lanes.stop - lanes.start),
        PQ,
        ((q_s, base), (g_s, base), (q_s, base + PQ), (g_s, base + PQ)),
    )


def stats_kernel(q_ref, kv_ref, st_ref, q_s, g_s, k_s, v_s):
    unpack_keys(kv_ref, k_s, v_s, 0, 1)
    unpack_queries(q_ref, q_s, g_s, 0)

    def one_tile(t, _):
        q0 = pl.multiple_of(t * STQ, STQ)
        qt = q_s[:, pl.ds(q0, STQ)]
        gt = g_s[:, pl.ds(q0, STQ)]

        def one_chunk(j, carry):
            m, l, w = carry
            k0 = pl.multiple_of(j * STK, STK)
            s = mm(k_s[pl.ds(k0, STK), :], qt).reshape(STK // SUB, SUB // 8, 8, STQ)
            d = mm(v_s[pl.ds(k0, STK), :], gt).reshape(STK // SUB, SUB // 8, 8, STQ)
            for n in range(STK // SUB):
                top = jnp.maximum(m, jnp.max(s[n], axis=0))
                fade = jnp.exp2((m - top) * C2)
                e = jnp.exp2((s[n] - top[None]) * C2)
                m, l, w = top, l * fade + jnp.sum(e, axis=0), w * fade + jnp.sum(e * d[n], axis=0)
            return m, l, w

        zero = jnp.zeros((8, STQ), F32)
        m, l, w = lax.fori_loop(0, 2 * PK // STK, one_chunk, (jnp.full((8, STQ), NEG, F32), zero, zero), unroll=SUN)
        top = jnp.max(m, axis=0, keepdims=True)
        fade = jnp.exp2((m - top) * C2)
        st_ref[0:1, pl.ds(q0, STQ)] = top
        st_ref[1:2, pl.ds(q0, STQ)] = jnp.sum(l * fade, axis=0, keepdims=True)
        st_ref[2:3, pl.ds(q0, STQ)] = jnp.sum(w * fade, axis=0, keepdims=True)
        return 0

    lax.fori_loop(0, 2 * PQ // STQ, one_tile, 0)
    st_ref[3:8, :] = jnp.zeros((5, 2 * PQ), F32)


def stats(q, kv):
    vmem = pl.BlockSpec(memory_space=pltpu.VMEM)
    return pl.pallas_call(
        stats_kernel,
        out_shape=jax.ShapeDtypeStruct((8, 2 * PQ), F32),
        in_specs=[vmem, vmem],
        out_specs=vmem,
        scratch_shapes=[pltpu.VMEM((128, 2 * PQ), BF16)] * 2 + [pltpu.VMEM((2 * PK, 128), BF16)] * 2,
        cost_estimate=pl.CostEstimate(
            flops=4 * 2 * PQ * 2 * PK * 256, transcendentals=2 * PQ * 2 * PK, bytes_accessed=4 << 20
        ),
        name="stats",
    )(q, kv)


def joined(mine, theirs):
    top = jnp.maximum(mine[0:1], theirs[0:1])
    a = jnp.exp2((mine[0:1] - top) * C2)
    b = jnp.exp2((theirs[0:1] - top) * C2)
    total = mine[1:2] * a + theirs[1:2] * b
    return top * C2 + jnp.log2(total), (mine[2:3] * a + theirs[2:3] * b) / total


def grads_kernel(chunk, place_ref, qa_ref, qb_ref, kv_ref, sa_ref, sb_ref, ta_ref, tb_ref, *refs):
    first, last = chunk == 0, chunk == CHUNKS - 1
    so_far_ref = None if first else refs[0]
    dq_ref, dkv_ref, q_s, g_s, k_s, v_s, t_s, dq_s, dk_s, dv_s, log_s, mean_s = refs[0 if first else 1 :]
    if not last:
        dq_s = dq_ref
    unpack_keys(kv_ref, k_s, v_s, chunk, CHUNKS, t_s)
    unpack_query_rows(qa_ref, q_s, g_s, 0)
    unpack_query_rows(qb_ref, q_s, g_s, 2 * PQ)
    for n, (mine, theirs) in enumerate(((sa_ref, tb_ref), (sb_ref, ta_ref))):
        log_now, mean_now = joined(mine, theirs)
        log_s[:, n * 2 * PQ : (n + 1) * 2 * PQ] = jnp.broadcast_to(log_now, (8, 2 * PQ))
        mean_s[:, n * 2 * PQ : (n + 1) * 2 * PQ] = jnp.broadcast_to(mean_now, (8, 2 * PQ))
    dq_s[...] = jnp.zeros_like(dq_s) if first else so_far_ref[...]

    def one_chunk(j, _):
        k0 = pl.multiple_of(j * TK, TK)
        kc = k_s[pl.ds(k0, TK), :]
        vc = v_s[pl.ds(k0, TK), :]
        kt = t_s[:, pl.ds(k0, TK)]

        def one_tile(t, carry):
            dk, dv = carry
            q0 = pl.multiple_of(t * TQ, TQ)
            qt = q_s[pl.ds(q0, TQ), :]
            gt = g_s[pl.ds(q0, TQ), :]
            s = mm(kc, qt, CONTRACT_LAST).reshape(TK // 8, 8, TQ)
            d = mm(vc, gt, CONTRACT_LAST).reshape(TK // 8, 8, TQ)
            p = jnp.exp2(s * C2 - log_s[:, pl.ds(q0, TQ)][None])
            sg = ((d - mean_s[:, pl.ds(q0, TQ)][None]) * (p * SCALE)).astype(BF16).reshape(TK, TQ)
            p = p.astype(BF16).reshape(TK, TQ)
            dq_s[:, pl.ds(q0, TQ)] += mm(kt, sg)
            return dk + mm(sg, qt), dv + mm(p, gt)

        zero = jnp.zeros((TK, 128), F32)
        dk, dv = lax.fori_loop(0, 4 * PQ // TQ, one_tile, (zero, zero), unroll=GUN)
        dk_s[pl.ds(k0, TK), :] = dk.astype(BF16)
        dv_s[pl.ds(k0, TK), :] = dv.astype(BF16)
        return 0

    lax.fori_loop(0, 2 * PK // CHUNKS // TK, one_chunk, 0)
    place4 = [shift(HD, cols, 0, dst) for _, cols, dst in WINDOWS]
    rows = PK // CHUNKS
    parts = [
        mm(ref[half * rows : (half + 1) * rows, :HD], place4[n])
        for n, (ref, half) in enumerate(((dk_s, 0), (dv_s, 0), (dk_s, 1), (dv_s, 1)))
    ]
    for n, piece in enumerate(pack_four(parts)):
        dkv_ref[:, :, n * 128 : (n + 1) * 128] = piece.reshape(N_Z * N_G, HALF // CHUNKS, 128)
    if last:
        y = place_ref[0]
        for n, where in enumerate((y, 1 - y)):
            parts = []
            for quarter in range(4):
                r0 = n * 2 * PQ + quarter // 2 * PQ
                x = mm(dq_s[:, r0 : r0 + PQ].astype(BF16), place4[quarter], CONTRACT_FIRST)
                x = x.reshape(N_G, 2, PENCIL, x.shape[1])[:, quarter % 2]
                parts.append(x.reshape(N_G * PENCIL, x.shape[2]))
            for k, piece in enumerate(pack_four(parts)):
                dq_ref[where, :, :, k * 128 : (k + 1) * 128] = piece.reshape(N_G, PENCIL, 128)


def grads(chunk, place, qa, qb, kv, sa, sb, ta, tb, *so_far):
    vmem = pl.BlockSpec(memory_space=pltpu.VMEM)
    last = chunk == CHUNKS - 1
    return pl.pallas_call(
        functools.partial(grads_kernel, chunk),
        out_shape=(
            jax.ShapeDtypeStruct((N_Y, N_G, PENCIL, WIDE), BF16) if last else jax.ShapeDtypeStruct((HD, 4 * PQ), F32),
            jax.ShapeDtypeStruct((N_Z * N_G, HALF // CHUNKS, WIDE), BF16),
        ),
        in_specs=[pl.BlockSpec(memory_space=pltpu.SMEM)] + [vmem] * (7 + len(so_far)),
        out_specs=(vmem, vmem),
        scratch_shapes=[pltpu.VMEM((4 * PQ, 128), BF16)] * 2
        + [pltpu.VMEM((2 * PK // CHUNKS, 128), BF16)] * 2
        + [pltpu.VMEM((HD, 2 * PK // CHUNKS), BF16)]
        + [pltpu.VMEM((HD, 4 * PQ) if last else (8, 128), F32)]
        + [pltpu.VMEM((2 * PK // CHUNKS, 128), BF16)] * 2
        + [pltpu.VMEM((8, 4 * PQ), F32)] * 2,
        cost_estimate=pl.CostEstimate(
            flops=10 * 4 * PQ * 2 * PK * 128 // CHUNKS * 2,
            transcendentals=4 * PQ * 2 * PK // CHUNKS,
            bytes_accessed=8 << 20,
        ),
        name="grads",
    )(place, qa, qb, kv, sa, sb, ta, tb, *so_far)


def keys_out_kernel(*refs):
    key_ref, value_ref = refs[CHUNKS:]
    size = HALF // CHUNKS
    for n, got_ref in enumerate(refs[:CHUNKS]):
        for h in range(H):
            total = got_ref[0, h].astype(F32)
            for z in range(1, N_Z):
                total = total + got_ref[z, h].astype(F32)
            total = total.astype(BF16)
            for half in range(2):
                lane = half * 2 * HD
                rows = slice(half * HALF + n * size, half * HALF + (n + 1) * size)
                key_ref[rows, h * HD : (h + 1) * HD] = total[:, lane : lane + HD]
                value_ref[rows, h * HD : (h + 1) * HD] = total[:, lane + HD : lane + 2 * HD]


def queries_out_kernel(got_ref, query_ref):
    for h in range(H):
        total = (got_ref[0, h].astype(F32) + got_ref[1, h].astype(F32)).astype(BF16)
        for quarter in range(4):
            rows = slice(quarter * PENCIL, (quarter + 1) * PENCIL)
            query_ref[rows, h * HD : (h + 1) * HD] = total[:, quarter * HD : (quarter + 1) * HD]


def placed_out(kernel, got, outs):
    vmem = pl.BlockSpec(memory_space=pltpu.VMEM)
    return pl.pallas_call(
        kernel,
        out_shape=[jax.ShapeDtypeStruct((PD, D), BF16)] * outs,
        in_specs=[vmem] * len(got),
        out_specs=[vmem] * outs,
    )(*got)


def layer(obj_query, grad_out, pattern_key, pattern_value, pencil_order):
    place = jnp.stack([lax.axis_index("blk_1"), lax.axis_index(GRP)]).astype(jnp.int32)
    swap = functools.partial(lax.ppermute, axis_name="blk_1", perm=((0, 1), (1, 0)))
    sent = pack(pencil_order, place, obj_query, grad_out, pattern_key, pattern_value)
    got = lax.all_to_all(sent, GRP, 0, 0, tiled=True)
    qa = got[:, KR:, :]
    qb = swap(qa)
    sa = stats(qa, got)
    ta = swap(sa)
    sb = stats(qb, got)
    tb = swap(sb)
    so_far, pieces = (), []
    for chunk in range(CHUNKS):
        dq, dkv = grads(chunk, place, qa, qb, got, sa, sb, ta, tb, *so_far)
        so_far = (dq,)
        dkv = lax.all_to_all(dkv, ("blk_0", *GRP), 0, 0, tiled=True)
        pieces.append(dkv.reshape(N_Z, N_G, HALF // CHUNKS, WIDE))
    dq = lax.all_to_all(dq.reshape(N_Y * N_G, PENCIL, WIDE), ("blk_1", *GRP), 0, 0, tiled=True)
    (query_grad,) = placed_out(queries_out_kernel, [dq.reshape(N_Y, N_G, PENCIL, WIDE)], 1)
    key_grad, value_grad = placed_out(keys_out_kernel, pieces, 2)
    return query_grad, key_grad, value_grad


def solution(mesh):
    split = Mesh(mesh.devices.reshape(4, 2, 2, 4, 2), BLK_GRP)
    return jax.shard_map(
        layer,
        mesh=split,
        in_specs=(P(BLK_GRP, None), P(BLK_GRP, None), P(GRP, None), P(GRP, None), P()),
        out_specs=(P(BLK_GRP, None), P(BLK_GRP, None), P(BLK_GRP, None)),
        check_vma=False,
    )
```

time: 181 us -> 163 us (0.901)
  Pallas kernels: 90.3 us -> 60 us
  blocking collectives: 48.8 us -> 72 us
  waiting for transfers between devices: 24.4 us -> 16.2 us
  starting transfers between devices: 12.7 us -> 10.4 us
    all_to_all x2 -> x3, blocking collectives: 48.8 us -> 72 us  [the longest x1 31.8 us: layer(): got = lax.all_to_all(sent, GRP, 0, 0, tiled=True)]
    pallas_call x2 -> x3, Pallas kernels: 59.5 us -> 39.1 us  [the longest x2 34.3 us: grads(): pl.pallas_call(functools.partial(grads_kernel, chunk), out_shape=(jax.Sha...]
    pallas_call x2, Pallas kernels: 26.6 us -> 16.7 us  [stats(): pl.pallas_call(stats_kernel, out_shape=jax.ShapeDtypeStruct((8, 2 * PQ),...]
    all_to_all x1, waiting for transfers between devices: 21.6 us -> 13.4 us  [layer(): dkv = lax.all_to_all(dkv, ('blk_0', *GRP), 0, 0, tiled=True)]
    all_to_all x1, starting transfers between devices: 7.03 us -> 4.7 us  [layer(): dkv = lax.all_to_all(dkv, ('blk_0', *GRP), 0, 0, tiled=True)]
  transfers between devices with their start and end apart: 4 -> 4, of which waited for: 2 -> 2; matrix products, arithmetic and copies ran while one was open for 0% -> 0% of each run, Pallas kernels for 16% -> 11%
where the time goes in v2:
time: 163 us; the launch traced here: 162 us
  blocking collectives  72 us (44%)
  Pallas kernels  60 us (37%)
  waiting for transfers between devices  16.2 us (10%)
  starting transfers between devices  10.4 us (6%)
  local copies, waits for them, and re-layouts  2.33 us (1%)
    pallas_call x2, Pallas kernels, grads(): pl.pallas_call(functools.partial(grads_kernel, chunk), out_shape=(jax.Sha...  34.3 us
    all_to_all x1, blocking collectives, layer(): got = lax.all_to_all(sent, GRP, 0, 0, tiled=True)  31.8 us
    all_to_all x1, blocking collectives, layer(): dkv = lax.all_to_all(dkv, ('blk_0', *GRP), 0, 0, tiled=True)  22.4 us
    all_to_all x1, blocking collectives, layer(): lax.all_to_all(dq.reshape(N_Y * N_G, PENCIL, WIDE), ('blk_1', *GRP), 0, 0...  17.8 us
    pallas_call x2, Pallas kernels, stats(): pl.pallas_call(stats_kernel, out_shape=jax.ShapeDtypeStruct((8, 2 * PQ),...  16.7 us
    all_to_all x1, waiting for transfers between devices, layer(): dkv = lax.all_to_all(dkv, ('blk_0', *GRP), 0, 0, tiled=True)  13.4 us
    pallas_call x1, Pallas kernels, pack(): pl.pallas_call(pack_kernel, out_shape=jax.ShapeDtypeStruct((H, SR, WIDE),...  4.76 us
    all_to_all x1, starting transfers between devices, layer(): dkv = lax.all_to_all(dkv, ('blk_0', *GRP), 0, 0, tiled=True)  4.7 us
  transfers between devices with their start and end apart: 4, of which 2 were waited for; matrix products, arithmetic and copies ran while one was open for 0% of the time, Pallas kernels for 11%

profile of v2, /device:TPU:1, one launch (start us, length us, event | category | flops | bytes accessed | tf_op | source)
XLA Modules:
  0.0 162.3 jit_solution(2876513551670348714)
XLA Ops:
  0.6 0.7 pad_add_fusion.place_ref
  1.3 4.8 %pack.1 = bf16[16,160,384]{2,1,0:T(8,128)(2,1)} custom-call(s32[512]{0:T(512)} %order_ref.1, s32[2]{0:T(128)} %pad_add_fusion.place_ref, bf16[64,1536]{1,0:T(8,128)(2,1)} %q_ref.1, bf16[64,1536]{1,0:T(8,128)(2,1)} %g_ref.1, bf16[512,1536]{1,0:T(8,128)(2,1)} %k_ref.1, bf16[512,1536]{1,0:T(8,128)(2,1)} %v_ref.1), custom_call_target="tpu_custom_call" | custom-call | tf_op jit(solution)/shard_map/pack/pallas_call | solution.py:103
  6.1 31.8 %all_to_all.20.kv_ref = bf16[16,160,384]{2,1,0:T(8,128)(2,1)S(1)} all-to-all(bf16[16,160,384]{2,1,0:T(8,128)(2,1)} %pack.1), channel_id=1, replica_groups=mesh['blk_0'=4,'blk_1'=2,'grp_0'=2,'grp_1'=4,'grp_2'=2] {'grp_0','grp_1'..., dimensions={0} | all-to-all | bytes 3932160 | tf_op jit(solution)/shard_map/all_to_all | solution.py:339
  37.9 0.0 copy-start.2
  38.0 2.7 %collective-permute-start = (bf16[16,32,384]{2,1,0:T(8,128)(2,1)S(1)}, bf16[16,32,384]{2,1,0:T(8,128)(2,1)S(1)}, u32[]{:S(2)}, u32[]{:S(2)}) collective-permute-start(bf16[16,32,384]{2,1,0:T(8,128)(2,1)S(1)} %slice.4.q_ref.qa_ref), channel_id=1, source_target_pairs={{0,16},{16,0},{1,17},{17,1},{2,18},{18,2},{3,19},{19,3},{4,20},{20... | collective-permute-start | bytes 1179656 | tf_op jit(solution)/shard_map/ppermute | solution.py:341
  40.7 0.0 copy-done.1
  40.7 8.3 %stats.2.sa_ref = f32[8,1024]{1,0:T(8,128)} custom-call(bf16[16,32,384]{2,1,0:T(8,128)(2,1)} %copy-done.2, bf16[16,160,384]{2,1,0:T(8,128)(2,1)} %copy-done.1), custom_call_target="tpu_custom_call" | custom-call | flops 4294967296 | bytes 4194304 | tf_op jit(solution)/shard_map/stats/pallas_call | solution.py:192
  49.0 1.3 collective-permute-start.1
  50.3 0.0 collective-permute-done.q_ref.qb_ref
  50.3 0.8 copy-done.3
  51.1 8.3 %stats.3.sb_ref = f32[8,1024]{1,0:T(8,128)} custom-call(bf16[16,32,384]{2,1,0:T(8,128)(2,1)} %copy-done.3, bf16[16,160,384]{2,1,0:T(8,128)(2,1)} %copy-done.1), custom_call_target="tpu_custom_call" | custom-call | flops 4294967296 | bytes 4194304 | tf_op jit(solution)/shard_map/stats/pallas_call | solution.py:192
  59.4 1.6 %collective-permute-start.2 = (f32[8,1024]{1,0:T(8,128)}, f32[8,1024]{1,0:T(8,128)S(1)}, u32[]{:S(2)}, u32[]{:S(2)}) collective-permute-start(f32[8,1024]{1,0:T(8,128)} %stats.3.sb_ref), channel_id=1, source_target_pairs={{0,16},{16,0},{1,17},{17,1},{2,18},{18,2},{3,19},{19,3},{4,20},{20... | collective-permute-start | bytes 98312 | tf_op jit(solution)/shard_map/ppermute | solution.py:345
  61.1 0.0 collective-permute-done.1.ta_ref
  61.1 2.8 %collective-permute-done.2.tb_ref = f32[8,1024]{1,0:T(8,128)S(1)} collective-permute-done((f32[8,1024]{1,0:T(8,128)}, f32[8,1024]{1,0:T(8,128)S(1)}, u32[]{:S(2)}, u32[]{:S(2)}) %collective-permute-start.2) | collective-permute-done | bytes 32800 | tf_op jit(solution)/shard_map/ppermute | solution.py:345
  63.9 0.6 copy-done.5
  64.5 16.9 %grads.2 = (f32[96,2048]{1,0:T(8,128)}, bf16[64,16,384]{2,1,0:T(8,128)(2,1)}) custom-call(s32[2]{0:T(128)} %pad_add_fusion.place_ref, bf16[16,32,384]{2,1,0:T(8,128)(2,1)} %copy-done.2, bf16[16,32,384]{2,1,0:T(8,128)(2,1)} %copy-done.3, bf16[16,160,384]{2,1,0:T(8,128)(2,1)} %copy-done.1, f32[8,1024]{1,0:T(8,128)} %stats.2.sa_ref, f32[8,1024]{1,0:T(8,128)} %stats.3.sb_ref, ...), custom_call_target="tpu_custom_call" | custom-call | flops 10737418240 | bytes 8388608 | tf_op jit(solution)/shard_map/grads/pallas_call | solution.py:278
  81.5 17.4 %grads.3 = (bf16[2,16,16,384]{3,2,1,0:T(8,128)(2,1)}, bf16[64,16,384]{2,1,0:T(8,128)(2,1)}) custom-call(s32[2]{0:T(128)} %pad_add_fusion.place_ref, bf16[16,32,384]{2,1,0:T(8,128)(2,1)} %copy-done.2, bf16[16,32,384]{2,1,0:T(8,128)(2,1)} %copy-done.3, bf16[16,160,384]{2,1,0:T(8,128)(2,1)} %copy-done.1, f32[8,1024]{1,0:T(8,128)} %stats.2.sa_ref, ...), custom_call_target="tpu_custom_call" | custom-call | flops 10737418240 | bytes 8388608 | tf_op jit(solution)/shard_map/grads/pallas_call | solution.py:278
  98.9 17.8 %all_to_all.21 = bf16[32,16,384]{2,1,0:T(8,128)(2,1)} all-to-all(bf16[32,16,384]{2,1,0:T(8,128)(2,1)} %bitcast.9), channel_id=1, replica_groups=mesh['blk_0'=4,'blk_1'=2,'grp_0'=2,'grp_1'=4,'grp_2'=2] {'blk_1','grp_0'..., dimensions={0} | all-to-all | bytes 786432 | tf_op jit(solution)/shard_map/all_to_all | solution.py:352
  116.6 22.4 %all_to_all.22 = bf16[64,16,384]{2,1,0:T(8,128)(2,1)} all-to-all(bf16[64,16,384]{2,1,0:T(8,128)(2,1)} %get-tuple-element.12), channel_id=1, replica_groups=mesh['blk_0'=4,'blk_1'=2,'grp_0'=2,'grp_1'=4,'grp_2'=2] {'blk_0','grp_0'..., dimensions={0} | all-to-all | bytes 1572864 | tf_op jit(solution)/shard_map/all_to_all | solution.py:350
  139.0 4.7 %all-to-all-start.2 = ((bf16[64,16,384]{2,1,0:T(8,128)(2,1)}), bf16[64,16,384]{2,1,0:T(8,128)(2,1)S(1)}, u32[]{:S(2)}, u32[]{:S(2)}) async-start(bf16[64,16,384]{2,1,0:T(8,128)(2,1)} %get-tuple-element.11), calls=%async_computation.2 | async-start | bytes 1572864 | tf_op jit(solution)/shard_map/all_to_all | solution.py:350
  143.7 1.8 %shard_map.76 = bf16[64,1536]{1,0:T(8,128)(2,1)} custom-call(bf16[2,16,16,384]{3,2,1,0:T(8,128)(2,1)} %bitcast.8), custom_call_target="tpu_custom_call" | custom-call | tf_op jit(solution)/shard_map/pallas_call | solution.py:327
  145.5 13.4 %all-to-all-done.2 = bf16[64,16,384]{2,1,0:T(8,128)(2,1)S(1)} async-done(((bf16[64,16,384]{2,1,0:T(8,128)(2,1)}), bf16[64,16,384]{2,1,0:T(8,128)(2,1)S(1)}, u32[]{:S(2)}, u32[]{:S(2)}) %all-to-all-start.2) | async-done | bytes 786464 | tf_op jit(solution)/shard_map/all_to_all | solution.py:350
  159.0 0.9 copy-done
  159.9 2.4 %shard_map.77 = (bf16[64,1536]{1,0:T(8,128)(2,1)}, bf16[64,1536]{1,0:T(8,128)(2,1)}) custom-call(bf16[4,16,16,384]{3,2,1,0:T(8,128)(2,1)} %bitcast.7, bf16[4,16,16,384]{3,2,1,0:T(8,128)(2,1)} %bitcast.6), custom_call_target="tpu_custom_call" | custom-call | tf_op jit(solution)/shard_map/pallas_call | solution.py:327
  (8 shorter events, 0.1 us)
Async XLA Ops:
  37.9 2.8 %copy-start.1 = (bf16[16,160,384]{2,1,0:T(8,128)(2,1)}, bf16[16,160,384]{2,1,0:T(8,128)(2,1)S(1)}, u32[]{:S(2)}) copy-start(bf16[16,160,384]{2,1,0:T(8,128)(2,1)S(1)} %all_to_all.20.kv_ref) | copy-start | bytes 5898244
  37.9 2.7 %copy-start.2 = (bf16[16,32,384]{2,1,0:T(8,128)(2,1)}, bf16[16,32,384]{2,1,0:T(8,128)(2,1)S(1)}, u32[]{:S(2)}) copy-start(bf16[16,32,384]{2,1,0:T(8,128)(2,1)S(1)} %slice.4.q_ref.qa_ref) | copy-start | bytes 1179652
  38.0 12.4 %collective-permute-start = (bf16[16,32,384]{2,1,0:T(8,128)(2,1)S(1)}, bf16[16,32,384]{2,1,0:T(8,128)(2,1)S(1)}, u32[]{:S(2)}, u32[]{:S(2)}) collective-permute-start(bf16[16,32,384]{2,1,0:T(8,128)(2,1)S(1)} %slice.4.q_ref.qa_ref), channel_id=1, source_target_pairs={{0,16},{16,0},{1,17},{17,1},{2,18},{18,2},{3,19},{19,3},{4,20},{20... | collective-permute-start | bytes 1179656 | tf_op jit(solution)/shard_map/ppermute | solution.py:341
  49.0 12.1 %collective-permute-start.1 = (f32[8,1024]{1,0:T(8,128)}, f32[8,1024]{1,0:T(8,128)S(1)}, u32[]{:S(2)}, u32[]{:S(2)}) collective-permute-start(f32[8,1024]{1,0:T(8,128)} %stats.2.sa_ref), channel_id=1, source_target_pairs={{0,16},{16,0},{1,17},{17,1},{2,18},{18,2},{3,19},{19,3},{4,20},{20... | collective-permute-start | bytes 98312 | tf_op jit(solution)/shard_map/ppermute | solution.py:343
  50.3 0.8 copy-start.3
  59.4 4.5 %collective-permute-start.2 = (f32[8,1024]{1,0:T(8,128)}, f32[8,1024]{1,0:T(8,128)S(1)}, u32[]{:S(2)}, u32[]{:S(2)}) collective-permute-start(f32[8,1024]{1,0:T(8,128)} %stats.3.sb_ref), channel_id=1, source_target_pairs={{0,16},{16,0},{1,17},{17,1},{2,18},{18,2},{3,19},{19,3},{4,20},{20... | collective-permute-start | bytes 98312 | tf_op jit(solution)/shard_map/ppermute | solution.py:345
  61.1 2.8 %copy-start.4 = (f32[8,1024]{1,0:T(8,128)}, f32[8,1024]{1,0:T(8,128)S(1)}, u32[]{:S(2)}) copy-start(f32[8,1024]{1,0:T(8,128)S(1)} %collective-permute-done.1.ta_ref) | copy-start | bytes 98308
  63.9 0.6 copy-start.5
  139.0 20.0 %all-to-all-start.2 = ((bf16[64,16,384]{2,1,0:T(8,128)(2,1)}), bf16[64,16,384]{2,1,0:T(8,128)(2,1)S(1)}, u32[]{:S(2)}, u32[]{:S(2)}) async-start(bf16[64,16,384]{2,1,0:T(8,128)(2,1)} %get-tuple-element.11), calls=%async_computation.2 | async-start | bytes 1572864 | tf_op jit(solution)/shard_map/all_to_all | solution.py:350
  159.0 0.9 copy-start

commit v3 on v2

--- a/solution.py
+++ b/solution.py
@@ -21,6 +21,9 @@
 N_Y = 2
 N_G = 16
 GRP = ("grp_0", "grp_1", "grp_2")
+HEADS = ("blk_1", "grp_0", "grp_1")
+Z = "blk_0"
+CORE = "grp_2"
 BLK_GRP = ("blk_0", "blk_1", "grp_0", "grp_1", "grp_2")
 SCALE = 1.0 / math.sqrt(HD)
 C2 = SCALE * math.log2(math.e)
@@ -153,9 +156,10 @@
     )
 
 
-def stats_kernel(q_ref, kv_ref, st_ref, q_s, g_s, k_s, v_s):
+def stats_kernel(qa_ref, qb_ref, kv_ref, st_ref, q_s, g_s, k_s, v_s):
     unpack_keys(kv_ref, k_s, v_s, 0, 1)
-    unpack_queries(q_ref, q_s, g_s, 0)
+    unpack_queries(qa_ref, q_s, g_s, 0)
+    unpack_queries(qb_ref, q_s, g_s, 2 * PQ)
 
     def one_tile(t, _):
         q0 = pl.multiple_of(t * STQ, STQ)
@@ -183,23 +187,23 @@
         st_ref[2:3, pl.ds(q0, STQ)] = jnp.sum(w * fade, axis=0, keepdims=True)
         return 0
 
-    lax.fori_loop(0, 2 * PQ // STQ, one_tile, 0)
-    st_ref[3:8, :] = jnp.zeros((5, 2 * PQ), F32)
-
-
-def stats(q, kv):
+    lax.fori_loop(0, 4 * PQ // STQ, one_tile, 0)
+    st_ref[3:8, :] = jnp.zeros((5, 4 * PQ), F32)
+
+
+def stats(qa, qb, kv):
     vmem = pl.BlockSpec(memory_space=pltpu.VMEM)
     return pl.pallas_call(
         stats_kernel,
-        out_shape=jax.ShapeDtypeStruct((8, 2 * PQ), F32),
-        in_specs=[vmem, vmem],
+        out_shape=jax.ShapeDtypeStruct((8, 4 * PQ), F32),
+        in_specs=[vmem] * 3,
         out_specs=vmem,
-        scratch_shapes=[pltpu.VMEM((128, 2 * PQ), BF16)] * 2 + [pltpu.VMEM((2 * PK, 128), BF16)] * 2,
+        scratch_shapes=[pltpu.VMEM((128, 4 * PQ), BF16)] * 2 + [pltpu.VMEM((2 * PK, 128), BF16)] * 2,
         cost_estimate=pl.CostEstimate(
-            flops=4 * 2 * PQ * 2 * PK * 256, transcendentals=2 * PQ * 2 * PK, bytes_accessed=4 << 20
+            flops=4 * 4 * PQ * 2 * PK * 256, transcendentals=4 * PQ * 2 * PK, bytes_accessed=4 << 20
         ),
         name="stats",
-    )(q, kv)
+    )(qa, qb, kv)
 
 
 def joined(mine, theirs):
@@ -210,19 +214,22 @@
     return top * C2 + jnp.log2(total), (mine[2:3] * a + theirs[2:3] * b) / total
 
 
-def grads_kernel(chunk, place_ref, qa_ref, qb_ref, kv_ref, sa_ref, sb_ref, ta_ref, tb_ref, *refs):
+def grads_kernel(chunk, place_ref, qa_ref, qb_ref, kv_ref, mine_ref, theirs_ref, *refs):
     first, last = chunk == 0, chunk == CHUNKS - 1
     so_far_ref = None if first else refs[0]
-    dq_ref, dkv_ref, q_s, g_s, k_s, v_s, t_s, dq_s, dk_s, dv_s, log_s, mean_s = refs[0 if first else 1 :]
+    refs = refs[0 if first else 1 :]
+    dq_refs, dkv_refs = (refs[:2], refs[2:6]) if last else (refs[:1], refs[1:5])
+    q_s, g_s, k_s, v_s, t_s, dq_s, dk_s, dv_s, log_s, mean_s, out_s = refs[6 if last else 5 :]
     if not last:
-        dq_s = dq_ref
+        dq_s = dq_refs[0]
     unpack_keys(kv_ref, k_s, v_s, chunk, CHUNKS, t_s)
     unpack_query_rows(qa_ref, q_s, g_s, 0)
     unpack_query_rows(qb_ref, q_s, g_s, 2 * PQ)
-    for n, (mine, theirs) in enumerate(((sa_ref, tb_ref), (sb_ref, ta_ref))):
-        log_now, mean_now = joined(mine, theirs)
-        log_s[:, n * 2 * PQ : (n + 1) * 2 * PQ] = jnp.broadcast_to(log_now, (8, 2 * PQ))
-        mean_s[:, n * 2 * PQ : (n + 1) * 2 * PQ] = jnp.broadcast_to(mean_now, (8, 2 * PQ))
+    for n in range(2):
+        here, there = slice(n * 2 * PQ, (n + 1) * 2 * PQ), slice((1 - n) * 2 * PQ, (2 - n) * 2 * PQ)
+        log_now, mean_now = joined(mine_ref[:, here], theirs_ref[:, there])
+        log_s[:, here] = jnp.broadcast_to(log_now, (8, 2 * PQ))
+        mean_s[:, here] = jnp.broadcast_to(mean_now, (8, 2 * PQ))
     dq_s[...] = jnp.zeros_like(dq_s) if first else so_far_ref[...]
 
     def one_chunk(j, _):
@@ -258,10 +265,12 @@
         for n, (ref, half) in enumerate(((dk_s, 0), (dv_s, 0), (dk_s, 1), (dv_s, 1)))
     ]
     for n, piece in enumerate(pack_four(parts)):
-        dkv_ref[:, :, n * 128 : (n + 1) * 128] = piece.reshape(N_Z * N_G, HALF // CHUNKS, 128)
+        out_s[:, :, n * 128 : (n + 1) * 128] = piece.reshape(N_Z, rows // N_Z, 128)
+    z = place_ref[2]
+    for step, ref in enumerate(dkv_refs):
+        ref[...] = out_s[(z + step) % N_Z].reshape(N_G, HALF // CHUNKS, WIDE)
     if last:
-        y = place_ref[0]
-        for n, where in enumerate((y, 1 - y)):
+        for n, ref in enumerate(dq_refs):
             parts = []
             for quarter in range(4):
                 r0 = n * 2 * PQ + quarter // 2 * PQ
@@ -269,90 +278,106 @@
                 x = x.reshape(N_G, 2, PENCIL, x.shape[1])[:, quarter % 2]
                 parts.append(x.reshape(N_G * PENCIL, x.shape[2]))
             for k, piece in enumerate(pack_four(parts)):
-                dq_ref[where, :, :, k * 128 : (k + 1) * 128] = piece.reshape(N_G, PENCIL, 128)
-
-
-def grads(chunk, place, qa, qb, kv, sa, sb, ta, tb, *so_far):
+                ref[:, :, k * 128 : (k + 1) * 128] = piece.reshape(N_G, PENCIL, 128)
+
+
+def grads(chunk, place, qa, qb, kv, mine, theirs, *so_far):
     vmem = pl.BlockSpec(memory_space=pltpu.VMEM)
     last = chunk == CHUNKS - 1
+    outs = [jax.ShapeDtypeStruct((N_G, HALF // CHUNKS, WIDE), BF16)] * N_Z
+    if last:
+        outs = [jax.ShapeDtypeStruct((N_G, PENCIL, WIDE), BF16)] * 2 + outs
+    else:
+        outs = [jax.ShapeDtypeStruct((HD, 4 * PQ), F32)] + outs
     return pl.pallas_call(
         functools.partial(grads_kernel, chunk),
-        out_shape=(
-            jax.ShapeDtypeStruct((N_Y, N_G, PENCIL, WIDE), BF16) if last else jax.ShapeDtypeStruct((HD, 4 * PQ), F32),
-            jax.ShapeDtypeStruct((N_Z * N_G, HALF // CHUNKS, WIDE), BF16),
-        ),
-        in_specs=[pl.BlockSpec(memory_space=pltpu.SMEM)] + [vmem] * (7 + len(so_far)),
-        out_specs=(vmem, vmem),
+        out_shape=outs,
+        in_specs=[pl.BlockSpec(memory_space=pltpu.SMEM)] + [vmem] * (5 + len(so_far)),
+        out_specs=[vmem] * len(outs),
         scratch_shapes=[pltpu.VMEM((4 * PQ, 128), BF16)] * 2
         + [pltpu.VMEM((2 * PK // CHUNKS, 128), BF16)] * 2
         + [pltpu.VMEM((HD, 2 * PK // CHUNKS), BF16)]
         + [pltpu.VMEM((HD, 4 * PQ) if last else (8, 128), F32)]
         + [pltpu.VMEM((2 * PK // CHUNKS, 128), BF16)] * 2
-        + [pltpu.VMEM((8, 4 * PQ), F32)] * 2,
+        + [pltpu.VMEM((8, 4 * PQ), F32)] * 2
+        + [pltpu.VMEM((N_Z, N_G * HALF // CHUNKS, WIDE), BF16)],
         cost_estimate=pl.CostEstimate(
             flops=10 * 4 * PQ * 2 * PK * 128 // CHUNKS * 2,
             transcendentals=4 * PQ * 2 * PK // CHUNKS,
             bytes_accessed=8 << 20,
         ),
         name="grads",
-    )(place, qa, qb, kv, sa, sb, ta, tb, *so_far)
-
-
-def keys_out_kernel(*refs):
-    key_ref, value_ref = refs[CHUNKS:]
-    size = HALF // CHUNKS
-    for n, got_ref in enumerate(refs[:CHUNKS]):
-        for h in range(H):
-            total = got_ref[0, h].astype(F32)
-            for z in range(1, N_Z):
-                total = total + got_ref[z, h].astype(F32)
-            total = total.astype(BF16)
-            for half in range(2):
-                lane = half * 2 * HD
-                rows = slice(half * HALF + n * size, half * HALF + (n + 1) * size)
-                key_ref[rows, h * HD : (h + 1) * HD] = total[:, lane : lane + HD]
-                value_ref[rows, h * HD : (h + 1) * HD] = total[:, lane + HD : lane + 2 * HD]
-
-
-def queries_out_kernel(got_ref, query_ref):
+    )(place, qa, qb, kv, mine, theirs, *so_far)
+
+
+def combine_kernel(*refs):
+    out_ref = refs[-1]
+    row = 0
+    for parts in [refs[n * N_Z : (n + 1) * N_Z] for n in range(CHUNKS)] + [refs[CHUNKS * N_Z : -1]]:
+        total = parts[0][...].astype(F32)
+        for part in parts[1:]:
+            total = total + part[...].astype(F32)
+        out_ref[:, row : row + total.shape[1], :] = total.astype(BF16)
+        row += total.shape[1]
+
+
+def combine(parts):
+    vmem = pl.BlockSpec(memory_space=pltpu.VMEM)
+    return pl.pallas_call(
+        combine_kernel,
+        out_shape=jax.ShapeDtypeStruct((N_G, HALF + PENCIL, WIDE), BF16),
+        in_specs=[vmem] * len(parts),
+        out_specs=vmem,
+        name="combine",
+    )(*parts)
+
+
+def finish_kernel(got_ref, query_ref, key_ref, value_ref):
     for h in range(H):
-        total = (got_ref[0, h].astype(F32) + got_ref[1, h].astype(F32)).astype(BF16)
+        here = slice(h * HD, (h + 1) * HD)
+        for half in range(2):
+            lane = half * 2 * HD
+            rows = slice(half * HALF, (half + 1) * HALF)
+            key_ref[rows, here] = got_ref[h, :HALF, lane : lane + HD]
+            value_ref[rows, here] = got_ref[h, :HALF, lane + HD : lane + 2 * HD]
         for quarter in range(4):
             rows = slice(quarter * PENCIL, (quarter + 1) * PENCIL)
-            query_ref[rows, h * HD : (h + 1) * HD] = total[:, quarter * HD : (quarter + 1) * HD]
-
-
-def placed_out(kernel, got, outs):
-    vmem = pl.BlockSpec(memory_space=pltpu.VMEM)
-    return pl.pallas_call(
-        kernel,
-        out_shape=[jax.ShapeDtypeStruct((PD, D), BF16)] * outs,
-        in_specs=[vmem] * len(got),
-        out_specs=[vmem] * outs,
-    )(*got)
+            query_ref[rows, here] = got_ref[h, HALF:, quarter * HD : (quarter + 1) * HD]
+
+
+def finish(got):
+    vmem = pl.BlockSpec(memory_space=pltpu.VMEM)
+    return pl.pallas_call(
+        finish_kernel,
+        out_shape=[jax.ShapeDtypeStruct((PD, D), BF16)] * 3,
+        in_specs=[vmem],
+        out_specs=[vmem] * 3,
+        name="finish",
+    )(got)
 
 
 def layer(obj_query, grad_out, pattern_key, pattern_value, pencil_order):
-    place = jnp.stack([lax.axis_index("blk_1"), lax.axis_index(GRP)]).astype(jnp.int32)
-    swap = functools.partial(lax.ppermute, axis_name="blk_1", perm=((0, 1), (1, 0)))
+    place = jnp.stack([lax.axis_index("blk_1"), lax.axis_index(GRP), lax.axis_index(Z)]).astype(jnp.int32)
+    swap = functools.partial(lax.ppermute, axis_name=CORE, perm=((0, 1), (1, 0)))
     sent = pack(pencil_order, place, obj_query, grad_out, pattern_key, pattern_value)
-    got = lax.all_to_all(sent, GRP, 0, 0, tiled=True)
+    got = lax.all_to_all(sent, HEADS, 0, 0, tiled=True)
     qa = got[:, KR:, :]
     qb = swap(qa)
-    sa = stats(qa, got)
-    ta = swap(sa)
-    sb = stats(qb, got)
-    tb = swap(sb)
-    so_far, pieces = (), []
+    mine = stats(qa, qb, got)
+    theirs = swap(mine)
+    so_far, parts = (), []
     for chunk in range(CHUNKS):
-        dq, dkv = grads(chunk, place, qa, qb, got, sa, sb, ta, tb, *so_far)
-        so_far = (dq,)
-        dkv = lax.all_to_all(dkv, ("blk_0", *GRP), 0, 0, tiled=True)
-        pieces.append(dkv.reshape(N_Z, N_G, HALF // CHUNKS, WIDE))
-    dq = lax.all_to_all(dq.reshape(N_Y * N_G, PENCIL, WIDE), ("blk_1", *GRP), 0, 0, tiled=True)
-    (query_grad,) = placed_out(queries_out_kernel, [dq.reshape(N_Y, N_G, PENCIL, WIDE)], 1)
-    key_grad, value_grad = placed_out(keys_out_kernel, pieces, 2)
-    return query_grad, key_grad, value_grad
+        outs = grads(chunk, place, qa, qb, got, mine, theirs, *so_far)
+        so_far = (outs[0],)
+        pieces = outs[-N_Z:]
+        parts.append(pieces[0])
+        for step in range(1, N_Z):
+            perm = tuple((k, (k + step) % N_Z) for k in range(N_Z))
+            parts.append(lax.ppermute(pieces[step], Z, perm))
+    parts += [outs[0], swap(outs[1])]
+    total = combine(parts)
+    total = lax.all_to_all(total, HEADS, 0, 0, tiled=True)
+    return tuple(finish(total))
 
 
 def solution(mesh):

time: 163 us -> 134 us (0.82)
  blocking collectives: 72 us -> 49.1 us
  waiting for transfers between devices: 16.2 us -> 9.61 us
  Pallas kernels: 60 us -> 57.5 us
  starting transfers between devices: 10.4 us -> 12.9 us
    all_to_all x3 -> x2, blocking collectives: 72 us -> 49.1 us  [the longest x1 33.7 us: layer(): got = lax.all_to_all(sent, HEADS, 0, 0, tiled=True)]
    all_to_all x1 -> x0, waiting for transfers between devices: 13.4 us -> none  [layer(): dkv = lax.all_to_all(dkv, ('blk_0', *GRP), 0, 0, tiled=True)]
    ppermute x2 -> x8, starting transfers between devices: 2.97 us -> 11 us  [the longest x6 8.88 us: layer(): parts.append(lax.ppermute(pieces[step], Z, perm))]
    ppermute x2 -> x8, waiting for transfers between devices: 2.83 us -> 8.26 us  [the longest x6 7.15 us: layer(): parts.append(lax.ppermute(pieces[step], Z, perm))]
    all_to_all x1 -> x0, starting transfers between devices: 4.7 us -> none  [layer(): dkv = lax.all_to_all(dkv, ('blk_0', *GRP), 0, 0, tiled=True)]
    pallas_call x6 -> x5, Pallas kernels: 55.3 us -> 52.7 us  [the longest x2 34.3 us: grads(): pl.pallas_call(functools.partial(grads_kernel, chunk), out_shape=outs, in...]
  transfers between devices with their start and end apart: 4 -> 9, of which waited for: 2 -> 5; matrix products, arithmetic and copies ran while one was open for 0% -> 0% of each run, Pallas kernels for 11% -> 13%
where the time goes in v3:
time: 134 us; the launch traced here: 133 us
  Pallas kernels  57.5 us (43%)
  blocking collectives  49.1 us (37%)
  starting transfers between devices  12.9 us (10%)
  waiting for transfers between devices  9.61 us (7%)
  local copies, waits for them, and re-layouts  2.13 us (2%)
    pallas_call x2, Pallas kernels, grads(): pl.pallas_call(functools.partial(grads_kernel, chunk), out_shape=outs, in...  34.3 us
    all_to_all x1, blocking collectives, layer(): got = lax.all_to_all(sent, HEADS, 0, 0, tiled=True)  33.7 us
    all_to_all x1, blocking collectives, layer(): total = lax.all_to_all(total, HEADS, 0, 0, tiled=True)  15.4 us
    pallas_call x1, Pallas kernels, stats(): pl.pallas_call(stats_kernel, out_shape=jax.ShapeDtypeStruct((8, 4 * PQ),...  13.5 us
    ppermute x6, starting transfers between devices, layer(): parts.append(lax.ppermute(pieces[step], Z, perm))  8.88 us
    ppermute x6, waiting for transfers between devices, layer(): parts.append(lax.ppermute(pieces[step], Z, perm))  7.15 us
    pallas_call x1, Pallas kernels, pack(): pl.pallas_call(pack_kernel, out_shape=jax.ShapeDtypeStruct((H, SR, WIDE),...  4.74 us
  transfers between devices with their start and end apart: 9, of which 5 were waited for; matrix products, arithmetic and copies ran while one was open for 0% of the time, Pallas kernels for 13%

profile of v3, /device:TPU:1, one launch (start us, length us, event | category | flops | bytes accessed | tf_op | source)
XLA Modules:
  0.0 132.5 jit_solution(18316284120541101869)
XLA Ops:
  0.6 0.6 pad_add_fusion.place_ref
  1.2 4.7 %pack.1 = bf16[16,160,384]{2,1,0:T(8,128)(2,1)} custom-call(s32[512]{0:T(512)} %order_ref.1, s32[3]{0:T(128)} %pad_add_fusion.place_ref, bf16[64,1536]{1,0:T(8,128)(2,1)} %q_ref.1, bf16[64,1536]{1,0:T(8,128)(2,1)} %g_ref.1, bf16[512,1536]{1,0:T(8,128)(2,1)} %k_ref.1, bf16[512,1536]{1,0:T(8,128)(2,1)} %v_ref.1), custom_call_target="tpu_custom_call" | custom-call | tf_op jit(solution)/shard_map/pack/pallas_call | solution.py:106
  6.0 33.7 %all_to_all.10.kv_ref = bf16[16,160,384]{2,1,0:T(8,128)(2,1)S(1)} all-to-all(bf16[16,160,384]{2,1,0:T(8,128)(2,1)} %pack.1), channel_id=1, replica_groups=mesh['blk_0'=4,'blk_1'=2,'grp_0'=2,'grp_1'=4,'grp_2'=2] {'blk_1','grp_0'..., dimensions={0} | all-to-all | bytes 3932160 | tf_op jit(solution)/shard_map/all_to_all | solution.py:363
  39.8 1.9 %collective-permute-start = (bf16[16,32,384]{2,1,0:T(8,128)(2,1)S(1)}, bf16[16,32,384]{2,1,0:T(8,128)(2,1)S(1)}, u32[]{:S(2)}, u32[]{:S(2)}) collective-permute-start(bf16[16,32,384]{2,1,0:T(8,128)(2,1)S(1)} %slice.4.qa_ref), channel_id=1, source_target_pairs={{0,1},{1,0},{2,3},{3,2},{4,5},{5,4},{6,7},{7,6},{8,9},{9,8},{10,11... | collective-permute-start | bytes 1179656 | tf_op jit(solution)/shard_map/ppermute | solution.py:365
  41.6 1.3 %collective-permute-done.qb_ref = bf16[16,32,384]{2,1,0:T(8,128)(2,1)S(1)} collective-permute-done((bf16[16,32,384]{2,1,0:T(8,128)(2,1)S(1)}, bf16[16,32,384]{2,1,0:T(8,128)(2,1)S(1)}, u32[]{:S(2)}, u32[]{:S(2)}) %collective-permute-start) | collective-permute-done | bytes 393248 | tf_op jit(solution)/shard_map/ppermute | solution.py:365
  43.0 0.8 copy-done.9
  43.7 13.5 %stats.1.mine_ref = f32[8,2048]{1,0:T(8,128)} custom-call(bf16[16,32,384]{2,1,0:T(8,128)(2,1)} %copy-done.1, bf16[16,32,384]{2,1,0:T(8,128)(2,1)} %copy-done.9, bf16[16,160,384]{2,1,0:T(8,128)(2,1)} %copy-done), custom_call_target="tpu_custom_call" | custom-call | flops 8589934592 | bytes 4194304 | tf_op jit(solution)/shard_map/stats/pallas_call | solution.py:196
  57.7 1.1 collective-permute-done.1.theirs_ref
  58.8 0.6 copy-done.10
  59.4 16.9 %grads.2 = (f32[96,2048]{1,0:T(8,128)}, bf16[16,16,384]{2,1,0:T(8,128)(2,1)}, bf16[16,16,384]{2,1,0:T(8,128)(2,1)}, bf16[16,16,384]{2,1,0:T(8,128)(2,1)}, bf16[16,16,384]{2,1,0:T(8,128)(2,1)}) custom-call(s32[3]{0:T(128)} %pad_add_fusion.place_ref, bf16[16,32,384]{2,1,0:T(8,128)(2,1)} %copy-done.1, bf16[16,32,384]{2,1,0:T(8,128)(2,1)} %copy-done.9, ...), custom_call_target="tpu_custom_call" | custom-call | flops 10737418240 | bytes 8388608 | tf_op jit(solution)/shard_map/grads/pallas_call | solution.py:292
  76.3 1.6 %collective-permute-start.2 = (bf16[16,16,384]{2,1,0:T(8,128)(2,1)}, bf16[16,16,384]{2,1,0:T(8,128)(2,1)S(1)}, u32[]{:S(2)}, u32[]{:S(2)}) collective-permute-start(bf16[16,16,384]{2,1,0:T(8,128)(2,1)} %get-tuple-element.15), channel_id=1, source_target_pairs={{0,32},{32,64},{64,96},{96,0},{1,33},{33,65},{65,97},{97,1},{2,34}... | collective-permute-start | bytes 589832 | tf_op jit(solution)/shard_map/ppermute | solution.py:376
  78.0 3.3 %collective-permute-start.3 = (bf16[16,16,384]{2,1,0:T(8,128)(2,1)}, bf16[16,16,384]{2,1,0:T(8,128)(2,1)S(1)}, u32[]{:S(2)}, u32[]{:S(2)}) collective-permute-start(bf16[16,16,384]{2,1,0:T(8,128)(2,1)} %get-tuple-element.16), channel_id=1, source_target_pairs={{0,64},{32,96},{64,0},{96,32},{1,65},{33,97},{65,1},{97,33},{2,66}... | collective-permute-start | bytes 589832 | tf_op jit(solution)/shard_map/ppermute | solution.py:376
  81.3 0.7 collective-permute-start.4
  82.0 17.4 %grads.3 = (bf16[16,16,384]{2,1,0:T(8,128)(2,1)}, bf16[16,16,384]{2,1,0:T(8,128)(2,1)}, bf16[16,16,384]{2,1,0:T(8,128)(2,1)}, bf16[16,16,384]{2,1,0:T(8,128)(2,1...) custom-call(s32[3]{0:T(128)} %pad_add_fusion.place_ref, bf16[16,32,384]{2,1,0:T(8,128)(2,1)} %copy-done.1, ...), custom_call_target="tpu_custom_call" | custom-call | flops 10737418240 | bytes 8388608 | tf_op jit(solution)/shard_map/grads/pallas_call | solution.py:292
  99.4 0.7 collective-permute-start.5
  100.6 2.0 %collective-permute-start.7 = (bf16[16,16,384]{2,1,0:T(8,128)(2,1)}, bf16[16,16,384]{2,1,0:T(8,128)(2,1)S(1)}, u32[]{:S(2)}, u32[]{:S(2)}) collective-permute-start(bf16[16,16,384]{2,1,0:T(8,128)(2,1)} %get-tuple-element.22), channel_id=1, source_target_pairs={{0,96},{32,0},{64,32},{96,64},{1,97},{33,1},{65,33},{97,65},{2,98}... | collective-permute-start | bytes 589832 | tf_op jit(solution)/shard_map/ppermute | solution.py:376
  102.6 1.8 %collective-permute-start.8 = (bf16[16,16,384]{2,1,0:T(8,128)(2,1)}, bf16[16,16,384]{2,1,0:T(8,128)(2,1)S(1)}, u32[]{:S(2)}, u32[]{:S(2)}) collective-permute-start(bf16[16,16,384]{2,1,0:T(8,128)(2,1)} %get-tuple-element.24), channel_id=1, source_target_pairs={{0,1},{1,0},{2,3},{3,2},{4,5},{5,4},{6,7},{7,6},{8,9},{9,8},{10,11... | collective-permute-start | bytes 589832 | tf_op jit(solution)/shard_map/ppermute | solution.py:377
  104.4 3.2 %collective-permute-done.5.refs_5_ = bf16[16,16,384]{2,1,0:T(8,128)(2,1)S(1)} collective-permute-done((bf16[16,16,384]{2,1,0:T(8,128)(2,1)}, bf16[16,16,384]{2,1,0:T(8,128)(2,1)S(1)}, u32[]{:S(2)}, u32[]{:S(2)}) %collective-permute-start.5) | collective-permute-done | bytes 196640 | tf_op jit(solution)/shard_map/ppermute | solution.py:376
  107.6 1.6 %collective-permute-done.6.refs_6_ = bf16[16,16,384]{2,1,0:T(8,128)(2,1)S(1)} collective-permute-done((bf16[16,16,384]{2,1,0:T(8,128)(2,1)}, bf16[16,16,384]{2,1,0:T(8,128)(2,1)S(1)}, u32[]{:S(2)}, u32[]{:S(2)}) %collective-permute-start.6) | collective-permute-done | bytes 196640 | tf_op jit(solution)/shard_map/ppermute | solution.py:376
  109.1 2.4 %collective-permute-done.7.refs_7_ = bf16[16,16,384]{2,1,0:T(8,128)(2,1)S(1)} collective-permute-done((bf16[16,16,384]{2,1,0:T(8,128)(2,1)}, bf16[16,16,384]{2,1,0:T(8,128)(2,1)S(1)}, u32[]{:S(2)}, u32[]{:S(2)}) %collective-permute-start.7) | collective-permute-done | bytes 196640 | tf_op jit(solution)/shard_map/ppermute | solution.py:376
  111.6 0.6 copy-done.7
  112.2 2.6 %combine.1 = bf16[16,48,384]{2,1,0:T(8,128)(2,1)} custom-call(bf16[16,16,384]{2,1,0:T(8,128)(2,1)} %get-tuple-element.14.refs_0_, bf16[16,16,384]{2,1,0:T(8,128)(2,1)} %copy-done.2, bf16[16,16,384]{2,1,0:T(8,128)(2,1)} %copy-done.3, bf16[16,16,384]{2,1,0:T(8,128)(2,1)} %copy-done.4, bf16[16,16,384]{2,1,0:T(8,128)(2,1)} %get-tuple-element.19.refs_4_, ...), custom_call_target="tpu_custom_call" | custom-call | tf_op jit(solution)/shard_map/combine/pallas_call | solution.py:326
  114.9 15.4 %all_to_all.11.got_ref = bf16[16,48,384]{2,1,0:T(8,128)(2,1)} all-to-all(bf16[16,48,384]{2,1,0:T(8,128)(2,1)} %combine.1), channel_id=1, replica_groups=mesh['blk_0'=4,'blk_1'=2,'grp_0'=2,'grp_1'=4,'grp_2'=2] {'blk_1','grp_0'..., dimensions={0} | all-to-all | bytes 1179648 | tf_op jit(solution)/shard_map/all_to_all | solution.py:379
  130.3 2.2 %finish.1 = (bf16[64,1536]{1,0:T(8,128)(2,1)}, bf16[64,1536]{1,0:T(8,128)(2,1)}, bf16[64,1536]{1,0:T(8,128)(2,1)}) custom-call(bf16[16,48,384]{2,1,0:T(8,128)(2,1)} %all_to_all.11.got_ref), custom_call_target="tpu_custom_call" | custom-call | tf_op jit(solution)/shard_map/finish/pallas_call | solution.py:350
  (26 shorter events, 1.0 us)
Async XLA Ops:
  39.7 3.3 %copy-start = (bf16[16,160,384]{2,1,0:T(8,128)(2,1)}, bf16[16,160,384]{2,1,0:T(8,128)(2,1)S(1)}, u32[]{:S(2)}) copy-start(bf16[16,160,384]{2,1,0:T(8,128)(2,1)S(1)} %all_to_all.10.kv_ref) | copy-start | bytes 5898244
  39.8 3.2 %copy-start.1 = (bf16[16,32,384]{2,1,0:T(8,128)(2,1)}, bf16[16,32,384]{2,1,0:T(8,128)(2,1)S(1)}, u32[]{:S(2)}) copy-start(bf16[16,32,384]{2,1,0:T(8,128)(2,1)S(1)} %slice.4.qa_ref) | copy-start | bytes 1179652
  39.8 3.2 %collective-permute-start = (bf16[16,32,384]{2,1,0:T(8,128)(2,1)S(1)}, bf16[16,32,384]{2,1,0:T(8,128)(2,1)S(1)}, u32[]{:S(2)}, u32[]{:S(2)}) collective-permute-start(bf16[16,32,384]{2,1,0:T(8,128)(2,1)S(1)} %slice.4.qa_ref), channel_id=1, source_target_pairs={{0,1},{1,0},{2,3},{3,2},{4,5},{5,4},{6,7},{7,6},{8,9},{9,8},{10,11... | collective-permute-start | bytes 1179656 | tf_op jit(solution)/shard_map/ppermute | solution.py:365
  43.0 0.8 copy-start.9
  57.3 1.5 %collective-permute-start.1 = (f32[8,2048]{1,0:T(8,128)}, f32[8,2048]{1,0:T(8,128)S(1)}, u32[]{:S(2)}, u32[]{:S(2)}) collective-permute-start(f32[8,2048]{1,0:T(8,128)} %stats.1.mine_ref), channel_id=1, source_target_pairs={{0,1},{1,0},{2,3},{3,2},{4,5},{5,4},{6,7},{7,6},{8,9},{9,8},{10,11... | collective-permute-start | bytes 196616 | tf_op jit(solution)/shard_map/ppermute | solution.py:367
  58.8 0.6 copy-start.10
  76.3 24.2 %collective-permute-start.2 = (bf16[16,16,384]{2,1,0:T(8,128)(2,1)}, bf16[16,16,384]{2,1,0:T(8,128)(2,1)S(1)}, u32[]{:S(2)}, u32[]{:S(2)}) collective-permute-start(bf16[16,16,384]{2,1,0:T(8,128)(2,1)} %get-tuple-element.15), channel_id=1, source_target_pairs={{0,32},{32,64},{64,96},{96,0},{1,33},{33,65},{65,97},{97,1},{2,34}... | collective-permute-start | bytes 589832 | tf_op jit(solution)/shard_map/ppermute | solution.py:376
  78.0 24.6 %collective-permute-start.3 = (bf16[16,16,384]{2,1,0:T(8,128)(2,1)}, bf16[16,16,384]{2,1,0:T(8,128)(2,1)S(1)}, u32[]{:S(2)}, u32[]{:S(2)}) collective-permute-start(bf16[16,16,384]{2,1,0:T(8,128)(2,1)} %get-tuple-element.16), channel_id=1, source_target_pairs={{0,64},{32,96},{64,0},{96,32},{1,65},{33,97},{65,1},{97,33},{2,66}... | collective-permute-start | bytes 589832 | tf_op jit(solution)/shard_map/ppermute | solution.py:376
  81.3 23.1 %collective-permute-start.4 = (bf16[16,16,384]{2,1,0:T(8,128)(2,1)}, bf16[16,16,384]{2,1,0:T(8,128)(2,1)S(1)}, u32[]{:S(2)}, u32[]{:S(2)}) collective-permute-start(bf16[16,16,384]{2,1,0:T(8,128)(2,1)} %get-tuple-element.17), channel_id=1, source_target_pairs={{0,96},{32,0},{64,32},{96,64},{1,97},{33,1},{65,33},{97,65},{2,98}... | collective-permute-start | bytes 589832 | tf_op jit(solution)/shard_map/ppermute | solution.py:376
  99.4 8.2 %collective-permute-start.5 = (bf16[16,16,384]{2,1,0:T(8,128)(2,1)}, bf16[16,16,384]{2,1,0:T(8,128)(2,1)S(1)}, u32[]{:S(2)}, u32[]{:S(2)}) collective-permute-start(bf16[16,16,384]{2,1,0:T(8,128)(2,1)} %get-tuple-element.20), channel_id=1, source_target_pairs={{0,32},{32,64},{64,96},{96,0},{1,33},{33,65},{65,97},{97,1},{2,34}... | collective-permute-start | bytes 589832 | tf_op jit(solution)/shard_map/ppermute | solution.py:376
  100.1 9.0 %collective-permute-start.6 = (bf16[16,16,384]{2,1,0:T(8,128)(2,1)}, bf16[16,16,384]{2,1,0:T(8,128)(2,1)S(1)}, u32[]{:S(2)}, u32[]{:S(2)}) collective-permute-start(bf16[16,16,384]{2,1,0:T(8,128)(2,1)} %get-tuple-element.21), channel_id=1, source_target_pairs={{0,64},{32,96},{64,0},{96,32},{1,65},{33,97},{65,1},{97,33},{2,66}... | collective-permute-start | bytes 589832 | tf_op jit(solution)/shard_map/ppermute | solution.py:376
  100.6 10.9 %copy-start.2 = (bf16[16,16,384]{2,1,0:T(8,128)(2,1)}, bf16[16,16,384]{2,1,0:T(8,128)(2,1)S(1)}, u32[]{:S(2)}) copy-start(bf16[16,16,384]{2,1,0:T(8,128)(2,1)S(1)} %collective-permute-done.2.refs_1_) | copy-start | bytes 589828
  100.6 10.9 %collective-permute-start.7 = (bf16[16,16,384]{2,1,0:T(8,128)(2,1)}, bf16[16,16,384]{2,1,0:T(8,128)(2,1)S(1)}, u32[]{:S(2)}, u32[]{:S(2)}) collective-permute-start(bf16[16,16,384]{2,1,0:T(8,128)(2,1)} %get-tuple-element.22), channel_id=1, source_target_pairs={{0,96},{32,0},{64,32},{96,64},{1,97},{33,1},{65,33},{97,65},{2,98}... | collective-permute-start | bytes 589832 | tf_op jit(solution)/shard_map/ppermute | solution.py:376
  102.6 8.9 %copy-start.3 = (bf16[16,16,384]{2,1,0:T(8,128)(2,1)}, bf16[16,16,384]{2,1,0:T(8,128)(2,1)S(1)}, u32[]{:S(2)}) copy-start(bf16[16,16,384]{2,1,0:T(8,128)(2,1)S(1)} %collective-permute-done.3.refs_2_) | copy-start | bytes 589828
  102.6 8.9 %collective-permute-start.8 = (bf16[16,16,384]{2,1,0:T(8,128)(2,1)}, bf16[16,16,384]{2,1,0:T(8,128)(2,1)S(1)}, u32[]{:S(2)}, u32[]{:S(2)}) collective-permute-start(bf16[16,16,384]{2,1,0:T(8,128)(2,1)} %get-tuple-element.24), channel_id=1, source_target_pairs={{0,1},{1,0},{2,3},{3,2},{4,5},{5,4},{6,7},{7,6},{8,9},{9,8},{10,11... | collective-permute-start | bytes 589832 | tf_op jit(solution)/shard_map/ppermute | solution.py:377
  104.4 7.2 %copy-start.4 = (bf16[16,16,384]{2,1,0:T(8,128)(2,1)}, bf16[16,16,384]{2,1,0:T(8,128)(2,1)S(1)}, u32[]{:S(2)}) copy-start(bf16[16,16,384]{2,1,0:T(8,128)(2,1)S(1)} %collective-permute-done.4.refs_3_) | copy-start | bytes 589828
  107.6 4.0 %copy-start.5 = (bf16[16,16,384]{2,1,0:T(8,128)(2,1)}, bf16[16,16,384]{2,1,0:T(8,128)(2,1)S(1)}, u32[]{:S(2)}) copy-start(bf16[16,16,384]{2,1,0:T(8,128)(2,1)S(1)} %collective-permute-done.5.refs_5_) | copy-start | bytes 589828
  109.1 2.4 %copy-start.6 = (bf16[16,16,384]{2,1,0:T(8,128)(2,1)}, bf16[16,16,384]{2,1,0:T(8,128)(2,1)S(1)}, u32[]{:S(2)}) copy-start(bf16[16,16,384]{2,1,0:T(8,128)(2,1)S(1)} %collective-permute-done.6.refs_6_) | copy-start | bytes 589828
  111.5 0.7 copy-start.7
  111.5 0.7 copy-start.8

commit v4 on v3

v4 whole, which is shorter than its diff:
```python
import functools
import math

import jax
import jax.numpy as jnp
from jax import lax
from jax.experimental import pallas as pl
from jax.experimental.pallas import tpu as pltpu
from jax.sharding import Mesh
from jax.sharding import PartitionSpec as P


D = 1536
H = 16
HD = D // H
PENCIL = 16
PD = 64
HALF = PD // 2
WIDE = 4 * HD
N_Z = 4
N_G = 16
BLK_GRP = ("blk_0", "blk_1", "grp_0", "grp_1", "grp_2")
GRP = ("grp_0", "grp_1", "grp_2")
HEADS = ("blk_1", "grp_0", "grp_1")
Z = "blk_0"
CORE = "grp_2"
SCALE = 1.0 / math.sqrt(HD)
C2 = SCALE * math.log2(math.e)
TQ = 1024
TK = 512
GUN = 1
STQ = 1024
STK = 2048
SUB = 64
SUN = 1
NEG = -1e30
F32 = jnp.float32
BF16 = jnp.bfloat16
CONTRACT_LAST = (((1,), (1,)), ((), ()))
CONTRACT_FIRST = (((0,), (0,)), ((), ()))
ROWS = N_G * PD
NQ = N_Z * ROWS
NK = 2 * ROWS
VMEM = pl.BlockSpec(memory_space=pltpu.VMEM)

WINDOWS = ((0, 128, 0), (0, 256, HD), (128, 256, 2 * HD - 128), (256, 128, 3 * HD - 256))


def mm(a, b, dims=(((1,), (0,)), ((), ()))):
    return lax.dot_general(a, b, dims, preferred_element_type=F32)


def shift(rows, cols, src, dst):
    i = lax.broadcasted_iota(jnp.int32, (rows, cols), 0) - src
    j = lax.broadcasted_iota(jnp.int32, (rows, cols), 1) - dst
    return jnp.where((i == j) & (i >= 0) & (i < HD), 1.0, 0.0).astype(BF16)


def turned_shift(cols, src):
    i = lax.broadcasted_iota(jnp.int32, (128, cols), 0)
    j = lax.broadcasted_iota(jnp.int32, (128, cols), 1) - src
    return jnp.where((i == j) & (i < HD), 1.0, 0.0).astype(BF16)


def pack_four(parts):
    a, b, c, d = parts
    return (
        (a + b[:, :128]).astype(BF16),
        (b[:, 128:] + c[:, :128]).astype(BF16),
        (c[:, 128:] + d).astype(BF16),
    )


def pack_rows(a_ref, b_ref, out_ref):
    for turn in range(4):
        heads = range(turn, H, 4)
        offset = turn * HD % 128
        width = 128 if offset + HD <= 128 else 256
        parts = []
        for n, (_, cols, dst) in enumerate(WINDOWS):
            ref = (a_ref, b_ref)[n % 2]
            rows = slice(n // 2 * HALF, (n // 2 + 1) * HALF)
            x = jnp.concatenate([ref[rows, h * HD // 128 * 128 : h * HD // 128 * 128 + width] for h in heads], axis=0)
            parts.append(mm(x, shift(width, cols, offset, dst)))
        for n, piece in enumerate(pack_four(parts)):
            for k, h in enumerate(heads):
                out_ref[h, :, n * 128 : (n + 1) * 128] = piece[k * HALF : (k + 1) * HALF]


def pack_queries(obj_query, grad_out):
    return pl.pallas_call(
        pack_rows,
        out_shape=jax.ShapeDtypeStruct((H, HALF, WIDE), BF16),
        in_specs=[VMEM, VMEM],
        out_specs=VMEM,
        name="pack_queries",
    )(obj_query, grad_out)


def pack_keys_kernel(blocks_ref, k_ref, v_ref, out_ref, k_s, v_s):
    i = pl.program_id(0)
    at = pl.ds(pl.multiple_of(i * PENCIL, PENCIL), PENCIL)
    k_s[at, :] = k_ref[...]
    v_s[at, :] = v_ref[...]

    @pl.when(i == PD // PENCIL - 1)
    def _():
        pack_rows(k_s, v_s, out_ref)


def pack_keys(blocks, pattern_key, pattern_value):
    block = pl.BlockSpec((PENCIL, D), lambda i, blocks: (blocks[i], 0))
    return pl.pallas_call(
        pack_keys_kernel,
        out_shape=jax.ShapeDtypeStruct((H, HALF, WIDE), BF16),
        grid_spec=pltpu.PrefetchScalarGridSpec(
            num_scalar_prefetch=1,
            grid=(PD // PENCIL,),
            in_specs=[block, block],
            out_specs=pl.BlockSpec((H, HALF, WIDE), lambda i, blocks: (0, 0, 0)),
            scratch_shapes=[pltpu.VMEM((PD, D), BF16)] * 2,
        ),
        name="pack_keys",
    )(blocks, pattern_key, pattern_value)


def unpack(ref, stores, turned=False):
    half = ROWS // 2
    for n, (start, width, offset) in enumerate(WINDOWS):
        out, base = stores[n % 2]
        if out is None:
            continue
        at = slice(base + n // 2 * half, base + n // 2 * half + half)
        x = ref[:, :, start : start + width].reshape(half, width)
        if turned:
            out[:, at] = mm(turned_shift(width, offset), x, CONTRACT_LAST)[: out.shape[0]].astype(BF16)
        else:
            out[at, :] = mm(x, shift(width, 128, offset, 0)).astype(BF16)


def stats_kernel(*refs):
    q_refs, kv_refs = refs[:N_Z], refs[N_Z : N_Z + 2]
    st_ref, q_s, g_s, k_s, v_s = refs[N_Z + 2 :]
    for n, ref in enumerate(kv_refs):
        unpack(ref, ((k_s, n * ROWS), (v_s, n * ROWS)))
    for n, ref in enumerate(q_refs):
        unpack(ref, ((q_s, n * ROWS), (g_s, n * ROWS)), turned=True)
    st_ref[...] = jnp.zeros_like(st_ref)

    for n in range(NQ // STQ):
        q0 = n * STQ
        qt = q_s[:, q0 : q0 + STQ]
        gt = g_s[:, q0 : q0 + STQ]

        def one_chunk(j, carry):
            m, l, w = carry
            k0 = pl.multiple_of(j * STK, STK)
            s = mm(k_s[pl.ds(k0, STK), :], qt).reshape(STK // SUB, SUB // 8, 8, STQ)
            d = mm(v_s[pl.ds(k0, STK), :], gt).reshape(STK // SUB, SUB // 8, 8, STQ)
            for i in range(STK // SUB):
                top = jnp.maximum(m, jnp.max(s[i], axis=0))
                fade = jnp.exp2((m - top) * C2)
                e = jnp.exp2((s[i] - top[None]) * C2)
                m, l, w = top, l * fade + jnp.sum(e, axis=0), w * fade + jnp.sum(e * d[i], axis=0)
            return m, l, w

        zero = jnp.zeros((8, STQ), F32)
        start = (jnp.full((8, STQ), NEG, F32), zero, zero)
        m, l, w = lax.fori_loop(0, NK // STK, one_chunk, start, unroll=SUN)
        top = jnp.max(m, axis=0, keepdims=True)
        fade = jnp.exp2((m - top) * C2)
        row, cols = q0 // (NQ // 2) * 4, slice(q0 % (NQ // 2), q0 % (NQ // 2) + STQ)
        st_ref[row : row + 1, cols] = top
        st_ref[row + 1 : row + 2, cols] = jnp.sum(l * fade, axis=0, keepdims=True)
        st_ref[row + 2 : row + 3, cols] = jnp.sum(w * fade, axis=0, keepdims=True)


def stats(queries, keys):
    return pl.pallas_call(
        stats_kernel,
        out_shape=jax.ShapeDtypeStruct((8, NQ // 2), F32),
        in_specs=[VMEM] * (N_Z + 2),
        out_specs=VMEM,
        scratch_shapes=[pltpu.VMEM((128, NQ), BF16)] * 2 + [pltpu.VMEM((NK, 128), BF16)] * 2,
        cost_estimate=pl.CostEstimate(flops=4 * NQ * NK * 256, transcendentals=NQ * NK, bytes_accessed=4 << 20),
        name="stats",
    )(*queries, *keys)


def block_of(ref, n):
    row, col = n // 2 * 4, n % 2 * ROWS
    return [ref[row + i : row + i + 1, col : col + ROWS] for i in range(3)]


def joined(parts):
    top = functools.reduce(jnp.maximum, [part[0] for part in parts])
    fades = [jnp.exp2((part[0] - top) * C2) for part in parts]
    total = sum(part[1] * fade for part, fade in zip(parts, fades))
    weighted = sum(part[2] * fade for part, fade in zip(parts, fades))
    return top * C2 + jnp.log2(total), weighted / total


def grads_kernel(*refs):
    q_refs, kv_refs, st_refs = refs[:N_Z], refs[N_Z : N_Z + 2], refs[N_Z + 2 : 2 * N_Z + 2]
    outs, scratch = refs[2 * N_Z + 2 : 3 * N_Z + 4], refs[3 * N_Z + 4 :]
    dkv_refs, dq_refs = outs[:2], outs[2:]
    q_s, g_s, k_s, v_s, t_s, dq_s, dk_s, dv_s, log_s, mean_s = scratch
    for n, ref in enumerate(kv_refs):
        unpack(ref, ((k_s, n * ROWS), (v_s, n * ROWS)))
        unpack(ref, ((t_s, n * ROWS), (None, 0)), turned=True)
    for n, ref in enumerate(q_refs):
        unpack(ref, ((q_s, n * ROWS), (g_s, n * ROWS)))
        log_now, mean_now = joined([block_of(st, (n - t) % N_Z) for t, st in enumerate(st_refs)])
        here = slice(n * ROWS, (n + 1) * ROWS)
        log_s[:, here] = jnp.broadcast_to(log_now, (8, ROWS))
        mean_s[:, here] = jnp.broadcast_to(mean_now, (8, ROWS))
    dq_s[...] = jnp.zeros_like(dq_s)

    def one_chunk(j, _):
        k0 = pl.multiple_of(j * TK, TK)
        kc = k_s[pl.ds(k0, TK), :]
        vc = v_s[pl.ds(k0, TK), :]
        kt = t_s[:, pl.ds(k0, TK)]

        def one_tile(t, carry):
            dk, dv = carry
            q0 = pl.multiple_of(t * TQ, TQ)
            qt = q_s[pl.ds(q0, TQ), :]
            gt = g_s[pl.ds(q0, TQ), :]
            s = mm(kc, qt, CONTRACT_LAST).reshape(TK // 8, 8, TQ)
            d = mm(vc, gt, CONTRACT_LAST).reshape(TK // 8, 8, TQ)
            p = jnp.exp2(s * C2 - log_s[:, pl.ds(q0, TQ)][None])
            sg = ((d - mean_s[:, pl.ds(q0, TQ)][None]) * (p * SCALE)).astype(BF16).reshape(TK, TQ)
            p = p.astype(BF16).reshape(TK, TQ)
            dq_s[:, pl.ds(q0, TQ)] += mm(kt, sg)
            return dk + mm(sg, qt), dv + mm(p, gt)

        zero = jnp.zeros((TK, 128), F32)
        dk, dv = lax.fori_loop(0, NQ // TQ, one_tile, (zero, zero), unroll=GUN)
        dk_s[pl.ds(k0, TK), :] = dk.astype(BF16)
        dv_s[pl.ds(k0, TK), :] = dv.astype(BF16)
        return 0

    lax.fori_loop(0, NK // TK, one_chunk, 0)
    place4 = [shift(HD, cols, 0, dst) for _, cols, dst in WINDOWS]
    half = ROWS // 2
    for n, ref in enumerate(dkv_refs):
        base = n * ROWS
        parts = [
            mm((dk_s, dv_s)[i % 2][base + i // 2 * half : base + (i // 2 + 1) * half, :HD], place4[i]) for i in range(4)
        ]
        for k, piece in enumerate(pack_four(parts)):
            ref[:, :, k * 128 : (k + 1) * 128] = piece.reshape(N_G, HALF, 128)
    for n, ref in enumerate(dq_refs):
        parts = []
        for quarter in range(4):
            r0 = n * ROWS + quarter // 2 * half
            x = mm(dq_s[:, r0 : r0 + half].astype(BF16), place4[quarter], CONTRACT_FIRST)
            x = x.reshape(N_G, 2, PENCIL, x.shape[1])[:, quarter % 2]
            parts.append(x.reshape(N_G * PENCIL, x.shape[2]))
        for k, piece in enumerate(pack_four(parts)):
            ref[:, :, k * 128 : (k + 1) * 128] = piece.reshape(N_G, PENCIL, 128)


def grads(queries, keys, statistics):
    return pl.pallas_call(
        grads_kernel,
        out_shape=[jax.ShapeDtypeStruct((N_G, HALF, WIDE), BF16)] * 2
        + [jax.ShapeDtypeStruct((N_G, PENCIL, WIDE), BF16)] * N_Z,
        in_specs=[VMEM] * (2 * N_Z + 2),
        out_specs=[VMEM] * (N_Z + 2),
        scratch_shapes=[pltpu.VMEM((NQ, 128), BF16)] * 2
        + [pltpu.VMEM((NK, 128), BF16)] * 2
        + [pltpu.VMEM((HD, NK), BF16)]
        + [pltpu.VMEM((HD, NQ), F32)]
        + [pltpu.VMEM((NK, 128), BF16)] * 2
        + [pltpu.VMEM((8, NQ), F32)] * 2,
        cost_estimate=pl.CostEstimate(flops=10 * NQ * NK * 256, transcendentals=NQ * NK, bytes_accessed=8 << 20),
        name="grads",
    )(*queries, *keys, *statistics)


def combine_kernel(*refs):
    out_ref = refs[-1]
    row = 0
    for parts in (refs[:2], refs[2:-1]):
        total = parts[0][...].astype(F32)
        for part in parts[1:]:
            total = total + part[...].astype(F32)
        out_ref[:, row : row + total.shape[1], :] = total.astype(BF16)
        row += total.shape[1]


def combine(parts):
    return pl.pallas_call(
        combine_kernel,
        out_shape=jax.ShapeDtypeStruct((N_G, HALF + PENCIL, WIDE), BF16),
        in_specs=[VMEM] * len(parts),
        out_specs=VMEM,
        name="combine",
    )(*parts)


def finish_kernel(got_ref, query_ref, key_ref, value_ref):
    for h in range(H):
        here = slice(h * HD, (h + 1) * HD)
        for half in range(2):
            lane = half * 2 * HD
            rows = slice(half * HALF, (half + 1) * HALF)
            key_ref[rows, here] = got_ref[h, :HALF, lane : lane + HD]
            value_ref[rows, here] = got_ref[h, :HALF, lane + HD : lane + 2 * HD]
        for quarter in range(4):
            rows = slice(quarter * PENCIL, (quarter + 1) * PENCIL)
            query_ref[rows, here] = got_ref[h, HALF:, quarter * HD : (quarter + 1) * HD]


def finish(got):
    return pl.pallas_call(
        finish_kernel,
        out_shape=[jax.ShapeDtypeStruct((PD, D), BF16)] * 3,
        in_specs=[VMEM],
        out_specs=[VMEM] * 3,
        name="finish",
    )(got)


def along_z(x, step):
    return lax.ppermute(x, Z, tuple((k, (k + step) % N_Z) for k in range(N_Z)))


def swapped(x):
    return lax.ppermute(x, CORE, ((0, 1), (1, 0)))


def to_heads(x):
    return lax.all_to_all(x, HEADS, 0, 0, tiled=True)


def layer(obj_query, grad_out, pattern_key, pattern_value, pencil_order):
    per_device = PD // PENCIL
    first = lax.axis_index(BLK_GRP) * per_device
    blocks = lax.dynamic_slice(pencil_order, (first,), (per_device,)) - lax.axis_index(GRP) * (pattern_key.shape[0] // PENCIL)
    queries = pack_queries(obj_query, grad_out)
    queries = [to_heads(queries)]
    keys = pack_keys(blocks, pattern_key, pattern_value)
    for step in range(1, N_Z):
        queries.append(along_z(queries[0], step))
    keys = [to_heads(keys)]
    keys.append(swapped(keys[0]))
    statistics = [stats(queries, keys)]
    for step in range(1, N_Z):
        statistics.append(along_z(statistics[0], step))
    outs = grads(queries, keys, statistics)
    parts = [outs[0], None, outs[2]]
    for step in range(1, N_Z):
        parts.append(along_z(outs[2 + step], N_Z - step))
    parts[1] = swapped(outs[1])
    total = combine(parts)
    total = to_heads(total)
    return tuple(finish(total))


def solution(mesh):
    split = Mesh(mesh.devices.reshape(4, 2, 2, 4, 2), BLK_GRP)
    return jax.shard_map(
        layer,
        mesh=split,
        in_specs=(P(BLK_GRP, None), P(BLK_GRP, None), P(GRP, None), P(GRP, None), P()),
        out_specs=(P(BLK_GRP, None), P(BLK_GRP, None), P(BLK_GRP, None)),
        check_vma=False,
    )
```

time: 134 us -> 141 us (1.052)
  blocking collectives: 49.1 us -> 18 us
  waiting for transfers between devices: 9.61 us -> 36.9 us
  starting transfers between devices: 12.9 us -> 25.2 us
  Pallas kernels: 57.5 us -> 54.9 us
    all_to_all x2 -> x1, blocking collectives: 49.1 us -> 18 us  [to_heads(): return lax.all_to_all(x, HEADS, 0, 0, tiled=True)]
    ppermute x9 -> x11, waiting for transfers between devices: 9.61 us -> 28.8 us  [the longest x9 28.8 us: along_z(): lax.ppermute(x, Z, tuple(((k, (k + step) % N_Z) for k in range(N_Z))))]
    all_to_all x0 -> x2, starting transfers between devices: none -> 11.1 us  [to_heads(): return lax.all_to_all(x, HEADS, 0, 0, tiled=True)]
    all_to_all x0 -> x2, waiting for transfers between devices: none -> 8.06 us  [to_heads(): return lax.all_to_all(x, HEADS, 0, 0, tiled=True)]
    pallas_call x4, Pallas kernels: 52.6 us -> 50.3 us  [the longest x1 30.1 us: grads(): pl.pallas_call(grads_kernel, out_shape=[jax.ShapeDtypeStruct((N_G, HALF,...]
    ppermute x9 -> x11, starting transfers between devices: 12.9 us -> 14.1 us  [the longest x9 7.91 us: along_z(): lax.ppermute(x, Z, tuple(((k, (k + step) % N_Z) for k in range(N_Z))))]
    unnamed x22 -> x26, local copies, waits for them, and re-layouts: 2.09 us -> 2.93 us
  transfers between devices with their start and end apart: 9 -> 13, of which waited for: 5 -> 11; matrix products, arithmetic and copies ran while one was open for 0% -> 1% of each run, Pallas kernels for 13% -> 3%
where the time goes in v4:
time: 141 us; the launch traced here: 140 us
  Pallas kernels  54.9 us (39%)
  waiting for transfers between devices  36.9 us (26%)
  starting transfers between devices  25.2 us (18%)
  blocking collectives  18 us (13%)
  local copies, waits for them, and re-layouts  2.93 us (2%)
    pallas_call x1, Pallas kernels, grads(): pl.pallas_call(grads_kernel, out_shape=[jax.ShapeDtypeStruct((N_G, HALF,...  30.1 us
    ppermute x9, waiting for transfers between devices, along_z(): lax.ppermute(x, Z, tuple(((k, (k + step) % N_Z) for k in range(N_Z))))  28.8 us
    all_to_all x1, blocking collectives, to_heads(): return lax.all_to_all(x, HEADS, 0, 0, tiled=True)  18 us
    pallas_call x1, Pallas kernels, stats(): pl.pallas_call(stats_kernel, out_shape=jax.ShapeDtypeStruct((8, NQ // 2),...  14.4 us
    all_to_all x2, starting transfers between devices, to_heads(): return lax.all_to_all(x, HEADS, 0, 0, tiled=True)  11.1 us
    all_to_all x2, waiting for transfers between devices, to_heads(): return lax.all_to_all(x, HEADS, 0, 0, tiled=True)  8.06 us
    ppermute x9, starting transfers between devices, along_z(): lax.ppermute(x, Z, tuple(((k, (k + step) % N_Z) for k in range(N_Z))))  7.91 us
    ppermute x2, starting transfers between devices, swapped(): return lax.ppermute(x, CORE, ((0, 1), (1, 0)))  6.19 us
  transfers between devices with their start and end apart: 13, of which 11 were waited for; matrix products, arithmetic and copies ran while one was open for 1% of the time, Pallas kernels for 3%

profile of v4, /device:TPU:1, one launch (start us, length us, event | category | flops | bytes accessed | tf_op | source)
XLA Modules:
  0.0 139.9 jit_solution(16715882057043302113)
XLA Ops:
  0.6 2.2 %pack_queries.1 = bf16[16,32,384]{2,1,0:T(8,128)(2,1)} custom-call(bf16[64,1536]{1,0:T(8,128)(2,1)} %a_ref.1, bf16[64,1536]{1,0:T(8,128)(2,1)} %b_ref.1), custom_call_target="tpu_custom_call" | custom-call | tf_op jit(solution)/shard_map/pack_queries/pallas_call | solution.py:91
  2.8 7.6 %all-to-all-start = ((bf16[16,32,384]{2,1,0:T(8,128)(2,1)}), bf16[16,32,384]{2,1,0:T(8,128)(2,1)S(1)}, u32[]{:S(2)}, u32[]{:S(2)}) async-start(bf16[16,32,384]{2,1,0:T(8,128)(2,1)} %pack_queries.1), calls=%async_computation | async-start | bytes 786432 | tf_op jit(solution)/shard_map/all_to_all | solution.py:336
  10.4 1.3 dynamic-slice_subtract_fusion.blocks_ref
  11.7 3.6 %pack_keys.1 = bf16[16,32,384]{2,1,0:T(8,128)(2,1)} custom-call(s32[4]{0:T(128)} %dynamic-slice_subtract_fusion.blocks_ref, bf16[512,1536]{1,0:T(8,128)(2,1)} %k_ref.1, bf16[512,1536]{1,0:T(8,128)(2,1)} %v_ref.1), custom_call_target="tpu_custom_call" | custom-call | tf_op jit(solution)/shard_map/pack_keys/pallas_call | solution.py:113
  15.3 4.4 %all-to-all-done.refs_0_ = bf16[16,32,384]{2,1,0:T(8,128)(2,1)S(1)} async-done(((bf16[16,32,384]{2,1,0:T(8,128)(2,1)}), bf16[16,32,384]{2,1,0:T(8,128)(2,1)S(1)}, u32[]{:S(2)}, u32[]{:S(2)}) %all-to-all-start) | async-done | bytes 393248 | tf_op jit(solution)/shard_map/all_to_all | solution.py:336
  19.6 3.6 %all-to-all-start.1 = ((bf16[16,32,384]{2,1,0:T(8,128)(2,1)}), bf16[16,32,384]{2,1,0:T(8,128)(2,1)S(1)}, u32[]{:S(2)}, u32[]{:S(2)}) async-start(bf16[16,32,384]{2,1,0:T(8,128)(2,1)} %pack_keys.1), calls=%async_computation.1 | async-start | bytes 786432 | tf_op jit(solution)/shard_map/all_to_all | solution.py:336
  23.2 3.8 %collective-permute-start.2 = (bf16[16,32,384]{2,1,0:T(8,128)(2,1)S(1)}, bf16[16,32,384]{2,1,0:T(8,128)(2,1)S(1)}, u32[]{:S(2)}, u32[]{:S(2)}) collective-permute-start(bf16[16,32,384]{2,1,0:T(8,128)(2,1)S(1)} %all-to-all-done.refs_0_), channel_id=1, source_target_pairs={{0,96},{32,0},{64,32},{96,64},{1,97},{33,1},{65,33},{97,65},{2,98}... | collective-permute-start | bytes 1179656 | tf_op jit(solution)/shard_map/ppermute | solution.py:328
  27.7 3.7 %all-to-all-done.1.refs_4_ = bf16[16,32,384]{2,1,0:T(8,128)(2,1)S(1)} async-done(((bf16[16,32,384]{2,1,0:T(8,128)(2,1)}), bf16[16,32,384]{2,1,0:T(8,128)(2,1)S(1)}, u32[]{:S(2)}, u32[]{:S(2)}) %all-to-all-start.1) | async-done | bytes 393248 | tf_op jit(solution)/shard_map/all_to_all | solution.py:336
  31.4 2.9 %collective-permute-start.3 = (bf16[16,32,384]{2,1,0:T(8,128)(2,1)S(1)}, bf16[16,32,384]{2,1,0:T(8,128)(2,1)S(1)}, u32[]{:S(2)}, u32[]{:S(2)}) collective-permute-start(bf16[16,32,384]{2,1,0:T(8,128)(2,1)S(1)} %all-to-all-done.1.refs_4_), channel_id=1, source_target_pairs={{0,1},{1,0},{2,3},{3,2},{4,5},{5,4},{6,7},{7,6},{8,9},{9,8},{10,11... | collective-permute-start | bytes 1179656 | tf_op jit(solution)/shard_map/ppermute | solution.py:332
  34.4 1.0 collective-permute-done.2.refs_3_
  35.4 1.8 %collective-permute-done.1.refs_2_ = bf16[16,32,384]{2,1,0:T(8,128)(2,1)S(1)} collective-permute-done((bf16[16,32,384]{2,1,0:T(8,128)(2,1)S(1)}, bf16[16,32,384]{2,1,0:T(8,128)(2,1)S(1)}, u32[]{:S(2)}, u32[]{:S(2)}) %collective-permute-start.1) | collective-permute-done | bytes 393248 | tf_op jit(solution)/shard_map/ppermute | solution.py:328
  37.2 10.2 %collective-permute-done.refs_1_ = bf16[16,32,384]{2,1,0:T(8,128)(2,1)S(1)} collective-permute-done((bf16[16,32,384]{2,1,0:T(8,128)(2,1)S(1)}, bf16[16,32,384]{2,1,0:T(8,128)(2,1)S(1)}, u32[]{:S(2)}, u32[]{:S(2)}) %collective-permute-start) | collective-permute-done | bytes 393248 | tf_op jit(solution)/shard_map/ppermute | solution.py:328
  48.9 14.4 %stats.1.refs_6_ = f32[8,2048]{1,0:T(8,128)} custom-call(bf16[16,32,384]{2,1,0:T(8,128)(2,1)} %copy-done, bf16[16,32,384]{2,1,0:T(8,128)(2,1)} %copy-done.8, bf16[16,32,384]{2,1,0:T(8,128)(2,1)} %copy-done.7, bf16[16,32,384]{2,1,0:T(8,128)(2,1)} %copy-done.6, bf16[16,32,384]{2,1,0:T(8,128)(2,1)} %copy-done.1, bf16[16,32,384]{2,1,0:T(8,128)(2,1)} %copy-done.9), custom_call_target="tpu_custom_call" | custom-call | flops 8589934592 | bytes 4194304 | tf_op jit(solution)/shard_map/stats/pallas_call | solution.py:179
  64.8 1.9 %collective-permute-done.6.refs_9_ = f32[8,2048]{1,0:T(8,128)S(1)} collective-permute-done((f32[8,2048]{1,0:T(8,128)}, f32[8,2048]{1,0:T(8,128)S(1)}, u32[]{:S(2)}, u32[]{:S(2)}) %collective-permute-start.6) | collective-permute-done | bytes 65568 | tf_op jit(solution)/shard_map/ppermute | solution.py:328
  66.7 1.5 %collective-permute-done.5.refs_8_ = f32[8,2048]{1,0:T(8,128)S(1)} collective-permute-done((f32[8,2048]{1,0:T(8,128)}, f32[8,2048]{1,0:T(8,128)S(1)}, u32[]{:S(2)}, u32[]{:S(2)}) %collective-permute-start.5) | collective-permute-done | bytes 65568 | tf_op jit(solution)/shard_map/ppermute | solution.py:328
  69.7 30.1 %grads.1 = (bf16[16,32,384]{2,1,0:T(8,128)(2,1)}, bf16[16,32,384]{2,1,0:T(8,128)(2,1)}, bf16[16,16,384]{2,1,0:T(8,128)(2,1)}, bf16[16,16,384]{2,1,0:T(8,128)(2,1...) custom-call(bf16[16,32,384]{2,1,0:T(8,128)(2,1)} %copy-done, bf16[16,32,384]{2,1,0:T(8,128)(2,1)} %copy-done.8, ...), custom_call_target="tpu_custom_call" | custom-call | flops 21474836480 | bytes 8388608 | tf_op jit(solution)/shard_map/grads/pallas_call | solution.py:266
  99.8 3.3 %collective-permute-start.7 = (bf16[16,32,384]{2,1,0:T(8,128)(2,1)}, bf16[16,32,384]{2,1,0:T(8,128)(2,1)S(1)}, u32[]{:S(2)}, u32[]{:S(2)}) collective-permute-start(bf16[16,32,384]{2,1,0:T(8,128)(2,1)} %get-tuple-element.10), channel_id=1, source_target_pairs={{0,1},{1,0},{2,3},{3,2},{4,5},{5,4},{6,7},{7,6},{8,9},{9,8},{10,11... | collective-permute-start | bytes 1179656 | tf_op jit(solution)/shard_map/ppermute | solution.py:332
  103.7 1.2 collective-permute-start.9
  104.9 4.7 %collective-permute-done.8.refs_3_ = bf16[16,16,384]{2,1,0:T(8,128)(2,1)S(1)} collective-permute-done((bf16[16,16,384]{2,1,0:T(8,128)(2,1)}, bf16[16,16,384]{2,1,0:T(8,128)(2,1)S(1)}, u32[]{:S(2)}, u32[]{:S(2)}) %collective-permute-start.8) | collective-permute-done | bytes 196640 | tf_op jit(solution)/shard_map/ppermute | solution.py:328
  109.6 1.9 %collective-permute-done.9.refs_4_ = bf16[16,16,384]{2,1,0:T(8,128)(2,1)S(1)} collective-permute-done((bf16[16,16,384]{2,1,0:T(8,128)(2,1)}, bf16[16,16,384]{2,1,0:T(8,128)(2,1)S(1)}, u32[]{:S(2)}, u32[]{:S(2)}) %collective-permute-start.9) | collective-permute-done | bytes 196640 | tf_op jit(solution)/shard_map/ppermute | solution.py:328
  111.6 4.9 %collective-permute-done.10.refs_5_ = bf16[16,16,384]{2,1,0:T(8,128)(2,1)S(1)} collective-permute-done((bf16[16,16,384]{2,1,0:T(8,128)(2,1)}, bf16[16,16,384]{2,1,0:T(8,128)(2,1)S(1)}, u32[]{:S(2)}, u32[]{:S(2)}) %collective-permute-start.10) | collective-permute-done | bytes 196640 | tf_op jit(solution)/shard_map/ppermute | solution.py:328
  117.3 2.4 %combine.1 = bf16[16,48,384]{2,1,0:T(8,128)(2,1)} custom-call(bf16[16,32,384]{2,1,0:T(8,128)(2,1)} %get-tuple-element.9.refs_0_, bf16[16,32,384]{2,1,0:T(8,128)(2,1)} %copy-done.2, bf16[16,16,384]{2,1,0:T(8,128)(2,1)} %get-tuple-element.11.refs_2_, bf16[16,16,384]{2,1,0:T(8,128)(2,1)} %copy-done.3, bf16[16,16,384]{2,1,0:T(8,128)(2,1)} %copy-done.4, ...), custom_call_target="tpu_custom_call" | custom-call | tf_op jit(solution)/shard_map/combine/pallas_call | solution.py:295
  119.7 18.0 %all_to_all.15.got_ref = bf16[16,48,384]{2,1,0:T(8,128)(2,1)} all-to-all(bf16[16,48,384]{2,1,0:T(8,128)(2,1)} %combine.1), channel_id=1, replica_groups=mesh['blk_0'=4,'blk_1'=2,'grp_0'=2,'grp_1'=4,'grp_2'=2] {'blk_1','grp_0'..., dimensions={0} | all-to-all | bytes 1179648 | tf_op jit(solution)/shard_map/all_to_all | solution.py:336
  137.7 2.2 %finish.1 = (bf16[64,1536]{1,0:T(8,128)(2,1)}, bf16[64,1536]{1,0:T(8,128)(2,1)}, bf16[64,1536]{1,0:T(8,128)(2,1)}) custom-call(bf16[16,48,384]{2,1,0:T(8,128)(2,1)} %all_to_all.15.got_ref), custom_call_target="tpu_custom_call" | custom-call | tf_op jit(solution)/shard_map/finish/pallas_call | solution.py:318
  (36 shorter events, 6.7 us)
Async XLA Ops:
  2.8 16.8 %all-to-all-start = ((bf16[16,32,384]{2,1,0:T(8,128)(2,1)}), bf16[16,32,384]{2,1,0:T(8,128)(2,1)S(1)}, u32[]{:S(2)}, u32[]{:S(2)}) async-start(bf16[16,32,384]{2,1,0:T(8,128)(2,1)} %pack_queries.1), calls=%async_computation | async-start | bytes 786432 | tf_op jit(solution)/shard_map/all_to_all | solution.py:336
  19.6 27.8 %copy-start = (bf16[16,32,384]{2,1,0:T(8,128)(2,1)}, bf16[16,32,384]{2,1,0:T(8,128)(2,1)S(1)}, u32[]{:S(2)}) copy-start(bf16[16,32,384]{2,1,0:T(8,128)(2,1)S(1)} %all-to-all-done.refs_0_) | copy-start | bytes 1179652
  19.6 11.8 %all-to-all-start.1 = ((bf16[16,32,384]{2,1,0:T(8,128)(2,1)}), bf16[16,32,384]{2,1,0:T(8,128)(2,1)S(1)}, u32[]{:S(2)}, u32[]{:S(2)}) async-start(bf16[16,32,384]{2,1,0:T(8,128)(2,1)} %pack_keys.1), calls=%async_computation.1 | async-start | bytes 786432 | tf_op jit(solution)/shard_map/all_to_all | solution.py:336
  23.2 12.2 %collective-permute-start.2 = (bf16[16,32,384]{2,1,0:T(8,128)(2,1)S(1)}, bf16[16,32,384]{2,1,0:T(8,128)(2,1)S(1)}, u32[]{:S(2)}, u32[]{:S(2)}) collective-permute-start(bf16[16,32,384]{2,1,0:T(8,128)(2,1)S(1)} %all-to-all-done.refs_0_), channel_id=1, source_target_pairs={{0,96},{32,0},{64,32},{96,64},{1,97},{33,1},{65,33},{97,65},{2,98}... | collective-permute-start | bytes 1179656 | tf_op jit(solution)/shard_map/ppermute | solution.py:328
  27.0 10.2 %collective-permute-start.1 = (bf16[16,32,384]{2,1,0:T(8,128)(2,1)S(1)}, bf16[16,32,384]{2,1,0:T(8,128)(2,1)S(1)}, u32[]{:S(2)}, u32[]{:S(2)}) collective-permute-start(bf16[16,32,384]{2,1,0:T(8,128)(2,1)S(1)} %all-to-all-done.refs_0_), channel_id=1, source_target_pairs={{0,64},{32,96},{64,0},{96,32},{1,65},{33,97},{65,1},{97,33},{2,66}... | collective-permute-start | bytes 1179656 | tf_op jit(solution)/shard_map/ppermute | solution.py:328
  27.0 20.4 %collective-permute-start = (bf16[16,32,384]{2,1,0:T(8,128)(2,1)S(1)}, bf16[16,32,384]{2,1,0:T(8,128)(2,1)S(1)}, u32[]{:S(2)}, u32[]{:S(2)}) collective-permute-start(bf16[16,32,384]{2,1,0:T(8,128)(2,1)S(1)} %all-to-all-done.refs_0_), channel_id=1, source_target_pairs={{0,32},{32,64},{64,96},{96,0},{1,33},{33,65},{65,97},{97,1},{2,34}... | collective-permute-start | bytes 1179656 | tf_op jit(solution)/shard_map/ppermute | solution.py:328
  31.4 16.0 %copy-start.1 = (bf16[16,32,384]{2,1,0:T(8,128)(2,1)}, bf16[16,32,384]{2,1,0:T(8,128)(2,1)S(1)}, u32[]{:S(2)}) copy-start(bf16[16,32,384]{2,1,0:T(8,128)(2,1)S(1)} %all-to-all-done.1.refs_4_) | copy-start | bytes 1179652
  31.4 16.0 %collective-permute-start.3 = (bf16[16,32,384]{2,1,0:T(8,128)(2,1)S(1)}, bf16[16,32,384]{2,1,0:T(8,128)(2,1)S(1)}, u32[]{:S(2)}, u32[]{:S(2)}) collective-permute-start(bf16[16,32,384]{2,1,0:T(8,128)(2,1)S(1)} %all-to-all-done.1.refs_4_), channel_id=1, source_target_pairs={{0,1},{1,0},{2,3},{3,2},{4,5},{5,4},{6,7},{7,6},{8,9},{9,8},{10,11... | collective-permute-start | bytes 1179656 | tf_op jit(solution)/shard_map/ppermute | solution.py:332
  35.4 12.0 %copy-start.6 = (bf16[16,32,384]{2,1,0:T(8,128)(2,1)}, bf16[16,32,384]{2,1,0:T(8,128)(2,1)S(1)}, u32[]{:S(2)}) copy-start(bf16[16,32,384]{2,1,0:T(8,128)(2,1)S(1)} %collective-permute-done.2.refs_3_) | copy-start | bytes 1179652
  37.2 10.2 %copy-start.7 = (bf16[16,32,384]{2,1,0:T(8,128)(2,1)}, bf16[16,32,384]{2,1,0:T(8,128)(2,1)S(1)}, u32[]{:S(2)}) copy-start(bf16[16,32,384]{2,1,0:T(8,128)(2,1)S(1)} %collective-permute-done.1.refs_2_) | copy-start | bytes 1179652
  47.4 0.8 copy-start.8
  48.2 0.8 copy-start.9
  63.4 3.3 %collective-permute-start.6 = (f32[8,2048]{1,0:T(8,128)}, f32[8,2048]{1,0:T(8,128)S(1)}, u32[]{:S(2)}, u32[]{:S(2)}) collective-permute-start(f32[8,2048]{1,0:T(8,128)} %stats.1.refs_6_), channel_id=1, source_target_pairs={{0,96},{32,0},{64,32},{96,64},{1,97},{33,1},{65,33},{97,65},{2,98}... | collective-permute-start | bytes 196616 | tf_op jit(solution)/shard_map/ppermute | solution.py:328
  63.4 4.8 %collective-permute-start.5 = (f32[8,2048]{1,0:T(8,128)}, f32[8,2048]{1,0:T(8,128)S(1)}, u32[]{:S(2)}, u32[]{:S(2)}) collective-permute-start(f32[8,2048]{1,0:T(8,128)} %stats.1.refs_6_), channel_id=1, source_target_pairs={{0,64},{32,96},{64,0},{96,32},{1,65},{33,97},{65,1},{97,33},{2,66}... | collective-permute-start | bytes 196616 | tf_op jit(solution)/shard_map/ppermute | solution.py:328
  63.9 5.2 %collective-permute-start.4 = (f32[8,2048]{1,0:T(8,128)}, f32[8,2048]{1,0:T(8,128)S(1)}, u32[]{:S(2)}, u32[]{:S(2)}) collective-permute-start(f32[8,2048]{1,0:T(8,128)} %stats.1.refs_6_), channel_id=1, source_target_pairs={{0,32},{32,64},{64,96},{96,0},{1,33},{33,65},{65,97},{97,1},{2,34}... | collective-permute-start | bytes 196616 | tf_op jit(solution)/shard_map/ppermute | solution.py:328
  66.7 2.4 %copy-start.10 = (f32[8,2048]{1,0:T(8,128)}, f32[8,2048]{1,0:T(8,128)S(1)}, u32[]{:S(2)}) copy-start(f32[8,2048]{1,0:T(8,128)S(1)} %collective-permute-done.6.refs_9_) | copy-start | bytes 196612
  68.2 0.9 copy-start.11
  99.8 16.7 %collective-permute-start.7 = (bf16[16,32,384]{2,1,0:T(8,128)(2,1)}, bf16[16,32,384]{2,1,0:T(8,128)(2,1)S(1)}, u32[]{:S(2)}, u32[]{:S(2)}) collective-permute-start(bf16[16,32,384]{2,1,0:T(8,128)(2,1)} %get-tuple-element.10), channel_id=1, source_target_pairs={{0,1},{1,0},{2,3},{3,2},{4,5},{5,4},{6,7},{7,6},{8,9},{9,8},{10,11... | collective-permute-start | bytes 1179656 | tf_op jit(solution)/shard_map/ppermute | solution.py:332
  103.0 6.6 %collective-permute-start.8 = (bf16[16,16,384]{2,1,0:T(8,128)(2,1)}, bf16[16,16,384]{2,1,0:T(8,128)(2,1)S(1)}, u32[]{:S(2)}, u32[]{:S(2)}) collective-permute-start(bf16[16,16,384]{2,1,0:T(8,128)(2,1)} %get-tuple-element.12), channel_id=1, source_target_pairs={{0,96},{32,0},{64,32},{96,64},{1,97},{33,1},{65,33},{97,65},{2,98}... | collective-permute-start | bytes 589832 | tf_op jit(solution)/shard_map/ppermute | solution.py:328
  103.7 7.9 %collective-permute-start.9 = (bf16[16,16,384]{2,1,0:T(8,128)(2,1)}, bf16[16,16,384]{2,1,0:T(8,128)(2,1)S(1)}, u32[]{:S(2)}, u32[]{:S(2)}) collective-permute-start(bf16[16,16,384]{2,1,0:T(8,128)(2,1)} %get-tuple-element.13), channel_id=1, source_target_pairs={{0,64},{32,96},{64,0},{96,32},{1,65},{33,97},{65,1},{97,33},{2,66}... | collective-permute-start | bytes 589832 | tf_op jit(solution)/shard_map/ppermute | solution.py:328
  104.9 11.5 %collective-permute-start.10 = (bf16[16,16,384]{2,1,0:T(8,128)(2,1)}, bf16[16,16,384]{2,1,0:T(8,128)(2,1)S(1)}, u32[]{:S(2)}, u32[]{:S(2)}) collective-permute-start(bf16[16,16,384]{2,1,0:T(8,128)(2,1)} %get-tuple-element.14), channel_id=1, source_target_pairs={{0,32},{32,64},{64,96},{96,0},{1,33},{33,65},{65,97},{97,1},{2,34}... | collective-permute-start | bytes 589832 | tf_op jit(solution)/shard_map/ppermute | solution.py:328
  109.6 6.8 %copy-start.3 = (bf16[16,16,384]{2,1,0:T(8,128)(2,1)}, bf16[16,16,384]{2,1,0:T(8,128)(2,1)S(1)}, u32[]{:S(2)}) copy-start(bf16[16,16,384]{2,1,0:T(8,128)(2,1)S(1)} %collective-permute-done.8.refs_3_) | copy-start | bytes 589828
  111.6 4.9 %copy-start.4 = (bf16[16,16,384]{2,1,0:T(8,128)(2,1)}, bf16[16,16,384]{2,1,0:T(8,128)(2,1)S(1)}, u32[]{:S(2)}) copy-start(bf16[16,16,384]{2,1,0:T(8,128)(2,1)S(1)} %collective-permute-done.9.refs_4_) | copy-start | bytes 589828
  116.5 0.8 copy-start.2
  (2 other events, 1.3 us)

commit v5 on v4

--- a/solution.py
+++ b/solution.py
@@ -71,7 +71,7 @@
     )
 
 
-def pack_rows(a_ref, b_ref, out_ref):
+def pack_rows(a_ref, b_ref, out_ref, base):
     for turn in range(4):
         heads = range(turn, H, 4)
         offset = turn * HD % 128
@@ -84,44 +84,39 @@
             parts.append(mm(x, shift(width, cols, offset, dst)))
         for n, piece in enumerate(pack_four(parts)):
             for k, h in enumerate(heads):
-                out_ref[h, :, n * 128 : (n + 1) * 128] = piece[k * HALF : (k + 1) * HALF]
-
-
-def pack_queries(obj_query, grad_out):
-    return pl.pallas_call(
-        pack_rows,
-        out_shape=jax.ShapeDtypeStruct((H, HALF, WIDE), BF16),
-        in_specs=[VMEM, VMEM],
-        out_specs=VMEM,
-        name="pack_queries",
-    )(obj_query, grad_out)
-
-
-def pack_keys_kernel(blocks_ref, k_ref, v_ref, out_ref, k_s, v_s):
+                out_ref[h, base : base + HALF, n * 128 : (n + 1) * 128] = piece[k * HALF : (k + 1) * HALF]
+
+
+def pack_kernel(order_ref, place_ref, q_ref, g_ref, k_ref, v_ref, out_ref, k_s, v_s):
     i = pl.program_id(0)
     at = pl.ds(pl.multiple_of(i * PENCIL, PENCIL), PENCIL)
     k_s[at, :] = k_ref[...]
     v_s[at, :] = v_ref[...]
 
+    @pl.when(i == 0)
+    def _():
+        pack_rows(q_ref, g_ref, out_ref, 0)
+
     @pl.when(i == PD // PENCIL - 1)
     def _():
-        pack_rows(k_s, v_s, out_ref)
-
-
-def pack_keys(blocks, pattern_key, pattern_value):
-    block = pl.BlockSpec((PENCIL, D), lambda i, blocks: (blocks[i], 0))
-    return pl.pallas_call(
-        pack_keys_kernel,
-        out_shape=jax.ShapeDtypeStruct((H, HALF, WIDE), BF16),
+        pack_rows(k_s, v_s, out_ref, HALF)
+
+
+def pack(order, place, obj_query, grad_out, pattern_key, pattern_value):
+    rows = pl.BlockSpec((PD, D), lambda i, order, place: (0, 0))
+    block = pl.BlockSpec((PENCIL, D), lambda i, order, place: (order[place[0] + i] - place[1], 0))
+    return pl.pallas_call(
+        pack_kernel,
+        out_shape=jax.ShapeDtypeStruct((H, PD, WIDE), BF16),
         grid_spec=pltpu.PrefetchScalarGridSpec(
-            num_scalar_prefetch=1,
+            num_scalar_prefetch=2,
             grid=(PD // PENCIL,),
-            in_specs=[block, block],
-            out_specs=pl.BlockSpec((H, HALF, WIDE), lambda i, blocks: (0, 0, 0)),
+            in_specs=[rows, rows, block, block],
+            out_specs=pl.BlockSpec((H, PD, WIDE), lambda i, order, place: (0, 0, 0)),
             scratch_shapes=[pltpu.VMEM((PD, D), BF16)] * 2,
         ),
-        name="pack_keys",
-    )(blocks, pattern_key, pattern_value)
+        name="pack",
+    )(order, place, obj_query, grad_out, pattern_key, pattern_value)
 
 
 def unpack(ref, stores, turned=False):
@@ -202,15 +197,15 @@
 
 def grads_kernel(*refs):
     q_refs, kv_refs, st_refs = refs[:N_Z], refs[N_Z : N_Z + 2], refs[N_Z + 2 : 2 * N_Z + 2]
-    outs, scratch = refs[2 * N_Z + 2 : 3 * N_Z + 4], refs[3 * N_Z + 4 :]
-    dkv_refs, dq_refs = outs[:2], outs[2:]
+    dkv_refs, dq_refs = refs[2 * N_Z + 2 : 2 * N_Z + 4], refs[2 * N_Z + 4 : 2 * N_Z + 6]
+    scratch = refs[2 * N_Z + 6 :]
     q_s, g_s, k_s, v_s, t_s, dq_s, dk_s, dv_s, log_s, mean_s = scratch
     for n, ref in enumerate(kv_refs):
         unpack(ref, ((k_s, n * ROWS), (v_s, n * ROWS)))
         unpack(ref, ((t_s, n * ROWS), (None, 0)), turned=True)
     for n, ref in enumerate(q_refs):
         unpack(ref, ((q_s, n * ROWS), (g_s, n * ROWS)))
-        log_now, mean_now = joined([block_of(st, (n - t) % N_Z) for t, st in enumerate(st_refs)])
+        log_now, mean_now = joined([block_of(st, n ^ t) for t, st in enumerate(st_refs)])
         here = slice(n * ROWS, (n + 1) * ROWS)
         log_s[:, here] = jnp.broadcast_to(log_now, (8, ROWS))
         mean_s[:, here] = jnp.broadcast_to(mean_now, (8, ROWS))
@@ -251,7 +246,8 @@
         ]
         for k, piece in enumerate(pack_four(parts)):
             ref[:, :, k * 128 : (k + 1) * 128] = piece.reshape(N_G, HALF, 128)
-    for n, ref in enumerate(dq_refs):
+    for n in range(N_Z):
+        ref, row = dq_refs[n % 2], n // 2 * PENCIL
         parts = []
         for quarter in range(4):
             r0 = n * ROWS + quarter // 2 * half
@@ -259,16 +255,15 @@
             x = x.reshape(N_G, 2, PENCIL, x.shape[1])[:, quarter % 2]
             parts.append(x.reshape(N_G * PENCIL, x.shape[2]))
         for k, piece in enumerate(pack_four(parts)):
-            ref[:, :, k * 128 : (k + 1) * 128] = piece.reshape(N_G, PENCIL, 128)
+            ref[:, row : row + PENCIL, k * 128 : (k + 1) * 128] = piece.reshape(N_G, PENCIL, 128)
 
 
 def grads(queries, keys, statistics):
     return pl.pallas_call(
         grads_kernel,
-        out_shape=[jax.ShapeDtypeStruct((N_G, HALF, WIDE), BF16)] * 2
-        + [jax.ShapeDtypeStruct((N_G, PENCIL, WIDE), BF16)] * N_Z,
+        out_shape=[jax.ShapeDtypeStruct((N_G, HALF, WIDE), BF16)] * 4,
         in_specs=[VMEM] * (2 * N_Z + 2),
-        out_specs=[VMEM] * (N_Z + 2),
+        out_specs=[VMEM] * 4,
         scratch_shapes=[pltpu.VMEM((NQ, 128), BF16)] * 2
         + [pltpu.VMEM((NK, 128), BF16)] * 2
         + [pltpu.VMEM((HD, NK), BF16)]
@@ -280,14 +275,31 @@
     )(*queries, *keys, *statistics)
 
 
+def meet_kernel(mine_ref, theirs_ref, keep_ref, send_ref):
+    total = mine_ref[...].astype(F32) + theirs_ref[...].astype(F32)
+    keep_ref[...] = total[:, :PENCIL]
+    send_ref[...] = total[:, PENCIL:].astype(BF16)
+
+
+def meet(mine, theirs):
+    return pl.pallas_call(
+        meet_kernel,
+        out_shape=(
+            jax.ShapeDtypeStruct((N_G, PENCIL, WIDE), F32),
+            jax.ShapeDtypeStruct((N_G, PENCIL, WIDE), BF16),
+        ),
+        in_specs=[VMEM, VMEM],
+        out_specs=(VMEM, VMEM),
+        name="meet",
+    )(mine, theirs)
+
+
 def combine_kernel(*refs):
     out_ref = refs[-1]
     row = 0
     for parts in (refs[:2], refs[2:-1]):
-        total = parts[0][...].astype(F32)
-        for part in parts[1:]:
-            total = total + part[...].astype(F32)
-        out_ref[:, row : row + total.shape[1], :] = total.astype(BF16)
+        total = (parts[0][...].astype(F32) + parts[1][...].astype(F32)).astype(BF16)
+        out_ref[:, row : row + total.shape[1], :] = total
         row += total.shape[1]
 
 
@@ -324,11 +336,15 @@
     )(got)
 
 
-def along_z(x, step):
-    return lax.ppermute(x, Z, tuple((k, (k + step) % N_Z) for k in range(N_Z)))
-
-
-def swapped(x):
+def over_a(x):
+    return lax.ppermute(x, Z, ((0, 3), (3, 0), (1, 2), (2, 1)))
+
+
+def over_b(x):
+    return lax.ppermute(x, Z, ((0, 1), (1, 0), (2, 3), (3, 2)))
+
+
+def over_core(x):
     return lax.ppermute(x, CORE, ((0, 1), (1, 0)))
 
 
@@ -337,25 +353,24 @@
 
 
 def layer(obj_query, grad_out, pattern_key, pattern_value, pencil_order):
-    per_device = PD // PENCIL
-    first = lax.axis_index(BLK_GRP) * per_device
-    blocks = lax.dynamic_slice(pencil_order, (first,), (per_device,)) - lax.axis_index(GRP) * (pattern_key.shape[0] // PENCIL)
-    queries = pack_queries(obj_query, grad_out)
-    queries = [to_heads(queries)]
-    keys = pack_keys(blocks, pattern_key, pattern_value)
-    for step in range(1, N_Z):
-        queries.append(along_z(queries[0], step))
-    keys = [to_heads(keys)]
-    keys.append(swapped(keys[0]))
+    place = jnp.stack(
+        [lax.axis_index(BLK_GRP) * (PD // PENCIL), lax.axis_index(GRP) * (pattern_key.shape[0] // PENCIL)]
+    ).astype(jnp.int32)
+    sent = pack(pencil_order, place, obj_query, grad_out, pattern_key, pattern_value)
+    got = to_heads(sent)
+    queries, keys = [got[:, :HALF]], [got[:, HALF:]]
+    third = over_b(queries[0])
+    keys.append(over_a(keys[0]))
+    queries += [over_core(queries[0]), third, over_core(third)]
     statistics = [stats(queries, keys)]
-    for step in range(1, N_Z):
-        statistics.append(along_z(statistics[0], step))
-    outs = grads(queries, keys, statistics)
-    parts = [outs[0], None, outs[2]]
-    for step in range(1, N_Z):
-        parts.append(along_z(outs[2 + step], N_Z - step))
-    parts[1] = swapped(outs[1])
-    total = combine(parts)
+    third = over_b(statistics[0])
+    statistics += [over_core(statistics[0]), third, over_core(third)]
+    keys_here, keys_there, queries_here, queries_there = grads(queries, keys, statistics)
+    keys_got = over_a(keys_there)
+    queries_got = over_core(queries_there)
+    keep, send = meet(queries_here, queries_got)
+    queries_got = over_b(send)
+    total = combine([keys_here, keys_got, keep, queries_got])
     total = to_heads(total)
     return tuple(finish(total))
 

time: 141 us -> 130 us (0.922)
  waiting for transfers between devices: 36.9 us -> 16.9 us
  blocking collectives: 18 us -> 36.6 us
  starting transfers between devices: 25.2 us -> 14.5 us
    all_to_all x1 -> x2, blocking collectives: 18 us -> 36.6 us  [to_heads(): return lax.all_to_all(x, HEADS, 0, 0, tiled=True)]
    ppermute x11 -> x10, waiting for transfers between devices: 28.8 us -> 16.9 us  [the longest x2 10.8 us: over_a(): return lax.ppermute(x, Z, ((0, 3), (3, 0), (1, 2), (2, 1)))]
    all_to_all x2 -> x0, starting transfers between devices: 11.1 us -> none  [to_heads(): return lax.all_to_all(x, HEADS, 0, 0, tiled=True)]
    all_to_all x2 -> x0, waiting for transfers between devices: 8.06 us -> none  [to_heads(): return lax.all_to_all(x, HEADS, 0, 0, tiled=True)]
    unnamed x26 -> x24, local copies, waits for them, and re-layouts: 2.93 us -> 3.85 us
    ppermute x11 -> x10, starting transfers between devices: 14.1 us -> 14.5 us  [the longest x5 7.74 us: over_core(): return lax.ppermute(x, CORE, ((0, 1), (1, 0)))]
  transfers between devices with their start and end apart: 13 -> 10, of which waited for: 11 -> 5; matrix products, arithmetic and copies ran while one was open for 1% -> 0% of each run, Pallas kernels for 3% -> 2%
where the time goes in v5:
time: 130 us; the launch traced here: 129 us
  Pallas kernels  55.4 us (43%)
  blocking collectives  36.6 us (28%)
  waiting for transfers between devices  16.9 us (13%)
  starting transfers between devices  14.5 us (11%)
  local copies, waits for them, and re-layouts  3.94 us (3%)
    all_to_all x2, blocking collectives, to_heads(): return lax.all_to_all(x, HEADS, 0, 0, tiled=True)  36.6 us
    pallas_call x1, Pallas kernels, grads(): pl.pallas_call(grads_kernel, out_shape=[jax.ShapeDtypeStruct((N_G, HALF,...  30.1 us
    pallas_call x1, Pallas kernels, stats(): pl.pallas_call(stats_kernel, out_shape=jax.ShapeDtypeStruct((8, NQ // 2),...  14.4 us
    ppermute x2, waiting for transfers between devices, over_a(): return lax.ppermute(x, Z, ((0, 3), (3, 0), (1, 2), (2, 1)))  10.8 us
    ppermute x5, starting transfers between devices, over_core(): return lax.ppermute(x, CORE, ((0, 1), (1, 0)))  7.74 us
    ppermute x3, waiting for transfers between devices, over_b(): return lax.ppermute(x, Z, ((0, 1), (1, 0), (2, 3), (3, 2)))  5.2 us
    ppermute x2, starting transfers between devices, over_a(): return lax.ppermute(x, Z, ((0, 3), (3, 0), (1, 2), (2, 1)))  4.47 us
    pallas_call x1, Pallas kernels, pack(): pl.pallas_call(pack_kernel, out_shape=jax.ShapeDtypeStruct((H, PD, WIDE),...  4.43 us
  transfers between devices with their start and end apart: 10, of which 5 were waited for; matrix products, arithmetic and copies ran while one was open for 0% of the time, Pallas kernels for 2%

profile of v5, /device:TPU:1, one launch (start us, length us, event | category | flops | bytes accessed | tf_op | source)
XLA Modules:
  0.0 128.7 jit_solution(16605323592169718739)
XLA Ops:
  1.2 4.4 %pack.1 = bf16[16,64,384]{2,1,0:T(8,128)(2,1)} custom-call(s32[512]{0:T(512)} %order_ref.1, s32[2]{0:T(128)} %pad_add_fusion.place_ref, bf16[64,1536]{1,0:T(8,128)(2,1)} %q_ref.1, bf16[64,1536]{1,0:T(8,128)(2,1)} %g_ref.1, bf16[512,1536]{1,0:T(8,128)(2,1)} %k_ref.1, bf16[512,1536]{1,0:T(8,128)(2,1)} %v_ref.1), custom_call_target="tpu_custom_call" | custom-call | tf_op jit(solution)/shard_map/pack/pallas_call | solution.py:108
  5.7 21.1 %all_to_all.10 = bf16[16,64,384]{2,1,0:T(8,128)(2,1)S(1)} all-to-all(bf16[16,64,384]{2,1,0:T(8,128)(2,1)} %pack.1), channel_id=1, replica_groups=mesh['blk_0'=4,'blk_1'=2,'grp_0'=2,'grp_1'=4,'grp_2'=2] {'blk_1','grp_0'..., dimensions={0} | all-to-all | bytes 1572864 | tf_op jit(solution)/shard_map/all_to_all | solution.py:352
  26.9 1.7 %collective-permute-start.1 = (bf16[16,32,384]{2,1,0:T(8,128)(2,1)S(1)}, bf16[16,32,384]{2,1,0:T(8,128)(2,1)S(1)}, u32[]{:S(2)}, u32[]{:S(2)}) collective-permute-start(bf16[16,32,384]{2,1,0:T(8,128)(2,1)S(1)} %get-tuple-element.16.refs_0_), channel_id=1, source_target_pairs={{0,32},{32,0},{64,96},{96,64},{1,33},{33,1},{65,97},{97,65},{2,34}... | collective-permute-start | bytes 1179656 | tf_op jit(solution)/shard_map/ppermute | solution.py:344
  28.6 2.1 %collective-permute-start = (bf16[16,32,384]{2,1,0:T(8,128)(2,1)S(1)}, bf16[16,32,384]{2,1,0:T(8,128)(2,1)S(1)}, u32[]{:S(2)}, u32[]{:S(2)}) collective-permute-start(bf16[16,32,384]{2,1,0:T(8,128)(2,1)S(1)} %get-tuple-element.16.refs_0_), channel_id=1, source_target_pairs={{0,1},{1,0},{2,3},{3,2},{4,5},{5,4},{6,7},{7,6},{8,9},{9,8},{10,11... | collective-permute-start | bytes 1179656 | tf_op jit(solution)/shard_map/ppermute | solution.py:348
  30.6 2.2 %collective-permute-start.3 = (bf16[16,32,384]{2,1,0:T(8,128)(2,1)S(1)}, bf16[16,32,384]{2,1,0:T(8,128)(2,1)S(1)}, u32[]{:S(2)}, u32[]{:S(2)}) collective-permute-start(bf16[16,32,384]{2,1,0:T(8,128)(2,1)S(1)} %get-tuple-element.15.refs_4_), channel_id=1, source_target_pairs={{0,96},{96,0},{32,64},{64,32},{1,97},{97,1},{33,65},{65,33},{2,98}... | collective-permute-start | bytes 1179656 | tf_op jit(solution)/shard_map/ppermute | solution.py:340
  32.9 3.3 %collective-permute-done.1.refs_2_ = bf16[16,32,384]{2,1,0:T(8,128)(2,1)S(1)} collective-permute-done((bf16[16,32,384]{2,1,0:T(8,128)(2,1)S(1)}, bf16[16,32,384]{2,1,0:T(8,128)(2,1)S(1)}, u32[]{:S(2)}, u32[]{:S(2)}) %collective-permute-start.1) | collective-permute-done | bytes 393248 | tf_op jit(solution)/shard_map/ppermute | solution.py:344
  36.2 2.4 %collective-permute-start.2 = (bf16[16,32,384]{2,1,0:T(8,128)(2,1)S(1)}, bf16[16,32,384]{2,1,0:T(8,128)(2,1)S(1)}, u32[]{:S(2)}, u32[]{:S(2)}) collective-permute-start(bf16[16,32,384]{2,1,0:T(8,128)(2,1)S(1)} %collective-permute-done.1.refs_2_), channel_id=1, source_target_pairs={{0,1},{1,0},{2,3},{3,2},{4,5},{5,4},{6,7},{7,6},{8,9},{9,8},{10,11... | collective-permute-start | bytes 1179656 | tf_op jit(solution)/shard_map/ppermute | solution.py:348
  38.7 3.9 %collective-permute-done.3.refs_5_ = bf16[16,32,384]{2,1,0:T(8,128)(2,1)S(1)} collective-permute-done((bf16[16,32,384]{2,1,0:T(8,128)(2,1)S(1)}, bf16[16,32,384]{2,1,0:T(8,128)(2,1)S(1)}, u32[]{:S(2)}, u32[]{:S(2)}) %collective-permute-start.3) | collective-permute-done | bytes 393248 | tf_op jit(solution)/shard_map/ppermute | solution.py:340
  42.6 0.7 copy-done.7
  43.4 0.8 copy-done.8
  44.2 14.4 %stats.1.refs_6_ = f32[8,2048]{1,0:T(8,128)} custom-call(bf16[16,32,384]{2,1,0:T(8,128)(2,1)} %copy-done.2, bf16[16,32,384]{2,1,0:T(8,128)(2,1)} %copy-done.6, bf16[16,32,384]{2,1,0:T(8,128)(2,1)} %copy-done.5, bf16[16,32,384]{2,1,0:T(8,128)(2,1)} %copy-done.8, bf16[16,32,384]{2,1,0:T(8,128)(2,1)} %copy-done.1, bf16[16,32,384]{2,1,0:T(8,128)(2,1)} %copy-done.7), custom_call_target="tpu_custom_call" | custom-call | flops 8589934592 | bytes 4194304 | tf_op jit(solution)/shard_map/stats/pallas_call | solution.py:174
  59.2 0.9 collective-permute-start.4
  60.1 1.9 %collective-permute-done.5.refs_8_ = f32[8,2048]{1,0:T(8,128)S(1)} collective-permute-done((f32[8,2048]{1,0:T(8,128)}, f32[8,2048]{1,0:T(8,128)S(1)}, u32[]{:S(2)}, u32[]{:S(2)}) %collective-permute-start.5) | collective-permute-done | bytes 65568 | tf_op jit(solution)/shard_map/ppermute | solution.py:344
  61.9 2.0 %collective-permute-start.6 = (f32[8,2048]{1,0:T(8,128)S(1)}, f32[8,2048]{1,0:T(8,128)S(1)}, u32[]{:S(2)}, u32[]{:S(2)}) collective-permute-start(f32[8,2048]{1,0:T(8,128)S(1)} %collective-permute-done.5.refs_8_), channel_id=1, source_target_pairs={{0,1},{1,0},{2,3},{3,2},{4,5},{5,4},{6,7},{7,6},{8,9},{9,8},{10,11... | collective-permute-start | bytes 196616 | tf_op jit(solution)/shard_map/ppermute | solution.py:348
  64.0 0.9 collective-permute-done.6.refs_9_
  65.5 30.1 %grads.1 = (bf16[16,32,384]{2,1,0:T(8,128)(2,1)}, bf16[16,32,384]{2,1,0:T(8,128)(2,1)}, bf16[16,32,384]{2,1,0:T(8,128)(2,1)}, bf16[16,32,384]{2,1,0:T(8,128)(2,1)}) custom-call(bf16[16,32,384]{2,1,0:T(8,128)(2,1)} %copy-done.2, bf16[16,32,384]{2,1,0:T(8,128)(2,1)} %copy-done.6, bf16[16,32,384]{2,1,0:T(8,128)(2,1)} %copy-done.5, ...), custom_call_target="tpu_custom_call" | custom-call | flops 21474836480 | bytes 8388608 | tf_op jit(solution)/shard_map/grads/pallas_call | solution.py:262
  95.9 2.2 %collective-permute-start.7 = (bf16[16,32,384]{2,1,0:T(8,128)(2,1)}, bf16[16,32,384]{2,1,0:T(8,128)(2,1)S(1)}, u32[]{:S(2)}, u32[]{:S(2)}) collective-permute-start(bf16[16,32,384]{2,1,0:T(8,128)(2,1)} %get-tuple-element.10), channel_id=1, source_target_pairs={{0,96},{96,0},{32,64},{64,32},{1,97},{97,1},{33,65},{65,33},{2,98}... | collective-permute-start | bytes 1179656 | tf_op jit(solution)/shard_map/ppermute | solution.py:340
  98.2 0.8 copy-done
  99.0 2.0 %meet.1 = (f32[16,16,384]{2,1,0:T(8,128)}, bf16[16,16,384]{2,1,0:T(8,128)(2,1)}) custom-call(bf16[16,32,384]{2,1,0:T(8,128)(2,1)} %get-tuple-element.11.mine_ref, bf16[16,32,384]{2,1,0:T(8,128)(2,1)} %copy-done), custom_call_target="tpu_custom_call" | custom-call | tf_op jit(solution)/shard_map/meet/pallas_call | solution.py:285
  100.9 7.0 %collective-permute-done.7.refs_1_ = bf16[16,32,384]{2,1,0:T(8,128)(2,1)S(1)} collective-permute-done((bf16[16,32,384]{2,1,0:T(8,128)(2,1)}, bf16[16,32,384]{2,1,0:T(8,128)(2,1)S(1)}, u32[]{:S(2)}, u32[]{:S(2)}) %collective-permute-start.7) | collective-permute-done | bytes 393248 | tf_op jit(solution)/shard_map/ppermute | solution.py:340
  107.9 0.8 copy-done.3
  108.7 2.2 %combine.1 = bf16[16,48,384]{2,1,0:T(8,128)(2,1)} custom-call(bf16[16,32,384]{2,1,0:T(8,128)(2,1)} %get-tuple-element.9.refs_0_, bf16[16,32,384]{2,1,0:T(8,128)(2,1)} %copy-done.3, f32[16,16,384]{2,1,0:T(8,128)} %get-tuple-element.13.refs_2_, bf16[16,16,384]{2,1,0:T(8,128)(2,1)} %copy-done.4), custom_call_target="tpu_custom_call" | custom-call | tf_op jit(solution)/shard_map/combine/pallas_call | solution.py:307
  110.9 15.6 %all_to_all.11.got_ref = bf16[16,48,384]{2,1,0:T(8,128)(2,1)} all-to-all(bf16[16,48,384]{2,1,0:T(8,128)(2,1)} %combine.1), channel_id=1, replica_groups=mesh['blk_0'=4,'blk_1'=2,'grp_0'=2,'grp_1'=4,'grp_2'=2] {'blk_1','grp_0'..., dimensions={0} | all-to-all | bytes 1179648 | tf_op jit(solution)/shard_map/all_to_all | solution.py:352
  126.5 2.2 %finish.1 = (bf16[64,1536]{1,0:T(8,128)(2,1)}, bf16[64,1536]{1,0:T(8,128)(2,1)}, bf16[64,1536]{1,0:T(8,128)(2,1)}) custom-call(bf16[16,48,384]{2,1,0:T(8,128)(2,1)} %all_to_all.11.got_ref), custom_call_target="tpu_custom_call" | custom-call | tf_op jit(solution)/shard_map/finish/pallas_call | solution.py:330
  (30 shorter events, 2.5 us)
Async XLA Ops:
  26.8 15.7 %copy-start.1 = (bf16[16,32,384]{2,1,0:T(8,128)(2,1)}, bf16[16,32,384]{2,1,0:T(8,128)(2,1)S(1)}, u32[]{:S(2)}) copy-start(bf16[16,32,384]{2,1,0:T(8,128)(2,1)S(1)} %get-tuple-element.15.refs_4_) | copy-start | bytes 1179652
  26.9 15.7 %copy-start.2 = (bf16[16,32,384]{2,1,0:T(8,128)(2,1)}, bf16[16,32,384]{2,1,0:T(8,128)(2,1)S(1)}, u32[]{:S(2)}) copy-start(bf16[16,32,384]{2,1,0:T(8,128)(2,1)S(1)} %get-tuple-element.16.refs_0_) | copy-start | bytes 1179652
  26.9 9.3 %collective-permute-start.1 = (bf16[16,32,384]{2,1,0:T(8,128)(2,1)S(1)}, bf16[16,32,384]{2,1,0:T(8,128)(2,1)S(1)}, u32[]{:S(2)}, u32[]{:S(2)}) collective-permute-start(bf16[16,32,384]{2,1,0:T(8,128)(2,1)S(1)} %get-tuple-element.16.refs_0_), channel_id=1, source_target_pairs={{0,32},{32,0},{64,96},{96,64},{1,33},{33,1},{65,97},{97,65},{2,34}... | collective-permute-start | bytes 1179656 | tf_op jit(solution)/shard_map/ppermute | solution.py:344
  28.6 13.9 %collective-permute-start = (bf16[16,32,384]{2,1,0:T(8,128)(2,1)S(1)}, bf16[16,32,384]{2,1,0:T(8,128)(2,1)S(1)}, u32[]{:S(2)}, u32[]{:S(2)}) collective-permute-start(bf16[16,32,384]{2,1,0:T(8,128)(2,1)S(1)} %get-tuple-element.16.refs_0_), channel_id=1, source_target_pairs={{0,1},{1,0},{2,3},{3,2},{4,5},{5,4},{6,7},{7,6},{8,9},{9,8},{10,11... | collective-permute-start | bytes 1179656 | tf_op jit(solution)/shard_map/ppermute | solution.py:348
  30.6 11.9 %collective-permute-start.3 = (bf16[16,32,384]{2,1,0:T(8,128)(2,1)S(1)}, bf16[16,32,384]{2,1,0:T(8,128)(2,1)S(1)}, u32[]{:S(2)}, u32[]{:S(2)}) collective-permute-start(bf16[16,32,384]{2,1,0:T(8,128)(2,1)S(1)} %get-tuple-element.15.refs_4_), channel_id=1, source_target_pairs={{0,96},{96,0},{32,64},{64,32},{1,97},{97,1},{33,65},{65,33},{2,98}... | collective-permute-start | bytes 1179656 | tf_op jit(solution)/shard_map/ppermute | solution.py:340
  36.2 6.3 %copy-start.5 = (bf16[16,32,384]{2,1,0:T(8,128)(2,1)}, bf16[16,32,384]{2,1,0:T(8,128)(2,1)S(1)}, u32[]{:S(2)}) copy-start(bf16[16,32,384]{2,1,0:T(8,128)(2,1)S(1)} %collective-permute-done.1.refs_2_) | copy-start | bytes 1179652
  36.2 6.3 %collective-permute-start.2 = (bf16[16,32,384]{2,1,0:T(8,128)(2,1)S(1)}, bf16[16,32,384]{2,1,0:T(8,128)(2,1)S(1)}, u32[]{:S(2)}, u32[]{:S(2)}) collective-permute-start(bf16[16,32,384]{2,1,0:T(8,128)(2,1)S(1)} %collective-permute-done.1.refs_2_), channel_id=1, source_target_pairs={{0,1},{1,0},{2,3},{3,2},{4,5},{5,4},{6,7},{7,6},{8,9},{9,8},{10,11... | collective-permute-start | bytes 1179656 | tf_op jit(solution)/shard_map/ppermute | solution.py:348
  42.5 0.7 copy-start.7
  42.5 0.9 copy-start.6
  43.4 0.8 copy-start.8
  58.6 3.3 %collective-permute-start.5 = (f32[8,2048]{1,0:T(8,128)}, f32[8,2048]{1,0:T(8,128)S(1)}, u32[]{:S(2)}, u32[]{:S(2)}) collective-permute-start(f32[8,2048]{1,0:T(8,128)} %stats.1.refs_6_), channel_id=1, source_target_pairs={{0,32},{32,0},{64,96},{96,64},{1,33},{33,1},{65,97},{97,65},{2,34}... | collective-permute-start | bytes 196616 | tf_op jit(solution)/shard_map/ppermute | solution.py:344
  59.2 4.8 %collective-permute-start.4 = (f32[8,2048]{1,0:T(8,128)}, f32[8,2048]{1,0:T(8,128)S(1)}, u32[]{:S(2)}, u32[]{:S(2)}) collective-permute-start(f32[8,2048]{1,0:T(8,128)} %stats.1.refs_6_), channel_id=1, source_target_pairs={{0,1},{1,0},{2,3},{3,2},{4,5},{5,4},{6,7},{7,6},{8,9},{9,8},{10,11... | collective-permute-start | bytes 196616 | tf_op jit(solution)/shard_map/ppermute | solution.py:348
  61.9 2.9 %copy-start.9 = (f32[8,2048]{1,0:T(8,128)}, f32[8,2048]{1,0:T(8,128)S(1)}, u32[]{:S(2)}) copy-start(f32[8,2048]{1,0:T(8,128)S(1)} %collective-permute-done.5.refs_8_) | copy-start | bytes 196612
  61.9 2.9 %collective-permute-start.6 = (f32[8,2048]{1,0:T(8,128)S(1)}, f32[8,2048]{1,0:T(8,128)S(1)}, u32[]{:S(2)}, u32[]{:S(2)}) collective-permute-start(f32[8,2048]{1,0:T(8,128)S(1)} %collective-permute-done.5.refs_8_), channel_id=1, source_target_pairs={{0,1},{1,0},{2,3},{3,2},{4,5},{5,4},{6,7},{7,6},{8,9},{9,8},{10,11... | collective-permute-start | bytes 196616 | tf_op jit(solution)/shard_map/ppermute | solution.py:348
  63.9 0.9 copy-start.10
  64.9 0.6 copy-start.11
  95.6 2.6 %collective-permute-start.8 = (bf16[16,32,384]{2,1,0:T(8,128)(2,1)}, bf16[16,32,384]{2,1,0:T(8,128)(2,1)S(1)}, u32[]{:S(2)}, u32[]{:S(2)}) collective-permute-start(bf16[16,32,384]{2,1,0:T(8,128)(2,1)} %get-tuple-element.12), channel_id=1, source_target_pairs={{0,1},{1,0},{2,3},{3,2},{4,5},{5,4},{6,7},{7,6},{8,9},{9,8},{10,11... | collective-permute-start | bytes 1179656 | tf_op jit(solution)/shard_map/ppermute | solution.py:348
  95.9 11.9 %collective-permute-start.7 = (bf16[16,32,384]{2,1,0:T(8,128)(2,1)}, bf16[16,32,384]{2,1,0:T(8,128)(2,1)S(1)}, u32[]{:S(2)}, u32[]{:S(2)}) collective-permute-start(bf16[16,32,384]{2,1,0:T(8,128)(2,1)} %get-tuple-element.10), channel_id=1, source_target_pairs={{0,96},{96,0},{32,64},{64,32},{1,97},{97,1},{33,65},{65,33},{2,98}... | collective-permute-start | bytes 1179656 | tf_op jit(solution)/shard_map/ppermute | solution.py:340
  98.2 0.8 copy-start
  100.9 7.0 %collective-permute-start.9 = (bf16[16,16,384]{2,1,0:T(8,128)(2,1)}, bf16[16,16,384]{2,1,0:T(8,128)(2,1)S(1)}, u32[]{:S(2)}, u32[]{:S(2)}) collective-permute-start(bf16[16,16,384]{2,1,0:T(8,128)(2,1)} %get-tuple-element.14), channel_id=1, source_target_pairs={{0,32},{32,0},{64,96},{96,64},{1,33},{33,1},{65,97},{97,65},{2,34}... | collective-permute-start | bytes 589832 | tf_op jit(solution)/shard_map/ppermute | solution.py:344
  107.9 0.8 copy-start.3
  107.9 0.8 copy-start.4

commit v6 on v5

--- a/solution.py
+++ b/solution.py
@@ -28,11 +28,8 @@
 C2 = SCALE * math.log2(math.e)
 TQ = 1024
 TK = 512
-GUN = 1
-STQ = 1024
-STK = 2048
+GUN = 4
 SUB = 64
-SUN = 1
 NEG = -1e30
 F32 = jnp.float32
 BF16 = jnp.bfloat16
@@ -71,35 +68,31 @@
     )
 
 
-def pack_rows(a_ref, b_ref, out_ref, base):
-    for turn in range(4):
-        heads = range(turn, H, 4)
-        offset = turn * HD % 128
-        width = 128 if offset + HD <= 128 else 256
-        parts = []
-        for n, (_, cols, dst) in enumerate(WINDOWS):
-            ref = (a_ref, b_ref)[n % 2]
-            rows = slice(n // 2 * HALF, (n // 2 + 1) * HALF)
-            x = jnp.concatenate([ref[rows, h * HD // 128 * 128 : h * HD // 128 * 128 + width] for h in heads], axis=0)
-            parts.append(mm(x, shift(width, cols, offset, dst)))
-        for n, piece in enumerate(pack_four(parts)):
-            for k, h in enumerate(heads):
-                out_ref[h, base : base + HALF, n * 128 : (n + 1) * 128] = piece[k * HALF : (k + 1) * HALF]
-
-
-def pack_kernel(order_ref, place_ref, q_ref, g_ref, k_ref, v_ref, out_ref, k_s, v_s):
+def pack_kernel(order_ref, place_ref, q_ref, g_ref, k_ref, v_ref, out_ref, a_s, b_s):
     i = pl.program_id(0)
-    at = pl.ds(pl.multiple_of(i * PENCIL, PENCIL), PENCIL)
-    k_s[at, :] = k_ref[...]
-    v_s[at, :] = v_ref[...]
-
-    @pl.when(i == 0)
-    def _():
-        pack_rows(q_ref, g_ref, out_ref, 0)
+    at = pl.ds(pl.multiple_of(i // 2 * PD + HALF + i % 2 * PENCIL, PENCIL), PENCIL)
+    a_s[at, :] = k_ref[...]
+    b_s[at, :] = v_ref[...]
 
     @pl.when(i == PD // PENCIL - 1)
     def _():
-        pack_rows(k_s, v_s, out_ref, HALF)
+        for half in range(2):
+            rows = slice(half * HALF, (half + 1) * HALF)
+            a_s[half * PD : half * PD + HALF, :] = q_ref[rows, :]
+            b_s[half * PD : half * PD + HALF, :] = g_ref[rows, :]
+        for turn in range(4):
+            heads = range(turn, H, 4)
+            offset = turn * HD % 128
+            width = 128 if offset + HD <= 128 else 256
+            parts = []
+            for n, (_, cols, dst) in enumerate(WINDOWS):
+                ref = (a_s, b_s)[n % 2]
+                rows = slice(n // 2 * PD, (n // 2 + 1) * PD)
+                x = [ref[rows, h * HD // 128 * 128 : h * HD // 128 * 128 + width] for h in heads]
+                parts.append(mm(jnp.concatenate(x, axis=0), shift(width, cols, offset, dst)))
+            for n, piece in enumerate(pack_four(parts)):
+                for k, h in enumerate(heads):
+                    out_ref[h, :, n * 128 : (n + 1) * 128] = piece[k * PD : (k + 1) * PD]
 
 
 def pack(order, place, obj_query, grad_out, pattern_key, pattern_value):
@@ -113,7 +106,7 @@
             grid=(PD // PENCIL,),
             in_specs=[rows, rows, block, block],
             out_specs=pl.BlockSpec((H, PD, WIDE), lambda i, order, place: (0, 0, 0)),
-            scratch_shapes=[pltpu.VMEM((PD, D), BF16)] * 2,
+            scratch_shapes=[pltpu.VMEM((2 * PD, D), BF16)] * 2,
         ),
         name="pack",
     )(order, place, obj_query, grad_out, pattern_key, pattern_value)
@@ -133,52 +126,106 @@
             out[at, :] = mm(x, shift(width, 128, offset, 0)).astype(BF16)
 
 
-def stats_kernel(*refs):
+def sweep(state, k_ref, v_ref, qt, gt):
+    m, l, w = state
+    rows, cols = k_ref.shape[0], qt.shape[1]
+    s = mm(k_ref[...], qt).reshape(rows // SUB, SUB // 8, 8, cols)
+    d = mm(v_ref[...], gt).reshape(rows // SUB, SUB // 8, 8, cols)
+    for i in range(rows // SUB):
+        top = jnp.maximum(m, jnp.max(s[i], axis=0))
+        fade = jnp.exp2((m - top) * C2)
+        e = jnp.exp2((s[i] - top[None]) * C2)
+        m, l, w = top, l * fade + jnp.sum(e, axis=0), w * fade + jnp.sum(e * d[i], axis=0)
+    return m, l, w
+
+
+def write_stats(st_ref, n, state):
+    m, l, w = state
+    top = jnp.max(m, axis=0, keepdims=True)
+    fade = jnp.exp2((m - top) * C2)
+    row, cols = n // 2 * 4, slice(n % 2 * ROWS, (n % 2 + 1) * ROWS)
+    st_ref[row : row + 1, cols] = top
+    st_ref[row + 1 : row + 2, cols] = jnp.sum(l * fade, axis=0, keepdims=True)
+    st_ref[row + 2 : row + 3, cols] = jnp.sum(w * fade, axis=0, keepdims=True)
+
+
+def first_stats_kernel(qa_ref, qb_ref, kv_ref, st_ref, q_ref, g_ref, k_ref, v_ref):
+    unpack(kv_ref, ((k_ref, 0), (v_ref, 0)))
+    for n, ref in enumerate((qa_ref, qb_ref)):
+        unpack(ref, ((q_ref, n * ROWS), (g_ref, n * ROWS)), turned=True)
+    st_ref[...] = jnp.zeros_like(st_ref)
+    for n in range(2):
+        here = slice(n * ROWS, (n + 1) * ROWS)
+        zero = jnp.zeros((8, ROWS), F32)
+        state = (jnp.full((8, ROWS), NEG, F32), zero, zero)
+        write_stats(st_ref, n, sweep(state, k_ref, v_ref, q_ref[:, here], g_ref[:, here]))
+
+
+def first_stats(qa, qb, kv):
+    return pl.pallas_call(
+        first_stats_kernel,
+        out_shape=[jax.ShapeDtypeStruct((8, NQ // 2), F32)]
+        + [jax.ShapeDtypeStruct((128, 2 * ROWS), BF16)] * 2
+        + [jax.ShapeDtypeStruct((ROWS, 128), BF16)] * 2,
+        in_specs=[VMEM] * 3,
+        out_specs=[VMEM] * 5,
+        cost_estimate=pl.CostEstimate(flops=NQ * NK * 256, transcendentals=NQ * NK // 4, bytes_accessed=2 << 20),
+        name="first_stats",
+    )(qa, qb, kv)
+
+
+def stats_kernel(
+    qa_ref, qb_ref, kv_ref, part_ref, q_own, g_own, k_own, v_own, st_ref, q_s, g_s, k_s, v_s
+):
+    unpack(kv_ref, ((k_s, 0), (v_s, 0)))
+    for n, ref in enumerate((qa_ref, qb_ref)):
+        unpack(ref, ((q_s, n * ROWS), (g_s, n * ROWS)), turned=True)
+    st_ref[...] = jnp.zeros_like(st_ref)
+    zero = jnp.zeros((8, ROWS), F32)
+    for n in range(2):
+        here = slice(n * ROWS, (n + 1) * ROWS)
+        top, total, weighted = (part_ref[i : i + 1, here] for i in range(3))
+        first = lax.broadcasted_iota(jnp.int32, (8, ROWS), 0) == 0
+        state = (zero + top, jnp.where(first, total, zero), jnp.where(first, weighted, zero))
+        write_stats(st_ref, n, sweep(state, k_s, v_s, q_own[:, here], g_own[:, here]))
+    for n in range(2):
+        here = slice(n * ROWS, (n + 1) * ROWS)
+        qt, gt = q_s[:, here], g_s[:, here]
+        state = sweep((jnp.full((8, ROWS), NEG, F32), zero, zero), k_own, v_own, qt, gt)
+        write_stats(st_ref, 2 + n, sweep(state, k_s, v_s, qt, gt))
+
+
+def stats(qa, qb, kv, first):
+    return pl.pallas_call(
+        stats_kernel,
+        out_shape=jax.ShapeDtypeStruct((8, NQ // 2), F32),
+        in_specs=[VMEM] * 8,
+        out_specs=VMEM,
+        scratch_shapes=[pltpu.VMEM((128, 2 * ROWS), BF16)] * 2 + [pltpu.VMEM((ROWS, 128), BF16)] * 2,
+        cost_estimate=pl.CostEstimate(flops=3 * NQ * NK * 256, transcendentals=NQ * NK, bytes_accessed=4 << 20),
+        name="stats",
+    )(qa, qb, kv, *first)
+
+
+def rows_kernel(*refs):
     q_refs, kv_refs = refs[:N_Z], refs[N_Z : N_Z + 2]
-    st_ref, q_s, g_s, k_s, v_s = refs[N_Z + 2 :]
+    q_s, g_s, k_s, v_s, t_s = refs[N_Z + 2 :]
     for n, ref in enumerate(kv_refs):
         unpack(ref, ((k_s, n * ROWS), (v_s, n * ROWS)))
+        unpack(ref, ((t_s, n * ROWS), (None, 0)), turned=True)
     for n, ref in enumerate(q_refs):
-        unpack(ref, ((q_s, n * ROWS), (g_s, n * ROWS)), turned=True)
-    st_ref[...] = jnp.zeros_like(st_ref)
-
-    for n in range(NQ // STQ):
-        q0 = n * STQ
-        qt = q_s[:, q0 : q0 + STQ]
-        gt = g_s[:, q0 : q0 + STQ]
-
-        def one_chunk(j, carry):
-            m, l, w = carry
-            k0 = pl.multiple_of(j * STK, STK)
-            s = mm(k_s[pl.ds(k0, STK), :], qt).reshape(STK // SUB, SUB // 8, 8, STQ)
-            d = mm(v_s[pl.ds(k0, STK), :], gt).reshape(STK // SUB, SUB // 8, 8, STQ)
-            for i in range(STK // SUB):
-                top = jnp.maximum(m, jnp.max(s[i], axis=0))
-                fade = jnp.exp2((m - top) * C2)
-                e = jnp.exp2((s[i] - top[None]) * C2)
-                m, l, w = top, l * fade + jnp.sum(e, axis=0), w * fade + jnp.sum(e * d[i], axis=0)
-            return m, l, w
-
-        zero = jnp.zeros((8, STQ), F32)
-        start = (jnp.full((8, STQ), NEG, F32), zero, zero)
-        m, l, w = lax.fori_loop(0, NK // STK, one_chunk, start, unroll=SUN)
-        top = jnp.max(m, axis=0, keepdims=True)
-        fade = jnp.exp2((m - top) * C2)
-        row, cols = q0 // (NQ // 2) * 4, slice(q0 % (NQ // 2), q0 % (NQ // 2) + STQ)
-        st_ref[row : row + 1, cols] = top
-        st_ref[row + 1 : row + 2, cols] = jnp.sum(l * fade, axis=0, keepdims=True)
-        st_ref[row + 2 : row + 3, cols] = jnp.sum(w * fade, axis=0, keepdims=True)
-
-
-def stats(queries, keys):
-    return pl.pallas_call(
-        stats_kernel,
-        out_shape=jax.ShapeDtypeStruct((8, NQ // 2), F32),
+        unpack(ref, ((q_s, n * ROWS), (g_s, n * ROWS)))
+
+
+def rows_of(queries, keys):
+    return pl.pallas_call(
+        rows_kernel,
+        out_shape=[jax.ShapeDtypeStruct((NQ, 128), BF16)] * 2
+        + [jax.ShapeDtypeStruct((NK, 128), BF16)] * 2
+        + [jax.ShapeDtypeStruct((HD, NK), BF16)],
         in_specs=[VMEM] * (N_Z + 2),
-        out_specs=VMEM,
-        scratch_shapes=[pltpu.VMEM((128, NQ), BF16)] * 2 + [pltpu.VMEM((NK, 128), BF16)] * 2,
-        cost_estimate=pl.CostEstimate(flops=4 * NQ * NK * 256, transcendentals=NQ * NK, bytes_accessed=4 << 20),
-        name="stats",
+        out_specs=[VMEM] * 5,
+        name="rows_of",
     )(*queries, *keys)
 
 
@@ -196,15 +243,10 @@
 
 
 def grads_kernel(*refs):
-    q_refs, kv_refs, st_refs = refs[:N_Z], refs[N_Z : N_Z + 2], refs[N_Z + 2 : 2 * N_Z + 2]
-    dkv_refs, dq_refs = refs[2 * N_Z + 2 : 2 * N_Z + 4], refs[2 * N_Z + 4 : 2 * N_Z + 6]
-    scratch = refs[2 * N_Z + 6 :]
-    q_s, g_s, k_s, v_s, t_s, dq_s, dk_s, dv_s, log_s, mean_s = scratch
-    for n, ref in enumerate(kv_refs):
-        unpack(ref, ((k_s, n * ROWS), (v_s, n * ROWS)))
-        unpack(ref, ((t_s, n * ROWS), (None, 0)), turned=True)
-    for n, ref in enumerate(q_refs):
-        unpack(ref, ((q_s, n * ROWS), (g_s, n * ROWS)))
+    q_s, g_s, k_s, v_s, t_s = refs[:5]
+    st_refs, dkv_refs, dq_refs = refs[5 : 5 + N_Z], refs[5 + N_Z : 7 + N_Z], refs[7 + N_Z : 9 + N_Z]
+    dq_s, dk_s, dv_s, log_s, mean_s = refs[9 + N_Z :]
+    for n in range(N_Z):
         log_now, mean_now = joined([block_of(st, n ^ t) for t, st in enumerate(st_refs)])
         here = slice(n * ROWS, (n + 1) * ROWS)
         log_s[:, here] = jnp.broadcast_to(log_now, (8, ROWS))
@@ -258,21 +300,18 @@
             ref[:, row : row + PENCIL, k * 128 : (k + 1) * 128] = piece.reshape(N_G, PENCIL, 128)
 
 
-def grads(queries, keys, statistics):
+def grads(rows, statistics):
     return pl.pallas_call(
         grads_kernel,
         out_shape=[jax.ShapeDtypeStruct((N_G, HALF, WIDE), BF16)] * 4,
-        in_specs=[VMEM] * (2 * N_Z + 2),
+        in_specs=[VMEM] * (5 + N_Z),
         out_specs=[VMEM] * 4,
-        scratch_shapes=[pltpu.VMEM((NQ, 128), BF16)] * 2
-        + [pltpu.VMEM((NK, 128), BF16)] * 2
-        + [pltpu.VMEM((HD, NK), BF16)]
-        + [pltpu.VMEM((HD, NQ), F32)]
+        scratch_shapes=[pltpu.VMEM((HD, NQ), F32)]
         + [pltpu.VMEM((NK, 128), BF16)] * 2
         + [pltpu.VMEM((8, NQ), F32)] * 2,
         cost_estimate=pl.CostEstimate(flops=10 * NQ * NK * 256, transcendentals=NQ * NK, bytes_accessed=8 << 20),
         name="grads",
-    )(*queries, *keys, *statistics)
+    )(*rows, *statistics)
 
 
 def meet_kernel(mine_ref, theirs_ref, keep_ref, send_ref):
@@ -359,13 +398,16 @@
     sent = pack(pencil_order, place, obj_query, grad_out, pattern_key, pattern_value)
     got = to_heads(sent)
     queries, keys = [got[:, :HALF]], [got[:, HALF:]]
-    third = over_b(queries[0])
+    queries.append(over_core(queries[0]))
+    queries.append(over_b(queries[0]))
     keys.append(over_a(keys[0]))
-    queries += [over_core(queries[0]), third, over_core(third)]
-    statistics = [stats(queries, keys)]
+    first = first_stats(queries[0], queries[1], keys[0])
+    queries.append(over_core(queries[2]))
+    statistics = [stats(queries[2], queries[3], keys[1], first)]
     third = over_b(statistics[0])
     statistics += [over_core(statistics[0]), third, over_core(third)]
-    keys_here, keys_there, queries_here, queries_there = grads(queries, keys, statistics)
+    rows = rows_of(queries, keys)
+    keys_here, keys_there, queries_here, queries_there = grads(rows, statistics)
     keys_got = over_a(keys_there)
     queries_got = over_core(queries_there)
     keep, send = meet(queries_here, queries_got)

time: 130 us -> 128 us (0.985)
  waiting for transfers between devices: 16.9 us -> 11.8 us
  Pallas kernels: 55.4 us -> 58.4 us
    pallas_call x0 -> x2, Pallas kernels: none -> 10 us  [the longest x1 5.28 us: first_stats(): pl.pallas_call(first_stats_kernel, out_shape=[jax.ShapeDtypeStruct((8, NQ...]
    ppermute x2, waiting for transfers between devices: 10.8 us -> 6.51 us  [over_a(): return lax.ppermute(x, Z, ((0, 3), (3, 0), (1, 2), (2, 1)))]
    pallas_call x1, Pallas kernels: 30.1 us -> 26.5 us  [grads(): pl.pallas_call(grads_kernel, out_shape=[jax.ShapeDtypeStruct((N_G, HALF,...]
    pallas_call x1, Pallas kernels: 14.4 us -> 11.1 us  [stats(): pl.pallas_call(stats_kernel, out_shape=jax.ShapeDtypeStruct((8, NQ // 2),...]
    ppermute x5, starting transfers between devices: 7.74 us -> 5.8 us  [over_core(): return lax.ppermute(x, CORE, ((0, 1), (1, 0)))]
    ppermute x2, starting transfers between devices: 4.47 us -> 5.82 us  [over_a(): return lax.ppermute(x, Z, ((0, 3), (3, 0), (1, 2), (2, 1)))]
  transfers between devices with their start and end apart: 10 -> 10, of which waited for: 5 -> 3; matrix products, arithmetic and copies ran while one was open for 0% -> 0% of each run, Pallas kernels for 2% -> 9%
where the time goes in v6:
time: 128 us; the launch traced here: 127 us
  Pallas kernels  58.4 us (46%)
  blocking collectives  36.6 us (29%)
  starting transfers between devices  14.8 us (12%)
  waiting for transfers between devices  11.8 us (9%)
  local copies, waits for them, and re-layouts  3.95 us (3%)
    all_to_all x2, blocking collectives, to_heads(): return lax.all_to_all(x, HEADS, 0, 0, tiled=True)  36.6 us
    pallas_call x1, Pallas kernels, grads(): pl.pallas_call(grads_kernel, out_shape=[jax.ShapeDtypeStruct((N_G, HALF,...  26.5 us
    pallas_call x1, Pallas kernels, stats(): pl.pallas_call(stats_kernel, out_shape=jax.ShapeDtypeStruct((8, NQ // 2),...  11.1 us
    ppermute x2, waiting for transfers between devices, over_a(): return lax.ppermute(x, Z, ((0, 3), (3, 0), (1, 2), (2, 1)))  6.51 us
    ppermute x2, starting transfers between devices, over_a(): return lax.ppermute(x, Z, ((0, 3), (3, 0), (1, 2), (2, 1)))  5.82 us
    ppermute x5, starting transfers between devices, over_core(): return lax.ppermute(x, CORE, ((0, 1), (1, 0)))  5.8 us
    ppermute x3, waiting for transfers between devices, over_b(): return lax.ppermute(x, Z, ((0, 1), (1, 0), (2, 3), (3, 2)))  5.32 us
    pallas_call x1, Pallas kernels, first_stats(): pl.pallas_call(first_stats_kernel, out_shape=[jax.ShapeDtypeStruct((8, NQ...  5.28 us
  transfers between devices with their start and end apart: 10, of which 3 were waited for; matrix products, arithmetic and copies ran while one was open for 0% of the time, Pallas kernels for 9%

profile of v6, /device:TPU:1, one launch (start us, length us, event | category | flops | bytes accessed | tf_op | source)
XLA Modules:
  0.0 126.9 jit_solution(16964696971216419103)
XLA Ops:
  1.2 4.3 %pack.1 = bf16[16,64,384]{2,1,0:T(8,128)(2,1)} custom-call(s32[512]{0:T(512)} %order_ref.1, s32[2]{0:T(128)} %pad_add_fusion.place_ref, bf16[64,1536]{1,0:T(8,128)(2,1)} %q_ref.1, bf16[64,1536]{1,0:T(8,128)(2,1)} %g_ref.1, bf16[512,1536]{1,0:T(8,128)(2,1)} %k_ref.1, bf16[512,1536]{1,0:T(8,128)(2,1)} %v_ref.1), custom_call_target="tpu_custom_call" | custom-call | tf_op jit(solution)/shard_map/pack/pallas_call | solution.py:101
  5.5 21.1 %all_to_all.10 = bf16[16,64,384]{2,1,0:T(8,128)(2,1)S(1)} all-to-all(bf16[16,64,384]{2,1,0:T(8,128)(2,1)} %pack.1), channel_id=1, replica_groups=mesh['blk_0'=4,'blk_1'=2,'grp_0'=2,'grp_1'=4,'grp_2'=2] {'blk_1','grp_0'..., dimensions={0} | all-to-all | bytes 1572864 | tf_op jit(solution)/shard_map/all_to_all | solution.py:391
  26.7 1.7 %collective-permute-start.1 = (bf16[16,32,384]{2,1,0:T(8,128)(2,1)S(1)}, bf16[16,32,384]{2,1,0:T(8,128)(2,1)S(1)}, u32[]{:S(2)}, u32[]{:S(2)}) collective-permute-start(bf16[16,32,384]{2,1,0:T(8,128)(2,1)S(1)} %get-tuple-element.36.refs_0_.qa_ref), channel_id=1, source_target_pairs={{0,32},{32,0},{64,96},{96,64},{1,33},{33,1},{65,97},{97,65},{2,34}... | collective-permute-start | bytes 1179656 | tf_op jit(solution)/shard_map/ppermute | solution.py:383
  28.4 2.0 %collective-permute-start = (bf16[16,32,384]{2,1,0:T(8,128)(2,1)S(1)}, bf16[16,32,384]{2,1,0:T(8,128)(2,1)S(1)}, u32[]{:S(2)}, u32[]{:S(2)}) collective-permute-start(bf16[16,32,384]{2,1,0:T(8,128)(2,1)S(1)} %get-tuple-element.36.refs_0_.qa_ref), channel_id=1, source_target_pairs={{0,1},{1,0},{2,3},{3,2},{4,5},{5,4},{6,7},{7,6},{8,9},{9,8},{10,11... | collective-permute-start | bytes 1179656 | tf_op jit(solution)/shard_map/ppermute | solution.py:387
  30.5 2.2 %collective-permute-start.3 = (bf16[16,32,384]{2,1,0:T(8,128)(2,1)S(1)}, bf16[16,32,384]{2,1,0:T(8,128)(2,1)S(1)}, u32[]{:S(2)}, u32[]{:S(2)}) collective-permute-start(bf16[16,32,384]{2,1,0:T(8,128)(2,1)S(1)} %get-tuple-element.35.refs_4_.kv_ref), channel_id=1, source_target_pairs={{0,96},{96,0},{32,64},{64,32},{1,97},{97,1},{33,65},{65,33},{2,98}... | collective-permute-start | bytes 1179656 | tf_op jit(solution)/shard_map/ppermute | solution.py:379
  32.7 3.3 %collective-permute-done.1.refs_2_.qa_ref = bf16[16,32,384]{2,1,0:T(8,128)(2,1)S(1)} collective-permute-done((bf16[16,32,384]{2,1,0:T(8,128)(2,1)S(1)}, bf16[16,32,384]{2,1,0:T(8,128)(2,1)S(1)}, u32[]{:S(2)}, u32[]{:S(2)}) %collective-permute-start.1) | collective-permute-done | bytes 393248 | tf_op jit(solution)/shard_map/ppermute | solution.py:383
  36.1 2.4 %collective-permute-start.2 = (bf16[16,32,384]{2,1,0:T(8,128)(2,1)S(1)}, bf16[16,32,384]{2,1,0:T(8,128)(2,1)S(1)}, u32[]{:S(2)}, u32[]{:S(2)}) collective-permute-start(bf16[16,32,384]{2,1,0:T(8,128)(2,1)S(1)} %collective-permute-done.1.refs_2_.qa_ref), channel_id=1, source_target_pairs={{0,1},{1,0},{2,3},{3,2},{4,5},{5,4},{6,7},{7,6},{8,9},{9,8},{10,11... | collective-permute-start | bytes 1179656 | tf_op jit(solution)/shard_map/ppermute | solution.py:387
  38.5 0.7 copy-done.3
  39.3 5.3 %first_stats.1 = (f32[8,2048]{1,0:T(8,128)}, bf16[128,2048]{1,0:T(8,128)(2,1)}, bf16[128,2048]{1,0:T(8,128)(2,1)}, bf16[1024,128]{1,0:T(8,128)(2,1)}, bf16[1024,128]{1,0:T(8,128)(2,1)}) custom-call(bf16[16,32,384]{2,1,0:T(8,128)(2,1)} %copy-done.1, bf16[16,32,384]{2,1,0:T(8,128)(2,1)} %copy-done.3, bf16[16,32,384]{2,1,0:T(8,128)(2,1)} %copy-done), custom_call_target="tpu_custom_call" | custom-call | flops 2147483648 | bytes 2097152 | tf_op jit(solution)/shard_map/first_stats/pallas_call | solution.py:165
  44.6 0.7 copy-done.4
  45.5 11.1 %stats.1.refs_5_ = f32[8,2048]{1,0:T(8,128)} custom-call(bf16[16,32,384]{2,1,0:T(8,128)(2,1)} %copy-done.2, bf16[16,32,384]{2,1,0:T(8,128)(2,1)} %copy-done.5, bf16[16,32,384]{2,1,0:T(8,128)(2,1)} %copy-done.4, f32[8,2048]{1,0:T(8,128)} %get-tuple-element.24.part_ref, bf16[128,2048]{1,0:T(8,128)(2,1)} %get-tuple-element.25.q_own, ...), custom_call_target="tpu_custom_call" | custom-call | flops 6442450944 | bytes 4194304 | tf_op jit(solution)/shard_map/stats/pallas_call | solution.py:199
  56.6 1.5 %collective-permute-start.5 = (f32[8,2048]{1,0:T(8,128)}, f32[8,2048]{1,0:T(8,128)S(1)}, u32[]{:S(2)}, u32[]{:S(2)}) collective-permute-start(f32[8,2048]{1,0:T(8,128)} %stats.1.refs_5_), channel_id=1, source_target_pairs={{0,32},{32,0},{64,96},{96,64},{1,33},{33,1},{65,97},{97,65},{2,34}... | collective-permute-start | bytes 196616 | tf_op jit(solution)/shard_map/ppermute | solution.py:383
  58.4 2.0 %collective-permute-done.5.refs_7_ = f32[8,2048]{1,0:T(8,128)S(1)} collective-permute-done((f32[8,2048]{1,0:T(8,128)}, f32[8,2048]{1,0:T(8,128)S(1)}, u32[]{:S(2)}, u32[]{:S(2)}) %collective-permute-start.5) | collective-permute-done | bytes 65568 | tf_op jit(solution)/shard_map/ppermute | solution.py:383
  60.4 0.9 collective-permute-start.6
  61.3 4.7 %rows_of.1 = (bf16[4096,128]{1,0:T(8,128)(2,1)}, bf16[4096,128]{1,0:T(8,128)(2,1)}, bf16[2048,128]{1,0:T(8,128)(2,1)}, bf16[2048,128]{1,0:T(8,128)(2,1)}, bf16[96,2048]{1,0:T(8,128)(2,1)}) custom-call(bf16[16,32,384]{2,1,0:T(8,128)(2,1)} %copy-done.1, bf16[16,32,384]{2,1,0:T(8,128)(2,1)} %copy-done.3, bf16[16,32,384]{2,1,0:T(8,128)(2,1)} %copy-done.2, ...), custom_call_target="tpu_custom_call" | custom-call | tf_op jit(solution)/shard_map/rows_of/pallas_call | solution.py:221
  66.7 26.5 %grads.1 = (bf16[16,32,384]{2,1,0:T(8,128)(2,1)}, bf16[16,32,384]{2,1,0:T(8,128)(2,1)}, bf16[16,32,384]{2,1,0:T(8,128)(2,1)}, bf16[16,32,384]{2,1,0:T(8,128)(2,1)}) custom-call(bf16[4096,128]{1,0:T(8,128)(2,1)} %get-tuple-element.19.refs_0_, bf16[4096,128]{1,0:T(8,128)(2,1)} %get-tuple-element.20.refs_1_, bf16[2048,128]{1,0:T(8,128)(2,1)} %get-tuple-element.21.refs_2_, ...), custom_call_target="tpu_custom_call" | custom-call | flops 21474836480 | bytes 8388608 | tf_op jit(solution)/shard_map/grads/pallas_call | solution.py:304
  93.3 3.6 %collective-permute-start.7 = (bf16[16,32,384]{2,1,0:T(8,128)(2,1)}, bf16[16,32,384]{2,1,0:T(8,128)(2,1)S(1)}, u32[]{:S(2)}, u32[]{:S(2)}) collective-permute-start(bf16[16,32,384]{2,1,0:T(8,128)(2,1)} %get-tuple-element.30), channel_id=1, source_target_pairs={{0,96},{96,0},{32,64},{64,32},{1,97},{97,1},{33,65},{65,33},{2,98}... | collective-permute-start | bytes 1179656 | tf_op jit(solution)/shard_map/ppermute | solution.py:379
  96.9 0.7 copy-done.6
  97.6 2.0 %meet.1 = (f32[16,16,384]{2,1,0:T(8,128)}, bf16[16,16,384]{2,1,0:T(8,128)(2,1)}) custom-call(bf16[16,32,384]{2,1,0:T(8,128)(2,1)} %get-tuple-element.31.mine_ref, bf16[16,32,384]{2,1,0:T(8,128)(2,1)} %copy-done.6), custom_call_target="tpu_custom_call" | custom-call | tf_op jit(solution)/shard_map/meet/pallas_call | solution.py:324
  99.6 6.5 %collective-permute-done.7.refs_1_ = bf16[16,32,384]{2,1,0:T(8,128)(2,1)S(1)} collective-permute-done((bf16[16,32,384]{2,1,0:T(8,128)(2,1)}, bf16[16,32,384]{2,1,0:T(8,128)(2,1)S(1)}, u32[]{:S(2)}, u32[]{:S(2)}) %collective-permute-start.7) | collective-permute-done | bytes 393248 | tf_op jit(solution)/shard_map/ppermute | solution.py:379
  106.1 0.8 copy-done.7
  106.9 2.3 %combine.1 = bf16[16,48,384]{2,1,0:T(8,128)(2,1)} custom-call(bf16[16,32,384]{2,1,0:T(8,128)(2,1)} %get-tuple-element.29.refs_0_, bf16[16,32,384]{2,1,0:T(8,128)(2,1)} %copy-done.7, f32[16,16,384]{2,1,0:T(8,128)} %get-tuple-element.33.refs_2_, bf16[16,16,384]{2,1,0:T(8,128)(2,1)} %copy-done.8), custom_call_target="tpu_custom_call" | custom-call | tf_op jit(solution)/shard_map/combine/pallas_call | solution.py:346
  109.2 15.5 %all_to_all.11.got_ref = bf16[16,48,384]{2,1,0:T(8,128)(2,1)} all-to-all(bf16[16,48,384]{2,1,0:T(8,128)(2,1)} %combine.1), channel_id=1, replica_groups=mesh['blk_0'=4,'blk_1'=2,'grp_0'=2,'grp_1'=4,'grp_2'=2] {'blk_1','grp_0'..., dimensions={0} | all-to-all | bytes 1179648 | tf_op jit(solution)/shard_map/all_to_all | solution.py:391
  124.7 2.2 %finish.1 = (bf16[64,1536]{1,0:T(8,128)(2,1)}, bf16[64,1536]{1,0:T(8,128)(2,1)}, bf16[64,1536]{1,0:T(8,128)(2,1)}) custom-call(bf16[16,48,384]{2,1,0:T(8,128)(2,1)} %all_to_all.11.got_ref), custom_call_target="tpu_custom_call" | custom-call | tf_op jit(solution)/shard_map/finish/pallas_call | solution.py:369
  (32 shorter events, 2.0 us)
Async XLA Ops:
  26.7 11.8 %copy-start = (bf16[16,32,384]{2,1,0:T(8,128)(2,1)}, bf16[16,32,384]{2,1,0:T(8,128)(2,1)S(1)}, u32[]{:S(2)}) copy-start(bf16[16,32,384]{2,1,0:T(8,128)(2,1)S(1)} %get-tuple-element.35.refs_4_.kv_ref) | copy-start | bytes 1179652
  26.7 11.8 %copy-start.1 = (bf16[16,32,384]{2,1,0:T(8,128)(2,1)}, bf16[16,32,384]{2,1,0:T(8,128)(2,1)S(1)}, u32[]{:S(2)}) copy-start(bf16[16,32,384]{2,1,0:T(8,128)(2,1)S(1)} %get-tuple-element.36.refs_0_.qa_ref) | copy-start | bytes 1179652
  26.7 9.3 %collective-permute-start.1 = (bf16[16,32,384]{2,1,0:T(8,128)(2,1)S(1)}, bf16[16,32,384]{2,1,0:T(8,128)(2,1)S(1)}, u32[]{:S(2)}, u32[]{:S(2)}) collective-permute-start(bf16[16,32,384]{2,1,0:T(8,128)(2,1)S(1)} %get-tuple-element.36.refs_0_.qa_ref), channel_id=1, source_target_pairs={{0,32},{32,0},{64,96},{96,64},{1,33},{33,1},{65,97},{97,65},{2,34}... | collective-permute-start | bytes 1179656 | tf_op jit(solution)/shard_map/ppermute | solution.py:383
  28.4 10.1 %collective-permute-start = (bf16[16,32,384]{2,1,0:T(8,128)(2,1)S(1)}, bf16[16,32,384]{2,1,0:T(8,128)(2,1)S(1)}, u32[]{:S(2)}, u32[]{:S(2)}) collective-permute-start(bf16[16,32,384]{2,1,0:T(8,128)(2,1)S(1)} %get-tuple-element.36.refs_0_.qa_ref), channel_id=1, source_target_pairs={{0,1},{1,0},{2,3},{3,2},{4,5},{5,4},{6,7},{7,6},{8,9},{9,8},{10,11... | collective-permute-start | bytes 1179656 | tf_op jit(solution)/shard_map/ppermute | solution.py:387
  30.5 14.1 %collective-permute-start.3 = (bf16[16,32,384]{2,1,0:T(8,128)(2,1)S(1)}, bf16[16,32,384]{2,1,0:T(8,128)(2,1)S(1)}, u32[]{:S(2)}, u32[]{:S(2)}) collective-permute-start(bf16[16,32,384]{2,1,0:T(8,128)(2,1)S(1)} %get-tuple-element.35.refs_4_.kv_ref), channel_id=1, source_target_pairs={{0,96},{96,0},{32,64},{64,32},{1,97},{97,1},{33,65},{65,33},{2,98}... | collective-permute-start | bytes 1179656 | tf_op jit(solution)/shard_map/ppermute | solution.py:379
  36.0 8.5 %copy-start.2 = (bf16[16,32,384]{2,1,0:T(8,128)(2,1)}, bf16[16,32,384]{2,1,0:T(8,128)(2,1)S(1)}, u32[]{:S(2)}) copy-start(bf16[16,32,384]{2,1,0:T(8,128)(2,1)S(1)} %collective-permute-done.1.refs_2_.qa_ref) | copy-start | bytes 1179652
  36.1 8.5 %collective-permute-start.2 = (bf16[16,32,384]{2,1,0:T(8,128)(2,1)S(1)}, bf16[16,32,384]{2,1,0:T(8,128)(2,1)S(1)}, u32[]{:S(2)}, u32[]{:S(2)}) collective-permute-start(bf16[16,32,384]{2,1,0:T(8,128)(2,1)S(1)} %collective-permute-done.1.refs_2_.qa_ref), channel_id=1, source_target_pairs={{0,1},{1,0},{2,3},{3,2},{4,5},{5,4},{6,7},{7,6},{8,9},{9,8},{10,11... | collective-permute-start | bytes 1179656 | tf_op jit(solution)/shard_map/ppermute | solution.py:387
  38.5 0.7 copy-start.3
  44.5 0.8 copy-start.4
  44.6 0.9 copy-start.5
  56.6 3.8 %collective-permute-start.5 = (f32[8,2048]{1,0:T(8,128)}, f32[8,2048]{1,0:T(8,128)S(1)}, u32[]{:S(2)}, u32[]{:S(2)}) collective-permute-start(f32[8,2048]{1,0:T(8,128)} %stats.1.refs_5_), channel_id=1, source_target_pairs={{0,32},{32,0},{64,96},{96,64},{1,33},{33,1},{65,97},{97,65},{2,34}... | collective-permute-start | bytes 196616 | tf_op jit(solution)/shard_map/ppermute | solution.py:383
  58.1 8.0 %collective-permute-start.4 = (f32[8,2048]{1,0:T(8,128)}, f32[8,2048]{1,0:T(8,128)S(1)}, u32[]{:S(2)}, u32[]{:S(2)}) collective-permute-start(f32[8,2048]{1,0:T(8,128)} %stats.1.refs_5_), channel_id=1, source_target_pairs={{0,1},{1,0},{2,3},{3,2},{4,5},{5,4},{6,7},{7,6},{8,9},{9,8},{10,11... | collective-permute-start | bytes 196616 | tf_op jit(solution)/shard_map/ppermute | solution.py:387
  60.4 5.7 %copy-start.9 = (f32[8,2048]{1,0:T(8,128)}, f32[8,2048]{1,0:T(8,128)S(1)}, u32[]{:S(2)}) copy-start(f32[8,2048]{1,0:T(8,128)S(1)} %collective-permute-done.5.refs_7_) | copy-start | bytes 196612
  60.4 5.7 %collective-permute-start.6 = (f32[8,2048]{1,0:T(8,128)S(1)}, f32[8,2048]{1,0:T(8,128)S(1)}, u32[]{:S(2)}, u32[]{:S(2)}) collective-permute-start(f32[8,2048]{1,0:T(8,128)S(1)} %collective-permute-done.5.refs_7_), channel_id=1, source_target_pairs={{0,1},{1,0},{2,3},{3,2},{4,5},{5,4},{6,7},{7,6},{8,9},{9,8},{10,11... | collective-permute-start | bytes 196616 | tf_op jit(solution)/shard_map/ppermute | solution.py:387
  66.1 0.6 copy-start.10
  66.1 0.7 copy-start.11
  93.3 3.6 %collective-permute-start.8 = (bf16[16,32,384]{2,1,0:T(8,128)(2,1)}, bf16[16,32,384]{2,1,0:T(8,128)(2,1)S(1)}, u32[]{:S(2)}, u32[]{:S(2)}) collective-permute-start(bf16[16,32,384]{2,1,0:T(8,128)(2,1)} %get-tuple-element.32), channel_id=1, source_target_pairs={{0,1},{1,0},{2,3},{3,2},{4,5},{5,4},{6,7},{7,6},{8,9},{9,8},{10,11... | collective-permute-start | bytes 1179656 | tf_op jit(solution)/shard_map/ppermute | solution.py:387
  93.3 12.8 %collective-permute-start.7 = (bf16[16,32,384]{2,1,0:T(8,128)(2,1)}, bf16[16,32,384]{2,1,0:T(8,128)(2,1)S(1)}, u32[]{:S(2)}, u32[]{:S(2)}) collective-permute-start(bf16[16,32,384]{2,1,0:T(8,128)(2,1)} %get-tuple-element.30), channel_id=1, source_target_pairs={{0,96},{96,0},{32,64},{64,32},{1,97},{97,1},{33,65},{65,33},{2,98}... | collective-permute-start | bytes 1179656 | tf_op jit(solution)/shard_map/ppermute | solution.py:379
  96.9 0.7 copy-start.6
  99.6 6.5 %collective-permute-start.9 = (bf16[16,16,384]{2,1,0:T(8,128)(2,1)}, bf16[16,16,384]{2,1,0:T(8,128)(2,1)S(1)}, u32[]{:S(2)}, u32[]{:S(2)}) collective-permute-start(bf16[16,16,384]{2,1,0:T(8,128)(2,1)} %get-tuple-element.34), channel_id=1, source_target_pairs={{0,32},{32,0},{64,96},{96,64},{1,33},{33,1},{65,97},{97,65},{2,34}... | collective-permute-start | bytes 589832 | tf_op jit(solution)/shard_map/ppermute | solution.py:383
  106.1 0.8 copy-start.7
  106.1 0.8 copy-start.8

commit v7 on v6

--- a/solution.py
+++ b/solution.py
@@ -40,6 +40,15 @@
 NK = 2 * ROWS
 VMEM = pl.BlockSpec(memory_space=pltpu.VMEM)
 
+
+def here(*arrays):
+    return [pltpu.with_memory_space_constraint(x, pltpu.VMEM) for x in arrays]
+
+
+def away(x):
+    return pltpu.with_memory_space_constraint(x, pltpu.HBM)
+
+
 WINDOWS = ((0, 128, 0), (0, 256, HD), (128, 256, 2 * HD - 128), (256, 128, 3 * HD - 256))
 
 
@@ -108,8 +117,9 @@
             out_specs=pl.BlockSpec((H, PD, WIDE), lambda i, order, place: (0, 0, 0)),
             scratch_shapes=[pltpu.VMEM((2 * PD, D), BF16)] * 2,
         ),
+        compiler_params=pltpu.CompilerParams(vmem_limit_bytes=16 << 20),
         name="pack",
-    )(order, place, obj_query, grad_out, pattern_key, pattern_value)
+    )(away(order), place, *map(away, (obj_query, grad_out, pattern_key, pattern_value)))
 
 
 def unpack(ref, stores, turned=False):
@@ -164,14 +174,15 @@
 def first_stats(qa, qb, kv):
     return pl.pallas_call(
         first_stats_kernel,
-        out_shape=[jax.ShapeDtypeStruct((8, NQ // 2), F32)]
-        + [jax.ShapeDtypeStruct((128, 2 * ROWS), BF16)] * 2
-        + [jax.ShapeDtypeStruct((ROWS, 128), BF16)] * 2,
+        out_shape=[pltpu.VMEM((8, NQ // 2), F32)]
+        + [pltpu.VMEM((128, 2 * ROWS), BF16)] * 2
+        + [pltpu.VMEM((ROWS, 128), BF16)] * 2,
         in_specs=[VMEM] * 3,
         out_specs=[VMEM] * 5,
         cost_estimate=pl.CostEstimate(flops=NQ * NK * 256, transcendentals=NQ * NK // 4, bytes_accessed=2 << 20),
+        compiler_params=pltpu.CompilerParams(vmem_limit_bytes=32 << 20),
         name="first_stats",
-    )(qa, qb, kv)
+    )(*here(qa, qb, kv))
 
 
 def stats_kernel(
@@ -198,13 +209,14 @@
 def stats(qa, qb, kv, first):
     return pl.pallas_call(
         stats_kernel,
-        out_shape=jax.ShapeDtypeStruct((8, NQ // 2), F32),
+        out_shape=pltpu.VMEM((8, NQ // 2), F32),
         in_specs=[VMEM] * 8,
         out_specs=VMEM,
         scratch_shapes=[pltpu.VMEM((128, 2 * ROWS), BF16)] * 2 + [pltpu.VMEM((ROWS, 128), BF16)] * 2,
         cost_estimate=pl.CostEstimate(flops=3 * NQ * NK * 256, transcendentals=NQ * NK, bytes_accessed=4 << 20),
+        compiler_params=pltpu.CompilerParams(vmem_limit_bytes=36 << 20),
         name="stats",
-    )(qa, qb, kv, *first)
+    )(*here(qa, qb, kv, *first))
 
 
 def rows_kernel(*refs):
@@ -220,13 +232,14 @@
 def rows_of(queries, keys):
     return pl.pallas_call(
         rows_kernel,
-        out_shape=[jax.ShapeDtypeStruct((NQ, 128), BF16)] * 2
-        + [jax.ShapeDtypeStruct((NK, 128), BF16)] * 2
-        + [jax.ShapeDtypeStruct((HD, NK), BF16)],
+        out_shape=[pltpu.VMEM((NQ, 128), BF16)] * 2
+        + [pltpu.VMEM((NK, 128), BF16)] * 2
+        + [pltpu.VMEM((HD, NK), BF16)],
         in_specs=[VMEM] * (N_Z + 2),
         out_specs=[VMEM] * 5,
+        compiler_params=pltpu.CompilerParams(vmem_limit_bytes=24 << 20),
         name="rows_of",
-    )(*queries, *keys)
+    )(*here(*queries, *keys))
 
 
 def block_of(ref, n):
@@ -303,15 +316,16 @@
 def grads(rows, statistics):
     return pl.pallas_call(
         grads_kernel,
-        out_shape=[jax.ShapeDtypeStruct((N_G, HALF, WIDE), BF16)] * 4,
+        out_shape=[pltpu.VMEM((N_G, HALF, WIDE), BF16)] * 4,
         in_specs=[VMEM] * (5 + N_Z),
         out_specs=[VMEM] * 4,
         scratch_shapes=[pltpu.VMEM((HD, NQ), F32)]
         + [pltpu.VMEM((NK, 128), BF16)] * 2
         + [pltpu.VMEM((8, NQ), F32)] * 2,
         cost_estimate=pl.CostEstimate(flops=10 * NQ * NK * 256, transcendentals=NQ * NK, bytes_accessed=8 << 20),
+        compiler_params=pltpu.CompilerParams(vmem_limit_bytes=40 << 20),
         name="grads",
-    )(*rows, *statistics)
+    )(*here(*rows, *statistics))
 
 
 def meet_kernel(mine_ref, theirs_ref, keep_ref, send_ref):
@@ -324,13 +338,14 @@
     return pl.pallas_call(
         meet_kernel,
         out_shape=(
-            jax.ShapeDtypeStruct((N_G, PENCIL, WIDE), F32),
-            jax.ShapeDtypeStruct((N_G, PENCIL, WIDE), BF16),
+            pltpu.VMEM((N_G, PENCIL, WIDE), F32),
+            pltpu.VMEM((N_G, PENCIL, WIDE), BF16),
         ),
         in_specs=[VMEM, VMEM],
         out_specs=(VMEM, VMEM),
+        compiler_params=pltpu.CompilerParams(vmem_limit_bytes=16 << 20),
         name="meet",
-    )(mine, theirs)
+    )(*here(mine, theirs))
 
 
 def combine_kernel(*refs):
@@ -348,8 +363,9 @@
         out_shape=jax.ShapeDtypeStruct((N_G, HALF + PENCIL, WIDE), BF16),
         in_specs=[VMEM] * len(parts),
         out_specs=VMEM,
+        compiler_params=pltpu.CompilerParams(vmem_limit_bytes=16 << 20),
         name="combine",
-    )(*parts)
+    )(*here(*parts))
 
 
 def finish_kernel(got_ref, query_ref, key_ref, value_ref):
@@ -371,6 +387,7 @@
         out_shape=[jax.ShapeDtypeStruct((PD, D), BF16)] * 3,
         in_specs=[VMEM],
         out_specs=[VMEM] * 3,
+        compiler_params=pltpu.CompilerParams(vmem_limit_bytes=16 << 20),
         name="finish",
     )(got)
 

time: 128 us -> 108 us (0.84)
  Pallas kernels: 58.4 us -> 42.3 us
  local copies, waits for them, and re-layouts: 3.95 us -> 0.08 us
  waiting for transfers between devices: 11.8 us -> 14.1 us
  blocking collectives: 36.6 us -> 35.3 us
    pallas_call x5, Pallas kernels: 49.6 us -> 37.6 us  [the longest x1 23.7 us: grads(): pl.pallas_call(grads_kernel, out_shape=[pltpu.VMEM((N_G, HALF, WIDE), BF1...]
    unnamed x24 -> x0, local copies, waits for them, and re-layouts: 3.87 us -> none
    ppermute x2, waiting for transfers between devices: 6.51 us -> 9.14 us  [over_a(): return lax.ppermute(x, Z, ((0, 3), (3, 0), (1, 2), (2, 1)))]
    pallas_call x1, Pallas kernels: 2.26 us -> 0.13 us  [combine(): pl.pallas_call(combine_kernel, out_shape=jax.ShapeDtypeStruct((N_G, HALF...]
  transfers between devices with their start and end apart: 10 -> 10, of which waited for: 3 -> 4; matrix products, arithmetic and copies ran while one was open for 0% -> 0% of each run, Pallas kernels for 9% -> 5%
where the time goes in v7:
time: 108 us; the launch traced here: 107 us
  Pallas kernels  42.3 us (39%)
  blocking collectives  35.3 us (33%)
  starting transfers between devices  14.8 us (14%)
  waiting for transfers between devices  14.1 us (13%)
    all_to_all x2, blocking collectives, to_heads(): return lax.all_to_all(x, HEADS, 0, 0, tiled=True)  35.3 us
    pallas_call x1, Pallas kernels, grads(): pl.pallas_call(grads_kernel, out_shape=[pltpu.VMEM((N_G, HALF, WIDE), BF1...  23.7 us
    ppermute x2, waiting for transfers between devices, over_a(): return lax.ppermute(x, Z, ((0, 3), (3, 0), (1, 2), (2, 1)))  9.14 us
    pallas_call x1, Pallas kernels, stats(): pl.pallas_call(stats_kernel, out_shape=pltpu.VMEM((8, NQ // 2), F32), in_...  8.78 us
    ppermute x5, starting transfers between devices, over_core(): return lax.ppermute(x, CORE, ((0, 1), (1, 0)))  7.01 us
    ppermute x3, waiting for transfers between devices, over_b(): return lax.ppermute(x, Z, ((0, 1), (1, 0), (2, 3), (3, 2)))  4.99 us
    ppermute x2, starting transfers between devices, over_a(): return lax.ppermute(x, Z, ((0, 3), (3, 0), (1, 2), (2, 1)))  4.89 us
    pallas_call x1, Pallas kernels, first_stats(): pl.pallas_call(first_stats_kernel, out_shape=[pltpu.VMEM((8, NQ // 2), F3...  3.43 us
  transfers between devices with their start and end apart: 10, of which 4 were waited for; matrix products, arithmetic and copies ran while one was open for 0% of the time, Pallas kernels for 5%

profile of v7, /device:TPU:1, one launch (start us, length us, event | category | flops | bytes accessed | tf_op | source)
XLA Modules:
  0.0 107.5 jit_solution(1913628563777195324)
XLA Ops:
  0.7 3.4 %pack.1 = bf16[16,64,384]{2,1,0:T(8,128)(2,1)S(1)} custom-call(s32[512]{0:T(512)} %order_ref.1, s32[2]{0:T(128)S(1)} %pad_add_fusion.place_ref, bf16[64,1536]{1,0:T(8,128)(2,1)} %q_ref.1, bf16[64,1536]{1,0:T(8,128)(2,1)} %g_ref.1, bf16[512,1536]{1,0:T(8,128)(2,1)} %k_ref.1, bf16[512,1536]{1,0:T(8,128)(2,1)} %v_ref.1), custom_call_target="tpu_custom_call" | custom-call | tf_op jit(solution)/shard_map/pack/pallas_call | solution.py:110
  4.1 20.9 %all_to_all.10 = bf16[16,64,384]{2,1,0:T(8,128)(2,1)S(1)} all-to-all(bf16[16,64,384]{2,1,0:T(8,128)(2,1)S(1)} %pack.1), channel_id=1, replica_groups=mesh['blk_0'=4,'blk_1'=2,'grp_0'=2,'grp_1'=4,'grp_2'=2] {'blk_1','grp_0'..., dimensions={0} | all-to-all | bytes 1572864 | tf_op jit(solution)/shard_map/all_to_all | solution.py:408
  25.1 1.7 %collective-permute-start.1 = (bf16[16,32,384]{2,1,0:T(8,128)(2,1)S(1)}, bf16[16,32,384]{2,1,0:T(8,128)(2,1)S(1)}, u32[]{:S(2)}, u32[]{:S(2)}) collective-permute-start(bf16[16,32,384]{2,1,0:T(8,128)(2,1)S(1)} %get-tuple-element.36.refs_0_.qa_ref), channel_id=1, source_target_pairs={{0,32},{32,0},{64,96},{96,64},{1,33},{33,1},{65,97},{97,65},{2,34}... | collective-permute-start | bytes 1179656 | tf_op jit(solution)/shard_map/ppermute | solution.py:400
  26.8 2.1 %collective-permute-start = (bf16[16,32,384]{2,1,0:T(8,128)(2,1)S(1)}, bf16[16,32,384]{2,1,0:T(8,128)(2,1)S(1)}, u32[]{:S(2)}, u32[]{:S(2)}) collective-permute-start(bf16[16,32,384]{2,1,0:T(8,128)(2,1)S(1)} %get-tuple-element.36.refs_0_.qa_ref), channel_id=1, source_target_pairs={{0,1},{1,0},{2,3},{3,2},{4,5},{5,4},{6,7},{7,6},{8,9},{9,8},{10,11... | collective-permute-start | bytes 1179656 | tf_op jit(solution)/shard_map/ppermute | solution.py:404
  28.9 2.2 %collective-permute-start.3 = (bf16[16,32,384]{2,1,0:T(8,128)(2,1)S(1)}, bf16[16,32,384]{2,1,0:T(8,128)(2,1)S(1)}, u32[]{:S(2)}, u32[]{:S(2)}) collective-permute-start(bf16[16,32,384]{2,1,0:T(8,128)(2,1)S(1)} %get-tuple-element.35.refs_4_.kv_ref), channel_id=1, source_target_pairs={{0,96},{96,0},{32,64},{64,32},{1,97},{97,1},{33,65},{65,33},{2,98}... | collective-permute-start | bytes 1179656 | tf_op jit(solution)/shard_map/ppermute | solution.py:396
  31.1 3.3 %collective-permute-done.1.refs_2_.qa_ref = bf16[16,32,384]{2,1,0:T(8,128)(2,1)S(1)} collective-permute-done((bf16[16,32,384]{2,1,0:T(8,128)(2,1)S(1)}, bf16[16,32,384]{2,1,0:T(8,128)(2,1)S(1)}, u32[]{:S(2)}, u32[]{:S(2)}) %collective-permute-start.1) | collective-permute-done | bytes 393248 | tf_op jit(solution)/shard_map/ppermute | solution.py:400
  34.5 2.5 %collective-permute-start.2 = (bf16[16,32,384]{2,1,0:T(8,128)(2,1)S(1)}, bf16[16,32,384]{2,1,0:T(8,128)(2,1)S(1)}, u32[]{:S(2)}, u32[]{:S(2)}) collective-permute-start(bf16[16,32,384]{2,1,0:T(8,128)(2,1)S(1)} %collective-permute-done.1.refs_2_.qa_ref), channel_id=1, source_target_pairs={{0,1},{1,0},{2,3},{3,2},{4,5},{5,4},{6,7},{7,6},{8,9},{9,8},{10,11... | collective-permute-start | bytes 1179656 | tf_op jit(solution)/shard_map/ppermute | solution.py:404
  36.9 3.4 %first_stats.1 = (f32[8,2048]{1,0:T(8,128)S(1)}, bf16[128,2048]{1,0:T(8,128)(2,1)S(1)}, bf16[128,2048]{1,0:T(8,128)(2,1)S(1)}, bf16[1024,128]{1,0:T(8,128)(2,1)S(1)}, bf16[1024,128]{1,0:T(8,128)(2,1)S(1)}) custom-call(bf16[16,32,384]{2,1,0:T(8,128)(2,1)S(1)} %get-tuple-element.36.refs_0_.qa_ref, ...), custom_call_target="tpu_custom_call" | custom-call | flops 2147483648 | bytes 2097152 | tf_op jit(solution)/shard_map/first_stats/pallas_call | solution.py:175
  40.3 0.4 collective-permute-done.3.refs_5_.kv_ref
  40.8 8.8 %stats.1.refs_5_ = f32[8,2048]{1,0:T(8,128)S(1)} custom-call(bf16[16,32,384]{2,1,0:T(8,128)(2,1)S(1)} %collective-permute-done.1.refs_2_.qa_ref, bf16[16,32,384]{2,1,0:T(8,128)(2,1)S(1)} %collective-permute-done.2.refs_3_.qb_ref, bf16[16,32,384]{2,1,0:T(8,128)(2,1)S(1)} %collective-permute-done.3.refs_5_.kv_ref, f32[8,2048]{1,0:T(8,128)S(1)} %get-tuple-element.24.part_ref, ...), custom_call_target="tpu_custom_call" | custom-call | flops 6442450944 | bytes 4194304 | tf_op jit(solution)/shard_map/stats/pallas_call | solution.py:210
  49.6 1.1 %collective-permute-start.5 = (f32[8,2048]{1,0:T(8,128)S(1)}, f32[8,2048]{1,0:T(8,128)S(1)}, u32[]{:S(2)}, u32[]{:S(2)}) collective-permute-start(f32[8,2048]{1,0:T(8,128)S(1)} %stats.1.refs_5_), channel_id=1, source_target_pairs={{0,32},{32,0},{64,96},{96,64},{1,33},{33,1},{65,97},{97,65},{2,34}... | collective-permute-start | bytes 196616 | tf_op jit(solution)/shard_map/ppermute | solution.py:400
  50.7 0.4 collective-permute-start.4
  51.1 1.7 %collective-permute-done.5.refs_7_ = f32[8,2048]{1,0:T(8,128)S(1)} collective-permute-done((f32[8,2048]{1,0:T(8,128)S(1)}, f32[8,2048]{1,0:T(8,128)S(1)}, u32[]{:S(2)}, u32[]{:S(2)}) %collective-permute-start.5) | collective-permute-done | bytes 65568 | tf_op jit(solution)/shard_map/ppermute | solution.py:400
  52.8 2.0 %collective-permute-start.6 = (f32[8,2048]{1,0:T(8,128)S(1)}, f32[8,2048]{1,0:T(8,128)S(1)}, u32[]{:S(2)}, u32[]{:S(2)}) collective-permute-start(f32[8,2048]{1,0:T(8,128)S(1)} %collective-permute-done.5.refs_7_), channel_id=1, source_target_pairs={{0,1},{1,0},{2,3},{3,2},{4,5},{5,4},{6,7},{7,6},{8,9},{9,8},{10,11... | collective-permute-start | bytes 196616 | tf_op jit(solution)/shard_map/ppermute | solution.py:404
  54.8 1.6 %rows_of.1 = (bf16[4096,128]{1,0:T(8,128)(2,1)S(1)}, bf16[4096,128]{1,0:T(8,128)(2,1)S(1)}, bf16[2048,128]{1,0:T(8,128)(2,1)S(1)}, bf16[2048,128]{1,0:T(8,128)(2,1)S(1)}, bf16[96,2048]{1,0:T(8,128)(2,1)S(1)}) custom-call(bf16[16,32,384]{2,1,0:T(8,128)(2,1)S(1)} %get-tuple-element.36.refs_0_.qa_ref, ...), custom_call_target="tpu_custom_call" | custom-call | tf_op jit(solution)/shard_map/rows_of/pallas_call | solution.py:233
  56.4 23.7 %grads.1 = (bf16[16,32,384]{2,1,0:T(8,128)(2,1)S(1)}, bf16[16,32,384]{2,1,0:T(8,128)(2,1)S(1)}, bf16[16,32,384]{2,1,0:T(8,128)(2,1)S(1)}, bf16[16,32,384]{2,1,0:T(8,128)(2,1)S(1)}) custom-call(bf16[4096,128]{1,0:T(8,128)(2,1)S(1)} %get-tuple-element.19.refs_0_, bf16[4096,128]{1,0:T(8,128)(2,1)S(1)} %get-tuple-element.20.refs_1_, ...), custom_call_target="tpu_custom_call" | custom-call | flops 21474836480 | bytes 8388608 | tf_op jit(solution)/shard_map/grads/pallas_call | solution.py:317
  80.1 0.1 collective-permute-start.8
  80.2 2.6 %collective-permute-start.7 = (bf16[16,32,384]{2,1,0:T(8,128)(2,1)S(1)}, bf16[16,32,384]{2,1,0:T(8,128)(2,1)S(1)}, u32[]{:S(2)}, u32[]{:S(2)}) collective-permute-start(bf16[16,32,384]{2,1,0:T(8,128)(2,1)S(1)} %get-tuple-element.30), channel_id=1, source_target_pairs={{0,96},{96,0},{32,64},{64,32},{1,97},{97,1},{33,65},{65,33},{2,98}... | collective-permute-start | bytes 1179656 | tf_op jit(solution)/shard_map/ppermute | solution.py:396
  82.8 0.1 meet.1
  82.9 0.1 collective-permute-start.9
  83.0 8.7 %collective-permute-done.7.refs_1_ = bf16[16,32,384]{2,1,0:T(8,128)(2,1)S(1)} collective-permute-done((bf16[16,32,384]{2,1,0:T(8,128)(2,1)S(1)}, bf16[16,32,384]{2,1,0:T(8,128)(2,1)S(1)}, u32[]{:S(2)}, u32[]{:S(2)}) %collective-permute-start.7) | collective-permute-done | bytes 393248 | tf_op jit(solution)/shard_map/ppermute | solution.py:396
  91.7 0.1 combine.1
  91.9 14.4 %all_to_all.11.got_ref = bf16[16,48,384]{2,1,0:T(8,128)(2,1)S(1)} all-to-all(bf16[16,48,384]{2,1,0:T(8,128)(2,1)S(1)} %combine.1), channel_id=1, replica_groups=mesh['blk_0'=4,'blk_1'=2,'grp_0'=2,'grp_1'=4,'grp_2'=2] {'blk_1','grp_0'..., dimensions={0} | all-to-all | bytes 1179648 | tf_op jit(solution)/shard_map/all_to_all | solution.py:408
  106.3 1.2 %finish.1 = (bf16[64,1536]{1,0:T(8,128)(2,1)}, bf16[64,1536]{1,0:T(8,128)(2,1)}, bf16[64,1536]{1,0:T(8,128)(2,1)}) custom-call(bf16[16,48,384]{2,1,0:T(8,128)(2,1)S(1)} %all_to_all.11.got_ref), custom_call_target="tpu_custom_call" | custom-call | tf_op jit(solution)/shard_map/finish/pallas_call | solution.py:385
  (8 shorter events, 0.2 us)
Async XLA Ops:
  25.1 9.3 %collective-permute-start.1 = (bf16[16,32,384]{2,1,0:T(8,128)(2,1)S(1)}, bf16[16,32,384]{2,1,0:T(8,128)(2,1)S(1)}, u32[]{:S(2)}, u32[]{:S(2)}) collective-permute-start(bf16[16,32,384]{2,1,0:T(8,128)(2,1)S(1)} %get-tuple-element.36.refs_0_.qa_ref), channel_id=1, source_target_pairs={{0,32},{32,0},{64,96},{96,64},{1,33},{33,1},{65,97},{97,65},{2,34}... | collective-permute-start | bytes 1179656 | tf_op jit(solution)/shard_map/ppermute | solution.py:400
  26.8 10.1 %collective-permute-start = (bf16[16,32,384]{2,1,0:T(8,128)(2,1)S(1)}, bf16[16,32,384]{2,1,0:T(8,128)(2,1)S(1)}, u32[]{:S(2)}, u32[]{:S(2)}) collective-permute-start(bf16[16,32,384]{2,1,0:T(8,128)(2,1)S(1)} %get-tuple-element.36.refs_0_.qa_ref), channel_id=1, source_target_pairs={{0,1},{1,0},{2,3},{3,2},{4,5},{5,4},{6,7},{7,6},{8,9},{9,8},{10,11... | collective-permute-start | bytes 1179656 | tf_op jit(solution)/shard_map/ppermute | solution.py:404
  28.9 11.9 %collective-permute-start.3 = (bf16[16,32,384]{2,1,0:T(8,128)(2,1)S(1)}, bf16[16,32,384]{2,1,0:T(8,128)(2,1)S(1)}, u32[]{:S(2)}, u32[]{:S(2)}) collective-permute-start(bf16[16,32,384]{2,1,0:T(8,128)(2,1)S(1)} %get-tuple-element.35.refs_4_.kv_ref), channel_id=1, source_target_pairs={{0,96},{96,0},{32,64},{64,32},{1,97},{97,1},{33,65},{65,33},{2,98}... | collective-permute-start | bytes 1179656 | tf_op jit(solution)/shard_map/ppermute | solution.py:396
  34.5 6.3 %collective-permute-start.2 = (bf16[16,32,384]{2,1,0:T(8,128)(2,1)S(1)}, bf16[16,32,384]{2,1,0:T(8,128)(2,1)S(1)}, u32[]{:S(2)}, u32[]{:S(2)}) collective-permute-start(bf16[16,32,384]{2,1,0:T(8,128)(2,1)S(1)} %collective-permute-done.1.refs_2_.qa_ref), channel_id=1, source_target_pairs={{0,1},{1,0},{2,3},{3,2},{4,5},{5,4},{6,7},{7,6},{8,9},{9,8},{10,11... | collective-permute-start | bytes 1179656 | tf_op jit(solution)/shard_map/ppermute | solution.py:404
  49.6 3.2 %collective-permute-start.5 = (f32[8,2048]{1,0:T(8,128)S(1)}, f32[8,2048]{1,0:T(8,128)S(1)}, u32[]{:S(2)}, u32[]{:S(2)}) collective-permute-start(f32[8,2048]{1,0:T(8,128)S(1)} %stats.1.refs_5_), channel_id=1, source_target_pairs={{0,32},{32,0},{64,96},{96,64},{1,33},{33,1},{65,97},{97,65},{2,34}... | collective-permute-start | bytes 196616 | tf_op jit(solution)/shard_map/ppermute | solution.py:400
  50.7 5.7 %collective-permute-start.4 = (f32[8,2048]{1,0:T(8,128)S(1)}, f32[8,2048]{1,0:T(8,128)S(1)}, u32[]{:S(2)}, u32[]{:S(2)}) collective-permute-start(f32[8,2048]{1,0:T(8,128)S(1)} %stats.1.refs_5_), channel_id=1, source_target_pairs={{0,1},{1,0},{2,3},{3,2},{4,5},{5,4},{6,7},{7,6},{8,9},{9,8},{10,11... | collective-permute-start | bytes 196616 | tf_op jit(solution)/shard_map/ppermute | solution.py:404
  52.8 3.7 %collective-permute-start.6 = (f32[8,2048]{1,0:T(8,128)S(1)}, f32[8,2048]{1,0:T(8,128)S(1)}, u32[]{:S(2)}, u32[]{:S(2)}) collective-permute-start(f32[8,2048]{1,0:T(8,128)S(1)} %collective-permute-done.5.refs_7_), channel_id=1, source_target_pairs={{0,1},{1,0},{2,3},{3,2},{4,5},{5,4},{6,7},{7,6},{8,9},{9,8},{10,11... | collective-permute-start | bytes 196616 | tf_op jit(solution)/shard_map/ppermute | solution.py:404
  80.1 2.7 %collective-permute-start.8 = (bf16[16,32,384]{2,1,0:T(8,128)(2,1)S(1)}, bf16[16,32,384]{2,1,0:T(8,128)(2,1)S(1)}, u32[]{:S(2)}, u32[]{:S(2)}) collective-permute-start(bf16[16,32,384]{2,1,0:T(8,128)(2,1)S(1)} %get-tuple-element.32), channel_id=1, source_target_pairs={{0,1},{1,0},{2,3},{3,2},{4,5},{5,4},{6,7},{7,6},{8,9},{9,8},{10,11... | collective-permute-start | bytes 1179656 | tf_op jit(solution)/shard_map/ppermute | solution.py:404
  80.2 11.5 %collective-permute-start.7 = (bf16[16,32,384]{2,1,0:T(8,128)(2,1)S(1)}, bf16[16,32,384]{2,1,0:T(8,128)(2,1)S(1)}, u32[]{:S(2)}, u32[]{:S(2)}) collective-permute-start(bf16[16,32,384]{2,1,0:T(8,128)(2,1)S(1)} %get-tuple-element.30), channel_id=1, source_target_pairs={{0,96},{96,0},{32,64},{64,32},{1,97},{97,1},{33,65},{65,33},{2,98}... | collective-permute-start | bytes 1179656 | tf_op jit(solution)/shard_map/ppermute | solution.py:396
  82.9 8.8 %collective-permute-start.9 = (bf16[16,16,384]{2,1,0:T(8,128)(2,1)S(1)}, bf16[16,16,384]{2,1,0:T(8,128)(2,1)S(1)}, u32[]{:S(2)}, u32[]{:S(2)}) collective-permute-start(bf16[16,16,384]{2,1,0:T(8,128)(2,1)S(1)} %get-tuple-element.34), channel_id=1, source_target_pairs={{0,32},{32,0},{64,96},{96,64},{1,33},{33,1},{65,97},{97,65},{2,34}... | collective-permute-start | bytes 589832 | tf_op jit(solution)/shard_map/ppermute | solution.py:400

commit v8 on v7

--- a/solution.py
+++ b/solution.py
@@ -26,9 +26,7 @@
 CORE = "grp_2"
 SCALE = 1.0 / math.sqrt(HD)
 C2 = SCALE * math.log2(math.e)
-TQ = 1024
 TK = 512
-GUN = 4
 SUB = 64
 NEG = -1e30
 F32 = jnp.float32
@@ -255,94 +253,100 @@
     return top * C2 + jnp.log2(total), weighted / total
 
 
-def grads_kernel(*refs):
+def grads_kernel(key_block, blocks, takes_dq, takes_dkv, gives_dq, gives_dkv, *refs):
+    refs = list(refs)
     q_s, g_s, k_s, v_s, t_s = refs[:5]
-    st_refs, dkv_refs, dq_refs = refs[5 : 5 + N_Z], refs[5 + N_Z : 7 + N_Z], refs[7 + N_Z : 9 + N_Z]
-    dq_s, dk_s, dv_s, log_s, mean_s = refs[9 + N_Z :]
-    for n in range(N_Z):
+    st_refs, refs = refs[5 : 5 + N_Z], refs[5 + N_Z :]
+    dq_in = refs.pop(0) if takes_dq else None
+    dk_in, dv_in = (refs.pop(0), refs.pop(0)) if takes_dkv else (None, None)
+    dq_outs = [refs.pop(0) for _ in (range(1) if gives_dq else blocks)]
+    dkv_outs = [refs.pop(0) for _ in range(1 if gives_dkv else 2)]
+    dq_s, dk_s, dv_s, log_s, mean_s = refs
+    if gives_dq:
+        dq_s = dq_outs[0]
+    if not gives_dkv:
+        dk_s, dv_s = dkv_outs
+    for i, n in enumerate(blocks):
         log_now, mean_now = joined([block_of(st, n ^ t) for t, st in enumerate(st_refs)])
-        here = slice(n * ROWS, (n + 1) * ROWS)
+        here = slice(i * ROWS, (i + 1) * ROWS)
         log_s[:, here] = jnp.broadcast_to(log_now, (8, ROWS))
         mean_s[:, here] = jnp.broadcast_to(mean_now, (8, ROWS))
-    dq_s[...] = jnp.zeros_like(dq_s)
+        dq_s[:, here] = dq_in[:, n * ROWS : (n + 1) * ROWS] if takes_dq else jnp.zeros((HD, ROWS), F32)
 
     def one_chunk(j, _):
-        k0 = pl.multiple_of(j * TK, TK)
+        j0 = pl.multiple_of(j * TK, TK)
+        k0 = pl.multiple_of(key_block * ROWS + j * TK, TK)
         kc = k_s[pl.ds(k0, TK), :]
         vc = v_s[pl.ds(k0, TK), :]
         kt = t_s[:, pl.ds(k0, TK)]
-
-        def one_tile(t, carry):
-            dk, dv = carry
-            q0 = pl.multiple_of(t * TQ, TQ)
-            qt = q_s[pl.ds(q0, TQ), :]
-            gt = g_s[pl.ds(q0, TQ), :]
-            s = mm(kc, qt, CONTRACT_LAST).reshape(TK // 8, 8, TQ)
-            d = mm(vc, gt, CONTRACT_LAST).reshape(TK // 8, 8, TQ)
-            p = jnp.exp2(s * C2 - log_s[:, pl.ds(q0, TQ)][None])
-            sg = ((d - mean_s[:, pl.ds(q0, TQ)][None]) * (p * SCALE)).astype(BF16).reshape(TK, TQ)
-            p = p.astype(BF16).reshape(TK, TQ)
-            dq_s[:, pl.ds(q0, TQ)] += mm(kt, sg)
-            return dk + mm(sg, qt), dv + mm(p, gt)
-
-        zero = jnp.zeros((TK, 128), F32)
-        dk, dv = lax.fori_loop(0, NQ // TQ, one_tile, (zero, zero), unroll=GUN)
-        dk_s[pl.ds(k0, TK), :] = dk.astype(BF16)
-        dv_s[pl.ds(k0, TK), :] = dv.astype(BF16)
+        if takes_dkv:
+            dk, dv = dk_in[pl.ds(j0, TK), :], dv_in[pl.ds(j0, TK), :]
+        else:
+            dk = dv = jnp.zeros((TK, 128), F32)
+        for i, n in enumerate(blocks):
+            here = slice(i * ROWS, (i + 1) * ROWS)
+            qt = q_s[n * ROWS : (n + 1) * ROWS, :]
+            gt = g_s[n * ROWS : (n + 1) * ROWS, :]
+            s = mm(kc, qt, CONTRACT_LAST).reshape(TK // 8, 8, ROWS)
+            d = mm(vc, gt, CONTRACT_LAST).reshape(TK // 8, 8, ROWS)
+            p = jnp.exp2(s * C2 - log_s[:, here][None])
+            sg = ((d - mean_s[:, here][None]) * (p * SCALE)).astype(BF16).reshape(TK, ROWS)
+            p = p.astype(BF16).reshape(TK, ROWS)
+            dq_s[:, here] += mm(kt, sg)
+            dk, dv = dk + mm(sg, qt), dv + mm(p, gt)
+        dk_s[pl.ds(j0, TK), :] = dk.astype(dk_s.dtype)
+        dv_s[pl.ds(j0, TK), :] = dv.astype(dv_s.dtype)
         return 0
 
-    lax.fori_loop(0, NK // TK, one_chunk, 0)
+    lax.fori_loop(0, ROWS // TK, one_chunk, 0, unroll=len(blocks) == 1)
     place4 = [shift(HD, cols, 0, dst) for _, cols, dst in WINDOWS]
     half = ROWS // 2
-    for n, ref in enumerate(dkv_refs):
-        base = n * ROWS
-        parts = [
-            mm((dk_s, dv_s)[i % 2][base + i // 2 * half : base + (i // 2 + 1) * half, :HD], place4[i]) for i in range(4)
-        ]
+    if gives_dkv:
+        parts = [mm((dk_s, dv_s)[i % 2][i // 2 * half : (i // 2 + 1) * half, :HD], place4[i]) for i in range(4)]
         for k, piece in enumerate(pack_four(parts)):
-            ref[:, :, k * 128 : (k + 1) * 128] = piece.reshape(N_G, HALF, 128)
-    for n in range(N_Z):
-        ref, row = dq_refs[n % 2], n // 2 * PENCIL
-        parts = []
-        for quarter in range(4):
-            r0 = n * ROWS + quarter // 2 * half
-            x = mm(dq_s[:, r0 : r0 + half].astype(BF16), place4[quarter], CONTRACT_FIRST)
-            x = x.reshape(N_G, 2, PENCIL, x.shape[1])[:, quarter % 2]
-            parts.append(x.reshape(N_G * PENCIL, x.shape[2]))
-        for k, piece in enumerate(pack_four(parts)):
-            ref[:, row : row + PENCIL, k * 128 : (k + 1) * 128] = piece.reshape(N_G, PENCIL, 128)
-
-
-def grads(rows, statistics):
-    return pl.pallas_call(
-        grads_kernel,
-        out_shape=[pltpu.VMEM((N_G, HALF, WIDE), BF16)] * 4,
-        in_specs=[VMEM] * (5 + N_Z),
-        out_specs=[VMEM] * 4,
-        scratch_shapes=[pltpu.VMEM((HD, NQ), F32)]
-        + [pltpu.VMEM((NK, 128), BF16)] * 2
-        + [pltpu.VMEM((8, NQ), F32)] * 2,
-        cost_estimate=pl.CostEstimate(flops=10 * NQ * NK * 256, transcendentals=NQ * NK, bytes_accessed=8 << 20),
+            dkv_outs[0][:, :, k * 128 : (k + 1) * 128] = piece.reshape(N_G, HALF, 128)
+    if not gives_dq:
+        for i, ref in enumerate(dq_outs):
+            parts = []
+            for quarter in range(4):
+                r0 = i * ROWS + quarter // 2 * half
+                x = mm(dq_s[:, r0 : r0 + half].astype(BF16), place4[quarter], CONTRACT_FIRST)
+                x = x.reshape(N_G, 2, PENCIL, x.shape[1])[:, quarter % 2]
+                parts.append(x.reshape(N_G * PENCIL, x.shape[2]))
+            for k, piece in enumerate(pack_four(parts)):
+                ref[:, :, k * 128 : (k + 1) * 128] = piece.reshape(N_G, PENCIL, 128)
+
+
+def grads(key_block, blocks, rows, statistics, dq=None, dkv=None, gives_dq=False, gives_dkv=True):
+    taken = [*(() if dq is None else (dq,)), *(() if dkv is None else dkv)]
+    size = len(blocks) * ROWS
+    dq_out = [pltpu.VMEM((HD, size), F32)] if gives_dq else [pltpu.VMEM((N_G, PENCIL, WIDE), BF16)] * len(blocks)
+    dkv_out = [pltpu.VMEM((N_G, HALF, WIDE), BF16)] if gives_dkv else [pltpu.VMEM((ROWS, 128), F32)] * 2
+    return pl.pallas_call(
+        functools.partial(grads_kernel, key_block, blocks, dq is not None, dkv is not None, gives_dq, gives_dkv),
+        out_shape=dq_out + dkv_out,
+        in_specs=[VMEM] * (5 + N_Z + len(taken)),
+        out_specs=[VMEM] * len(dq_out + dkv_out),
+        scratch_shapes=[pltpu.VMEM((8, 128) if gives_dq else (HD, size), F32)]
+        + [pltpu.VMEM((ROWS, 128), BF16)] * 2
+        + [pltpu.VMEM((8, size), F32)] * 2,
+        cost_estimate=pl.CostEstimate(
+            flops=10 * size * ROWS * 256, transcendentals=size * ROWS, bytes_accessed=1 << 20
+        ),
         compiler_params=pltpu.CompilerParams(vmem_limit_bytes=40 << 20),
-        name="grads",
-    )(*here(*rows, *statistics))
-
-
-def meet_kernel(mine_ref, theirs_ref, keep_ref, send_ref):
-    total = mine_ref[...].astype(F32) + theirs_ref[...].astype(F32)
-    keep_ref[...] = total[:, :PENCIL]
-    send_ref[...] = total[:, PENCIL:].astype(BF16)
+    )(*here(*rows, *statistics, *taken))
+
+
+def meet_kernel(mine_ref, theirs_ref, send_ref):
+    send_ref[...] = (mine_ref[...].astype(F32) + theirs_ref[...].astype(F32)).astype(BF16)
 
 
 def meet(mine, theirs):
     return pl.pallas_call(
         meet_kernel,
-        out_shape=(
-            pltpu.VMEM((N_G, PENCIL, WIDE), F32),
-            pltpu.VMEM((N_G, PENCIL, WIDE), BF16),
-        ),
+        out_shape=pltpu.VMEM((N_G, PENCIL, WIDE), BF16),
         in_specs=[VMEM, VMEM],
-        out_specs=(VMEM, VMEM),
+        out_specs=VMEM,
         compiler_params=pltpu.CompilerParams(vmem_limit_bytes=16 << 20),
         name="meet",
     )(*here(mine, theirs))
@@ -352,8 +356,10 @@
     out_ref = refs[-1]
     row = 0
     for parts in (refs[:2], refs[2:-1]):
-        total = (parts[0][...].astype(F32) + parts[1][...].astype(F32)).astype(BF16)
-        out_ref[:, row : row + total.shape[1], :] = total
+        total = parts[0][...].astype(F32)
+        for part in parts[1:]:
+            total = total + part[...].astype(F32)
+        out_ref[:, row : row + total.shape[1], :] = total.astype(BF16)
         row += total.shape[1]
 
 
@@ -424,12 +430,14 @@
     third = over_b(statistics[0])
     statistics += [over_core(statistics[0]), third, over_core(third)]
     rows = rows_of(queries, keys)
-    keys_here, keys_there, queries_here, queries_there = grads(rows, statistics)
+    dq, keys_there = grads(1, (0, 1, 2, 3), rows, statistics, gives_dq=True)
     keys_got = over_a(keys_there)
-    queries_got = over_core(queries_there)
-    keep, send = meet(queries_here, queries_got)
-    queries_got = over_b(send)
-    total = combine([keys_here, keys_got, keep, queries_got])
+    core, beside, both, *dkv = grads(0, (1, 2, 3), rows, statistics, dq, gives_dkv=False)
+    core_got, both_got = over_core(core), over_core(both)
+    send = meet(beside, both_got)
+    beside_got = over_b(send)
+    own, keys_here = grads(0, (0,), rows, statistics, dq, dkv)
+    total = combine([keys_here, keys_got, own, core_got, beside_got])
     total = to_heads(total)
     return tuple(finish(total))
 

time: 108 us -> 106 us (0.981)
  waiting for transfers between devices: 14.1 us -> 10.7 us
    ppermute x2, waiting for transfers between devices: 9.14 us -> 5.73 us  [over_a(): return lax.ppermute(x, Z, ((0, 3), (3, 0), (1, 2), (2, 1)))]
    ppermute x5 -> x6, starting transfers between devices: 7.01 us -> 7.48 us  [over_core(): return lax.ppermute(x, CORE, ((0, 1), (1, 0)))]
    pallas_call x2 -> x4, Pallas kernels: 23.7 us -> 24.2 us  [the longest x3 24.1 us: grads(): pl.pallas_call(functools.partial(grads_kernel, key_block, blocks, dq is n...]
  transfers between devices with their start and end apart: 10 -> 11, of which waited for: 4 -> 4; matrix products, arithmetic and copies ran while one was open for 0% -> 0% of each run, Pallas kernels for 5% -> 8%
where the time goes in v8:
time: 106 us; the launch traced here: 105 us
  Pallas kernels  42.7 us (40%)
  blocking collectives  35.5 us (33%)
  starting transfers between devices  15.5 us (15%)
  waiting for transfers between devices  10.7 us (10%)
    all_to_all x2, blocking collectives, to_heads(): return lax.all_to_all(x, HEADS, 0, 0, tiled=True)  35.5 us
    pallas_call x3, Pallas kernels, grads(): pl.pallas_call(functools.partial(grads_kernel, key_block, blocks, dq is n...  24.1 us
    pallas_call x1, Pallas kernels, stats(): pl.pallas_call(stats_kernel, out_shape=pltpu.VMEM((8, NQ // 2), F32), in_...  8.78 us
    ppermute x6, starting transfers between devices, over_core(): return lax.ppermute(x, CORE, ((0, 1), (1, 0)))  7.48 us
    ppermute x2, waiting for transfers between devices, over_a(): return lax.ppermute(x, Z, ((0, 3), (3, 0), (1, 2), (2, 1)))  5.73 us
    ppermute x2, starting transfers between devices, over_a(): return lax.ppermute(x, Z, ((0, 3), (3, 0), (1, 2), (2, 1)))  5.08 us
    ppermute x3, waiting for transfers between devices, over_b(): return lax.ppermute(x, Z, ((0, 1), (1, 0), (2, 3), (3, 2)))  4.99 us
    pallas_call x1, Pallas kernels, first_stats(): pl.pallas_call(first_stats_kernel, out_shape=[pltpu.VMEM((8, NQ // 2), F3...  3.43 us
  transfers between devices with their start and end apart: 11, of which 4 were waited for; matrix products, arithmetic and copies ran while one was open for 0% of the time, Pallas kernels for 8%

profile of v8, /device:TPU:1, one launch (start us, length us, event | category | flops | bytes accessed | tf_op | source)
XLA Modules:
  0.0 105.4 jit_solution(4314556661326059950)
XLA Ops:
  0.7 3.4 %pack.1 = bf16[16,64,384]{2,1,0:T(8,128)(2,1)S(1)} custom-call(s32[512]{0:T(512)} %order_ref.1, s32[2]{0:T(128)S(1)} %pad_add_fusion.place_ref, bf16[64,1536]{1,0:T(8,128)(2,1)} %q_ref.1, bf16[64,1536]{1,0:T(8,128)(2,1)} %g_ref.1, bf16[512,1536]{1,0:T(8,128)(2,1)} %k_ref.1, bf16[512,1536]{1,0:T(8,128)(2,1)} %v_ref.1), custom_call_target="tpu_custom_call" | custom-call | tf_op jit(solution)/shard_map/pack/pallas_call | solution.py:108
  4.1 20.9 %all_to_all.10 = bf16[16,64,384]{2,1,0:T(8,128)(2,1)S(1)} all-to-all(bf16[16,64,384]{2,1,0:T(8,128)(2,1)S(1)} %pack.1), channel_id=1, replica_groups=mesh['blk_0'=4,'blk_1'=2,'grp_0'=2,'grp_1'=4,'grp_2'=2] {'blk_1','grp_0'..., dimensions={0} | all-to-all | bytes 1572864 | tf_op jit(solution)/shard_map/all_to_all | solution.py:414
  25.1 1.7 %collective-permute-start.1 = (bf16[16,32,384]{2,1,0:T(8,128)(2,1)S(1)}, bf16[16,32,384]{2,1,0:T(8,128)(2,1)S(1)}, u32[]{:S(2)}, u32[]{:S(2)}) collective-permute-start(bf16[16,32,384]{2,1,0:T(8,128)(2,1)S(1)} %get-tuple-element.42.refs_0_.qa_ref), channel_id=1, source_target_pairs={{0,32},{32,0},{64,96},{96,64},{1,33},{33,1},{65,97},{97,65},{2,34}... | collective-permute-start | bytes 1179656 | tf_op jit(solution)/shard_map/ppermute | solution.py:406
  26.8 2.1 %collective-permute-start = (bf16[16,32,384]{2,1,0:T(8,128)(2,1)S(1)}, bf16[16,32,384]{2,1,0:T(8,128)(2,1)S(1)}, u32[]{:S(2)}, u32[]{:S(2)}) collective-permute-start(bf16[16,32,384]{2,1,0:T(8,128)(2,1)S(1)} %get-tuple-element.42.refs_0_.qa_ref), channel_id=1, source_target_pairs={{0,1},{1,0},{2,3},{3,2},{4,5},{5,4},{6,7},{7,6},{8,9},{9,8},{10,11... | collective-permute-start | bytes 1179656 | tf_op jit(solution)/shard_map/ppermute | solution.py:410
  28.9 2.2 %collective-permute-start.3 = (bf16[16,32,384]{2,1,0:T(8,128)(2,1)S(1)}, bf16[16,32,384]{2,1,0:T(8,128)(2,1)S(1)}, u32[]{:S(2)}, u32[]{:S(2)}) collective-permute-start(bf16[16,32,384]{2,1,0:T(8,128)(2,1)S(1)} %get-tuple-element.41.refs_4_.kv_ref), channel_id=1, source_target_pairs={{0,96},{96,0},{32,64},{64,32},{1,97},{97,1},{33,65},{65,33},{2,98}... | collective-permute-start | bytes 1179656 | tf_op jit(solution)/shard_map/ppermute | solution.py:402
  31.1 3.3 %collective-permute-done.1.refs_2_.qa_ref = bf16[16,32,384]{2,1,0:T(8,128)(2,1)S(1)} collective-permute-done((bf16[16,32,384]{2,1,0:T(8,128)(2,1)S(1)}, bf16[16,32,384]{2,1,0:T(8,128)(2,1)S(1)}, u32[]{:S(2)}, u32[]{:S(2)}) %collective-permute-start.1) | collective-permute-done | bytes 393248 | tf_op jit(solution)/shard_map/ppermute | solution.py:406
  34.4 2.5 %collective-permute-start.2 = (bf16[16,32,384]{2,1,0:T(8,128)(2,1)S(1)}, bf16[16,32,384]{2,1,0:T(8,128)(2,1)S(1)}, u32[]{:S(2)}, u32[]{:S(2)}) collective-permute-start(bf16[16,32,384]{2,1,0:T(8,128)(2,1)S(1)} %collective-permute-done.1.refs_2_.qa_ref), channel_id=1, source_target_pairs={{0,1},{1,0},{2,3},{3,2},{4,5},{5,4},{6,7},{7,6},{8,9},{9,8},{10,11... | collective-permute-start | bytes 1179656 | tf_op jit(solution)/shard_map/ppermute | solution.py:410
  36.9 3.4 %first_stats.1 = (f32[8,2048]{1,0:T(8,128)S(1)}, bf16[128,2048]{1,0:T(8,128)(2,1)S(1)}, bf16[128,2048]{1,0:T(8,128)(2,1)S(1)}, bf16[1024,128]{1,0:T(8,128)(2,1)S(1)}, bf16[1024,128]{1,0:T(8,128)(2,1)S(1)}) custom-call(bf16[16,32,384]{2,1,0:T(8,128)(2,1)S(1)} %get-tuple-element.42.refs_0_.qa_ref, ...), custom_call_target="tpu_custom_call" | custom-call | flops 2147483648 | bytes 2097152 | tf_op jit(solution)/shard_map/first_stats/pallas_call | solution.py:173
  40.3 0.4 collective-permute-done.3.refs_5_.kv_ref
  40.8 8.8 %stats.1.refs_5_ = f32[8,2048]{1,0:T(8,128)S(1)} custom-call(bf16[16,32,384]{2,1,0:T(8,128)(2,1)S(1)} %collective-permute-done.1.refs_2_.qa_ref, bf16[16,32,384]{2,1,0:T(8,128)(2,1)S(1)} %collective-permute-done.2.refs_3_.qb_ref, bf16[16,32,384]{2,1,0:T(8,128)(2,1)S(1)} %collective-permute-done.3.refs_5_.kv_ref, f32[8,2048]{1,0:T(8,128)S(1)} %get-tuple-element.27.part_ref, ...), custom_call_target="tpu_custom_call" | custom-call | flops 6442450944 | bytes 4194304 | tf_op jit(solution)/shard_map/stats/pallas_call | solution.py:208
  49.6 1.1 %collective-permute-start.5 = (f32[8,2048]{1,0:T(8,128)S(1)}, f32[8,2048]{1,0:T(8,128)S(1)}, u32[]{:S(2)}, u32[]{:S(2)}) collective-permute-start(f32[8,2048]{1,0:T(8,128)S(1)} %stats.1.refs_5_), channel_id=1, source_target_pairs={{0,32},{32,0},{64,96},{96,64},{1,33},{33,1},{65,97},{97,65},{2,34}... | collective-permute-start | bytes 196616 | tf_op jit(solution)/shard_map/ppermute | solution.py:406
  50.7 0.4 collective-permute-start.4
  51.1 1.7 %collective-permute-done.5.refs_7_ = f32[8,2048]{1,0:T(8,128)S(1)} collective-permute-done((f32[8,2048]{1,0:T(8,128)S(1)}, f32[8,2048]{1,0:T(8,128)S(1)}, u32[]{:S(2)}, u32[]{:S(2)}) %collective-permute-start.5) | collective-permute-done | bytes 65568 | tf_op jit(solution)/shard_map/ppermute | solution.py:406
  52.8 2.0 %collective-permute-start.6 = (f32[8,2048]{1,0:T(8,128)S(1)}, f32[8,2048]{1,0:T(8,128)S(1)}, u32[]{:S(2)}, u32[]{:S(2)}) collective-permute-start(f32[8,2048]{1,0:T(8,128)S(1)} %collective-permute-done.5.refs_7_), channel_id=1, source_target_pairs={{0,1},{1,0},{2,3},{3,2},{4,5},{5,4},{6,7},{7,6},{8,9},{9,8},{10,11... | collective-permute-start | bytes 196616 | tf_op jit(solution)/shard_map/ppermute | solution.py:410
  54.8 1.6 %rows_of.1 = (bf16[4096,128]{1,0:T(8,128)(2,1)S(1)}, bf16[4096,128]{1,0:T(8,128)(2,1)S(1)}, bf16[2048,128]{1,0:T(8,128)(2,1)S(1)}, bf16[2048,128]{1,0:T(8,128)(2,1)S(1)}, bf16[96,2048]{1,0:T(8,128)(2,1)S(1)}) custom-call(bf16[16,32,384]{2,1,0:T(8,128)(2,1)S(1)} %get-tuple-element.42.refs_0_.qa_ref, ...), custom_call_target="tpu_custom_call" | custom-call | tf_op jit(solution)/shard_map/rows_of/pallas_call | solution.py:231
  56.4 11.6 %shard_map.76 = (f32[96,4096]{1,0:T(8,128)S(1)}, bf16[16,32,384]{2,1,0:T(8,128)(2,1)S(1)}) custom-call(bf16[4096,128]{1,0:T(8,128)(2,1)S(1)} %get-tuple-element.22.refs_0_, bf16[4096,128]{1,0:T(8,128)(2,1)S(1)} %get-tuple-element.23.refs_1_, bf16[2048,128]{1,0:T(8,128)(2,1)S(1)} %get-tuple-element.24.refs_2_, ...), custom_call_target="tpu_custom_call" | custom-call | flops 10737418240 | bytes 1048576 | tf_op jit(solution)/shard_map/pallas_call | solution.py:325
  68.0 9.3 %shard_map.77 = (bf16[16,16,384]{2,1,0:T(8,128)(2,1)S(1)}, bf16[16,16,384]{2,1,0:T(8,128)(2,1)S(1)}, bf16[16,16,384]{2,1,0:T(8,128)(2,1)S(1)}, f32[1024,128]{1,0:T(8,128)S(1)}, f32[1024,128]{1,0:T(8,128)S(1)}) custom-call(bf16[4096,128]{1,0:T(8,128)(2,1)S(1)} %get-tuple-element.22.refs_0_, bf16[4096,128]{1,0:T(8,128)(2,1)S(1)} %get-tuple-element.23.refs_1_, ...), custom_call_target="tpu_custom_call" | custom-call | flops 8053063680 | bytes 1048576 | tf_op jit(solution)/shard_map/pallas_call | solution.py:325
  77.5 2.8 %collective-permute-start.7 = (bf16[16,32,384]{2,1,0:T(8,128)(2,1)S(1)}, bf16[16,32,384]{2,1,0:T(8,128)(2,1)S(1)}, u32[]{:S(2)}, u32[]{:S(2)}) collective-permute-start(bf16[16,32,384]{2,1,0:T(8,128)(2,1)S(1)} %get-tuple-element.36), channel_id=1, source_target_pairs={{0,96},{96,0},{32,64},{64,32},{1,97},{97,1},{33,65},{65,33},{2,98}... | collective-permute-start | bytes 1179656 | tf_op jit(solution)/shard_map/ppermute | solution.py:402
  80.3 0.5 collective-permute-start.8
  80.9 3.2 %shard_map.78 = (bf16[16,16,384]{2,1,0:T(8,128)(2,1)S(1)}, bf16[16,32,384]{2,1,0:T(8,128)(2,1)S(1)}) custom-call(bf16[4096,128]{1,0:T(8,128)(2,1)S(1)} %get-tuple-element.22.refs_0_, bf16[4096,128]{1,0:T(8,128)(2,1)S(1)} %get-tuple-element.23.refs_1_, bf16[2048,128]{1,0:T(8,128)(2,1)S(1)} %get-tuple-element.24.refs_2_, ...), custom_call_target="tpu_custom_call" | custom-call | flops 2684354560 | bytes 1048576 | tf_op jit(solution)/shard_map/pallas_call | solution.py:325
  84.1 5.3 %collective-permute-done.7.refs_1_ = bf16[16,32,384]{2,1,0:T(8,128)(2,1)S(1)} collective-permute-done((bf16[16,32,384]{2,1,0:T(8,128)(2,1)S(1)}, bf16[16,32,384]{2,1,0:T(8,128)(2,1)S(1)}, u32[]{:S(2)}, u32[]{:S(2)}) %collective-permute-start.7) | collective-permute-done | bytes 393248 | tf_op jit(solution)/shard_map/ppermute | solution.py:402
  89.4 0.2 combine.1
  89.6 14.6 %all_to_all.11.got_ref = bf16[16,48,384]{2,1,0:T(8,128)(2,1)S(1)} all-to-all(bf16[16,48,384]{2,1,0:T(8,128)(2,1)S(1)} %combine.1), channel_id=1, replica_groups=mesh['blk_0'=4,'blk_1'=2,'grp_0'=2,'grp_1'=4,'grp_2'=2] {'blk_1','grp_0'..., dimensions={0} | all-to-all | bytes 1179648 | tf_op jit(solution)/shard_map/all_to_all | solution.py:414
  104.2 1.2 %finish.1 = (bf16[64,1536]{1,0:T(8,128)(2,1)}, bf16[64,1536]{1,0:T(8,128)(2,1)}, bf16[64,1536]{1,0:T(8,128)(2,1)}) custom-call(bf16[16,48,384]{2,1,0:T(8,128)(2,1)S(1)} %all_to_all.11.got_ref), custom_call_target="tpu_custom_call" | custom-call | tf_op jit(solution)/shard_map/finish/pallas_call | solution.py:391
  (12 shorter events, 0.4 us)
Async XLA Ops:
  25.1 9.3 %collective-permute-start.1 = (bf16[16,32,384]{2,1,0:T(8,128)(2,1)S(1)}, bf16[16,32,384]{2,1,0:T(8,128)(2,1)S(1)}, u32[]{:S(2)}, u32[]{:S(2)}) collective-permute-start(bf16[16,32,384]{2,1,0:T(8,128)(2,1)S(1)} %get-tuple-element.42.refs_0_.qa_ref), channel_id=1, source_target_pairs={{0,32},{32,0},{64,96},{96,64},{1,33},{33,1},{65,97},{97,65},{2,34}... | collective-permute-start | bytes 1179656 | tf_op jit(solution)/shard_map/ppermute | solution.py:406
  26.8 10.1 %collective-permute-start = (bf16[16,32,384]{2,1,0:T(8,128)(2,1)S(1)}, bf16[16,32,384]{2,1,0:T(8,128)(2,1)S(1)}, u32[]{:S(2)}, u32[]{:S(2)}) collective-permute-start(bf16[16,32,384]{2,1,0:T(8,128)(2,1)S(1)} %get-tuple-element.42.refs_0_.qa_ref), channel_id=1, source_target_pairs={{0,1},{1,0},{2,3},{3,2},{4,5},{5,4},{6,7},{7,6},{8,9},{9,8},{10,11... | collective-permute-start | bytes 1179656 | tf_op jit(solution)/shard_map/ppermute | solution.py:410
  28.9 11.9 %collective-permute-start.3 = (bf16[16,32,384]{2,1,0:T(8,128)(2,1)S(1)}, bf16[16,32,384]{2,1,0:T(8,128)(2,1)S(1)}, u32[]{:S(2)}, u32[]{:S(2)}) collective-permute-start(bf16[16,32,384]{2,1,0:T(8,128)(2,1)S(1)} %get-tuple-element.41.refs_4_.kv_ref), channel_id=1, source_target_pairs={{0,96},{96,0},{32,64},{64,32},{1,97},{97,1},{33,65},{65,33},{2,98}... | collective-permute-start | bytes 1179656 | tf_op jit(solution)/shard_map/ppermute | solution.py:402
  34.4 6.3 %collective-permute-start.2 = (bf16[16,32,384]{2,1,0:T(8,128)(2,1)S(1)}, bf16[16,32,384]{2,1,0:T(8,128)(2,1)S(1)}, u32[]{:S(2)}, u32[]{:S(2)}) collective-permute-start(bf16[16,32,384]{2,1,0:T(8,128)(2,1)S(1)} %collective-permute-done.1.refs_2_.qa_ref), channel_id=1, source_target_pairs={{0,1},{1,0},{2,3},{3,2},{4,5},{5,4},{6,7},{7,6},{8,9},{9,8},{10,11... | collective-permute-start | bytes 1179656 | tf_op jit(solution)/shard_map/ppermute | solution.py:410
  49.6 3.2 %collective-permute-start.5 = (f32[8,2048]{1,0:T(8,128)S(1)}, f32[8,2048]{1,0:T(8,128)S(1)}, u32[]{:S(2)}, u32[]{:S(2)}) collective-permute-start(f32[8,2048]{1,0:T(8,128)S(1)} %stats.1.refs_5_), channel_id=1, source_target_pairs={{0,32},{32,0},{64,96},{96,64},{1,33},{33,1},{65,97},{97,65},{2,34}... | collective-permute-start | bytes 196616 | tf_op jit(solution)/shard_map/ppermute | solution.py:406
  50.7 5.7 %collective-permute-start.4 = (f32[8,2048]{1,0:T(8,128)S(1)}, f32[8,2048]{1,0:T(8,128)S(1)}, u32[]{:S(2)}, u32[]{:S(2)}) collective-permute-start(f32[8,2048]{1,0:T(8,128)S(1)} %stats.1.refs_5_), channel_id=1, source_target_pairs={{0,1},{1,0},{2,3},{3,2},{4,5},{5,4},{6,7},{7,6},{8,9},{9,8},{10,11... | collective-permute-start | bytes 196616 | tf_op jit(solution)/shard_map/ppermute | solution.py:410
  52.8 3.7 %collective-permute-start.6 = (f32[8,2048]{1,0:T(8,128)S(1)}, f32[8,2048]{1,0:T(8,128)S(1)}, u32[]{:S(2)}, u32[]{:S(2)}) collective-permute-start(f32[8,2048]{1,0:T(8,128)S(1)} %collective-permute-done.5.refs_7_), channel_id=1, source_target_pairs={{0,1},{1,0},{2,3},{3,2},{4,5},{5,4},{6,7},{7,6},{8,9},{9,8},{10,11... | collective-permute-start | bytes 196616 | tf_op jit(solution)/shard_map/ppermute | solution.py:410
  77.4 3.4 %collective-permute-start.9 = (bf16[16,16,384]{2,1,0:T(8,128)(2,1)S(1)}, bf16[16,16,384]{2,1,0:T(8,128)(2,1)S(1)}, u32[]{:S(2)}, u32[]{:S(2)}) collective-permute-start(bf16[16,16,384]{2,1,0:T(8,128)(2,1)S(1)} %get-tuple-element.40), channel_id=1, source_target_pairs={{0,1},{1,0},{2,3},{3,2},{4,5},{5,4},{6,7},{7,6},{8,9},{9,8},{10,11... | collective-permute-start | bytes 589832 | tf_op jit(solution)/shard_map/ppermute | solution.py:410
  77.5 12.0 %collective-permute-start.7 = (bf16[16,32,384]{2,1,0:T(8,128)(2,1)S(1)}, bf16[16,32,384]{2,1,0:T(8,128)(2,1)S(1)}, u32[]{:S(2)}, u32[]{:S(2)}) collective-permute-start(bf16[16,32,384]{2,1,0:T(8,128)(2,1)S(1)} %get-tuple-element.36), channel_id=1, source_target_pairs={{0,96},{96,0},{32,64},{64,32},{1,97},{97,1},{33,65},{65,33},{2,98}... | collective-permute-start | bytes 1179656 | tf_op jit(solution)/shard_map/ppermute | solution.py:402
  80.3 3.8 %collective-permute-start.8 = (bf16[16,16,384]{2,1,0:T(8,128)(2,1)S(1)}, bf16[16,16,384]{2,1,0:T(8,128)(2,1)S(1)}, u32[]{:S(2)}, u32[]{:S(2)}) collective-permute-start(bf16[16,16,384]{2,1,0:T(8,128)(2,1)S(1)} %get-tuple-element.38), channel_id=1, source_target_pairs={{0,1},{1,0},{2,3},{3,2},{4,5},{5,4},{6,7},{7,6},{8,9},{9,8},{10,11... | collective-permute-start | bytes 589832 | tf_op jit(solution)/shard_map/ppermute | solution.py:410
  80.8 8.6 %collective-permute-start.10 = (bf16[16,16,384]{2,1,0:T(8,128)(2,1)S(1)}, bf16[16,16,384]{2,1,0:T(8,128)(2,1)S(1)}, u32[]{:S(2)}, u32[]{:S(2)}) collective-permute-start(bf16[16,16,384]{2,1,0:T(8,128)(2,1)S(1)} %meet.1), channel_id=1, source_target_pairs={{0,32},{32,0},{64,96},{96,64},{1,33},{33,1},{65,97},{97,65},{2,34}... | collective-permute-start | bytes 589832 | tf_op jit(solution)/shard_map/ppermute | solution.py:406

commit v9 on v8

--- a/solution.py
+++ b/solution.py
@@ -410,6 +410,12 @@
     return lax.ppermute(x, CORE, ((0, 1), (1, 0)))
 
 
+def over_b_and_core(x):
+    near = (1, 0, 3, 2)
+    pairs = tuple((2 * k + c, 2 * near[k] + 1 - c) for k in range(N_Z) for c in range(2))
+    return lax.ppermute(x, (Z, CORE), pairs)
+
+
 def to_heads(x):
     return lax.all_to_all(x, HEADS, 0, 0, tiled=True)
 
@@ -427,16 +433,18 @@
     first = first_stats(queries[0], queries[1], keys[0])
     queries.append(over_core(queries[2]))
     statistics = [stats(queries[2], queries[3], keys[1], first)]
-    third = over_b(statistics[0])
-    statistics += [over_core(statistics[0]), third, over_core(third)]
+    both = over_b_and_core(statistics[0])
+    beside = over_b(statistics[0])
+    statistics += [over_core(statistics[0]), beside, both]
     rows = rows_of(queries, keys)
     dq, keys_there = grads(1, (0, 1, 2, 3), rows, statistics, gives_dq=True)
     keys_got = over_a(keys_there)
-    core, beside, both, *dkv = grads(0, (1, 2, 3), rows, statistics, dq, gives_dkv=False)
-    core_got, both_got = over_core(core), over_core(both)
+    beside, both, *dkv = grads(0, (2, 3), rows, statistics, dq, gives_dkv=False)
+    both_got = over_core(both)
     send = meet(beside, both_got)
     beside_got = over_b(send)
-    own, keys_here = grads(0, (0,), rows, statistics, dq, dkv)
+    own, core, keys_here = grads(0, (0, 1), rows, statistics, dq, dkv)
+    core_got = over_core(core)
     total = combine([keys_here, keys_got, own, core_got, beside_got])
     total = to_heads(total)
     return tuple(finish(total))

time: 106 us -> 107 us (level)
    ppermute x2, waiting for transfers between devices: 5.73 us -> 0.43 us  [over_a(): return lax.ppermute(x, Z, ((0, 3), (3, 0), (1, 2), (2, 1)))]
    ppermute x3, waiting for transfers between devices: 4.99 us -> 9 us  [over_b(): return lax.ppermute(x, Z, ((0, 1), (1, 0), (2, 3), (3, 2)))]
    ppermute x0 -> x1, waiting for transfers between devices: none -> 1.66 us  [over_b_and_core(): return lax.ppermute(x, (Z, CORE), pairs)]
    ppermute x0 -> x1, starting transfers between devices: none -> 1.42 us  [over_b_and_core(): return lax.ppermute(x, (Z, CORE), pairs)]
    ppermute x6 -> x5, starting transfers between devices: 7.48 us -> 6.23 us  [over_core(): return lax.ppermute(x, CORE, ((0, 1), (1, 0)))]
  transfers between devices with their start and end apart: 11 -> 11, of which waited for: 4 -> 6; matrix products, arithmetic and copies ran while one was open for 0% -> 0% of each run, Pallas kernels for 8% -> 11%
where the time goes in v9:
time: 107 us; the launch traced here: 106 us
  Pallas kernels  43.3 us (40%)
  blocking collectives  35.2 us (33%)
  starting transfers between devices  15.1 us (14%)
  waiting for transfers between devices  11.5 us (11%)
    all_to_all x2, blocking collectives, to_heads(): return lax.all_to_all(x, HEADS, 0, 0, tiled=True)  35.2 us
    pallas_call x3, Pallas kernels, grads(): pl.pallas_call(functools.partial(grads_kernel, key_block, blocks, dq is n...  24.6 us
    ppermute x3, waiting for transfers between devices, over_b(): return lax.ppermute(x, Z, ((0, 1), (1, 0), (2, 3), (3, 2)))  9 us
    pallas_call x1, Pallas kernels, stats(): pl.pallas_call(stats_kernel, out_shape=pltpu.VMEM((8, NQ // 2), F32), in_...  8.78 us
    ppermute x5, starting transfers between devices, over_core(): return lax.ppermute(x, CORE, ((0, 1), (1, 0)))  6.23 us
    ppermute x2, starting transfers between devices, over_a(): return lax.ppermute(x, Z, ((0, 3), (3, 0), (1, 2), (2, 1)))  4.81 us
    pallas_call x1, Pallas kernels, first_stats(): pl.pallas_call(first_stats_kernel, out_shape=[pltpu.VMEM((8, NQ // 2), F3...  3.43 us
    pallas_call x1, Pallas kernels, pack(): pl.pallas_call(pack_kernel, out_shape=jax.ShapeDtypeStruct((H, PD, WIDE),...  3.4 us
  transfers between devices with their start and end apart: 11, of which 6 were waited for; matrix products, arithmetic and copies ran while one was open for 0% of the time, Pallas kernels for 11%

profile of v9, /device:TPU:1, one launch (start us, length us, event | category | flops | bytes accessed | tf_op | source)
XLA Modules:
  0.0 106.0 jit_solution(14469286722695829655)
XLA Ops:
  0.7 3.4 %pack.1 = bf16[16,64,384]{2,1,0:T(8,128)(2,1)S(1)} custom-call(s32[512]{0:T(512)} %order_ref.1, s32[2]{0:T(128)S(1)} %pad_add_fusion.place_ref, bf16[64,1536]{1,0:T(8,128)(2,1)} %q_ref.1, bf16[64,1536]{1,0:T(8,128)(2,1)} %g_ref.1, bf16[512,1536]{1,0:T(8,128)(2,1)} %k_ref.1, bf16[512,1536]{1,0:T(8,128)(2,1)} %v_ref.1), custom_call_target="tpu_custom_call" | custom-call | tf_op jit(solution)/shard_map/pack/pallas_call | solution.py:108
  4.1 20.9 %all_to_all.10 = bf16[16,64,384]{2,1,0:T(8,128)(2,1)S(1)} all-to-all(bf16[16,64,384]{2,1,0:T(8,128)(2,1)S(1)} %pack.1), channel_id=1, replica_groups=mesh['blk_0'=4,'blk_1'=2,'grp_0'=2,'grp_1'=4,'grp_2'=2] {'blk_1','grp_0'..., dimensions={0} | all-to-all | bytes 1572864 | tf_op jit(solution)/shard_map/all_to_all | solution.py:420
  25.1 1.7 %collective-permute-start.1 = (bf16[16,32,384]{2,1,0:T(8,128)(2,1)S(1)}, bf16[16,32,384]{2,1,0:T(8,128)(2,1)S(1)}, u32[]{:S(2)}, u32[]{:S(2)}) collective-permute-start(bf16[16,32,384]{2,1,0:T(8,128)(2,1)S(1)} %get-tuple-element.42.refs_0_.qa_ref), channel_id=1, source_target_pairs={{0,32},{32,0},{64,96},{96,64},{1,33},{33,1},{65,97},{97,65},{2,34}... | collective-permute-start | bytes 1179656 | tf_op jit(solution)/shard_map/ppermute | solution.py:406
  26.8 2.1 %collective-permute-start = (bf16[16,32,384]{2,1,0:T(8,128)(2,1)S(1)}, bf16[16,32,384]{2,1,0:T(8,128)(2,1)S(1)}, u32[]{:S(2)}, u32[]{:S(2)}) collective-permute-start(bf16[16,32,384]{2,1,0:T(8,128)(2,1)S(1)} %get-tuple-element.42.refs_0_.qa_ref), channel_id=1, source_target_pairs={{0,1},{1,0},{2,3},{3,2},{4,5},{5,4},{6,7},{7,6},{8,9},{9,8},{10,11... | collective-permute-start | bytes 1179656 | tf_op jit(solution)/shard_map/ppermute | solution.py:410
  28.9 2.2 %collective-permute-start.3 = (bf16[16,32,384]{2,1,0:T(8,128)(2,1)S(1)}, bf16[16,32,384]{2,1,0:T(8,128)(2,1)S(1)}, u32[]{:S(2)}, u32[]{:S(2)}) collective-permute-start(bf16[16,32,384]{2,1,0:T(8,128)(2,1)S(1)} %get-tuple-element.41.refs_4_.kv_ref), channel_id=1, source_target_pairs={{0,96},{96,0},{32,64},{64,32},{1,97},{97,1},{33,65},{65,33},{2,98}... | collective-permute-start | bytes 1179656 | tf_op jit(solution)/shard_map/ppermute | solution.py:402
  31.1 3.3 %collective-permute-done.1.refs_2_.qa_ref = bf16[16,32,384]{2,1,0:T(8,128)(2,1)S(1)} collective-permute-done((bf16[16,32,384]{2,1,0:T(8,128)(2,1)S(1)}, bf16[16,32,384]{2,1,0:T(8,128)(2,1)S(1)}, u32[]{:S(2)}, u32[]{:S(2)}) %collective-permute-start.1) | collective-permute-done | bytes 393248 | tf_op jit(solution)/shard_map/ppermute | solution.py:406
  34.4 2.5 %collective-permute-start.2 = (bf16[16,32,384]{2,1,0:T(8,128)(2,1)S(1)}, bf16[16,32,384]{2,1,0:T(8,128)(2,1)S(1)}, u32[]{:S(2)}, u32[]{:S(2)}) collective-permute-start(bf16[16,32,384]{2,1,0:T(8,128)(2,1)S(1)} %collective-permute-done.1.refs_2_.qa_ref), channel_id=1, source_target_pairs={{0,1},{1,0},{2,3},{3,2},{4,5},{5,4},{6,7},{7,6},{8,9},{9,8},{10,11... | collective-permute-start | bytes 1179656 | tf_op jit(solution)/shard_map/ppermute | solution.py:410
  36.9 3.4 %first_stats.1 = (f32[8,2048]{1,0:T(8,128)S(1)}, bf16[128,2048]{1,0:T(8,128)(2,1)S(1)}, bf16[128,2048]{1,0:T(8,128)(2,1)S(1)}, bf16[1024,128]{1,0:T(8,128)(2,1)S(1)}, bf16[1024,128]{1,0:T(8,128)(2,1)S(1)}) custom-call(bf16[16,32,384]{2,1,0:T(8,128)(2,1)S(1)} %get-tuple-element.42.refs_0_.qa_ref, ...), custom_call_target="tpu_custom_call" | custom-call | flops 2147483648 | bytes 2097152 | tf_op jit(solution)/shard_map/first_stats/pallas_call | solution.py:173
  40.3 0.4 collective-permute-done.3.refs_5_.kv_ref
  40.8 8.8 %stats.1.refs_5_ = f32[8,2048]{1,0:T(8,128)S(1)} custom-call(bf16[16,32,384]{2,1,0:T(8,128)(2,1)S(1)} %collective-permute-done.1.refs_2_.qa_ref, bf16[16,32,384]{2,1,0:T(8,128)(2,1)S(1)} %collective-permute-done.2.refs_3_.qb_ref, bf16[16,32,384]{2,1,0:T(8,128)(2,1)S(1)} %collective-permute-done.3.refs_5_.kv_ref, f32[8,2048]{1,0:T(8,128)S(1)} %get-tuple-element.27.part_ref, ...), custom_call_target="tpu_custom_call" | custom-call | flops 6442450944 | bytes 4194304 | tf_op jit(solution)/shard_map/stats/pallas_call | solution.py:208
  49.6 0.9 collective-permute-start.4
  50.8 1.4 %collective-permute-start.6 = (f32[8,2048]{1,0:T(8,128)S(1)}, f32[8,2048]{1,0:T(8,128)S(1)}, u32[]{:S(2)}, u32[]{:S(2)}) collective-permute-start(f32[8,2048]{1,0:T(8,128)S(1)} %stats.1.refs_5_), channel_id=1, source_target_pairs={{0,33},{1,32},{32,1},{33,0},{64,97},{65,96},{96,65},{97,64},{2,35}... | collective-permute-start | bytes 196616 | tf_op jit(solution)/shard_map/ppermute | solution.py:416
  52.2 1.6 %rows_of.1 = (bf16[4096,128]{1,0:T(8,128)(2,1)S(1)}, bf16[4096,128]{1,0:T(8,128)(2,1)S(1)}, bf16[2048,128]{1,0:T(8,128)(2,1)S(1)}, bf16[2048,128]{1,0:T(8,128)(2,1)S(1)}, bf16[96,2048]{1,0:T(8,128)(2,1)S(1)}) custom-call(bf16[16,32,384]{2,1,0:T(8,128)(2,1)S(1)} %get-tuple-element.42.refs_0_.qa_ref, ...), custom_call_target="tpu_custom_call" | custom-call | tf_op jit(solution)/shard_map/rows_of/pallas_call | solution.py:231
  54.1 1.7 %collective-permute-done.6.refs_8_ = f32[8,2048]{1,0:T(8,128)S(1)} collective-permute-done((f32[8,2048]{1,0:T(8,128)S(1)}, f32[8,2048]{1,0:T(8,128)S(1)}, u32[]{:S(2)}, u32[]{:S(2)}) %collective-permute-start.6) | collective-permute-done | bytes 65568 | tf_op jit(solution)/shard_map/ppermute | solution.py:416
  55.7 11.6 %shard_map.76 = (f32[96,4096]{1,0:T(8,128)S(1)}, bf16[16,32,384]{2,1,0:T(8,128)(2,1)S(1)}) custom-call(bf16[4096,128]{1,0:T(8,128)(2,1)S(1)} %get-tuple-element.22.refs_0_, bf16[4096,128]{1,0:T(8,128)(2,1)S(1)} %get-tuple-element.23.refs_1_, bf16[2048,128]{1,0:T(8,128)(2,1)S(1)} %get-tuple-element.24.refs_2_, ...), custom_call_target="tpu_custom_call" | custom-call | flops 10737418240 | bytes 1048576 | tf_op jit(solution)/shard_map/pallas_call | solution.py:325
  67.3 6.5 %shard_map.77 = (bf16[16,16,384]{2,1,0:T(8,128)(2,1)S(1)}, bf16[16,16,384]{2,1,0:T(8,128)(2,1)S(1)}, f32[1024,128]{1,0:T(8,128)S(1)}, f32[1024,128]{1,0:T(8,128)S(1)}) custom-call(bf16[4096,128]{1,0:T(8,128)(2,1)S(1)} %get-tuple-element.22.refs_0_, bf16[4096,128]{1,0:T(8,128)(2,1)S(1)} %get-tuple-element.23.refs_1_, ...), custom_call_target="tpu_custom_call" | custom-call | flops 5368709120 | bytes 1048576 | tf_op jit(solution)/shard_map/pallas_call | solution.py:325
  74.0 2.6 %collective-permute-start.7 = (bf16[16,32,384]{2,1,0:T(8,128)(2,1)S(1)}, bf16[16,32,384]{2,1,0:T(8,128)(2,1)S(1)}, u32[]{:S(2)}, u32[]{:S(2)}) collective-permute-start(bf16[16,32,384]{2,1,0:T(8,128)(2,1)S(1)} %get-tuple-element.36), channel_id=1, source_target_pairs={{0,96},{96,0},{32,64},{64,32},{1,97},{97,1},{33,65},{65,33},{2,98}... | collective-permute-start | bytes 1179656 | tf_op jit(solution)/shard_map/ppermute | solution.py:402
  76.6 6.6 %shard_map.78 = (bf16[16,16,384]{2,1,0:T(8,128)(2,1)S(1)}, bf16[16,16,384]{2,1,0:T(8,128)(2,1)S(1)}, bf16[16,32,384]{2,1,0:T(8,128)(2,1)S(1)}) custom-call(bf16[4096,128]{1,0:T(8,128)(2,1)S(1)} %get-tuple-element.22.refs_0_, bf16[4096,128]{1,0:T(8,128)(2,1)S(1)} %get-tuple-element.23.refs_1_, bf16[2048,128]{1,0:T(8,128)(2,1)S(1)} %get-tuple-element.24.refs_2_, ...), custom_call_target="tpu_custom_call" | custom-call | flops 5368709120 | bytes 1048576 | tf_op jit(solution)/shard_map/pallas_call | solution.py:325
  83.2 0.6 collective-permute-start.8
  83.8 0.6 collective-permute-start.10
  84.4 0.4 collective-permute-done.8.refs_3_
  84.8 5.5 %collective-permute-done.10.refs_4_ = bf16[16,16,384]{2,1,0:T(8,128)(2,1)S(1)} collective-permute-done((bf16[16,16,384]{2,1,0:T(8,128)(2,1)S(1)}, bf16[16,16,384]{2,1,0:T(8,128)(2,1)S(1)}, u32[]{:S(2)}, u32[]{:S(2)}) %collective-permute-start.10) | collective-permute-done | bytes 196640 | tf_op jit(solution)/shard_map/ppermute | solution.py:406
  90.5 14.3 %all_to_all.11.got_ref = bf16[16,48,384]{2,1,0:T(8,128)(2,1)S(1)} all-to-all(bf16[16,48,384]{2,1,0:T(8,128)(2,1)S(1)} %combine.1), channel_id=1, replica_groups=mesh['blk_0'=4,'blk_1'=2,'grp_0'=2,'grp_1'=4,'grp_2'=2] {'blk_1','grp_0'..., dimensions={0} | all-to-all | bytes 1179648 | tf_op jit(solution)/shard_map/all_to_all | solution.py:420
  104.8 1.2 %finish.1 = (bf16[64,1536]{1,0:T(8,128)(2,1)}, bf16[64,1536]{1,0:T(8,128)(2,1)}, bf16[64,1536]{1,0:T(8,128)(2,1)}) custom-call(bf16[16,48,384]{2,1,0:T(8,128)(2,1)S(1)} %all_to_all.11.got_ref), custom_call_target="tpu_custom_call" | custom-call | tf_op jit(solution)/shard_map/finish/pallas_call | solution.py:391
  (12 shorter events, 1.1 us)
Async XLA Ops:
  25.1 9.3 %collective-permute-start.1 = (bf16[16,32,384]{2,1,0:T(8,128)(2,1)S(1)}, bf16[16,32,384]{2,1,0:T(8,128)(2,1)S(1)}, u32[]{:S(2)}, u32[]{:S(2)}) collective-permute-start(bf16[16,32,384]{2,1,0:T(8,128)(2,1)S(1)} %get-tuple-element.42.refs_0_.qa_ref), channel_id=1, source_target_pairs={{0,32},{32,0},{64,96},{96,64},{1,33},{33,1},{65,97},{97,65},{2,34}... | collective-permute-start | bytes 1179656 | tf_op jit(solution)/shard_map/ppermute | solution.py:406
  26.8 10.1 %collective-permute-start = (bf16[16,32,384]{2,1,0:T(8,128)(2,1)S(1)}, bf16[16,32,384]{2,1,0:T(8,128)(2,1)S(1)}, u32[]{:S(2)}, u32[]{:S(2)}) collective-permute-start(bf16[16,32,384]{2,1,0:T(8,128)(2,1)S(1)} %get-tuple-element.42.refs_0_.qa_ref), channel_id=1, source_target_pairs={{0,1},{1,0},{2,3},{3,2},{4,5},{5,4},{6,7},{7,6},{8,9},{9,8},{10,11... | collective-permute-start | bytes 1179656 | tf_op jit(solution)/shard_map/ppermute | solution.py:410
  28.9 11.9 %collective-permute-start.3 = (bf16[16,32,384]{2,1,0:T(8,128)(2,1)S(1)}, bf16[16,32,384]{2,1,0:T(8,128)(2,1)S(1)}, u32[]{:S(2)}, u32[]{:S(2)}) collective-permute-start(bf16[16,32,384]{2,1,0:T(8,128)(2,1)S(1)} %get-tuple-element.41.refs_4_.kv_ref), channel_id=1, source_target_pairs={{0,96},{96,0},{32,64},{64,32},{1,97},{97,1},{33,65},{65,33},{2,98}... | collective-permute-start | bytes 1179656 | tf_op jit(solution)/shard_map/ppermute | solution.py:402
  34.4 6.3 %collective-permute-start.2 = (bf16[16,32,384]{2,1,0:T(8,128)(2,1)S(1)}, bf16[16,32,384]{2,1,0:T(8,128)(2,1)S(1)}, u32[]{:S(2)}, u32[]{:S(2)}) collective-permute-start(bf16[16,32,384]{2,1,0:T(8,128)(2,1)S(1)} %collective-permute-done.1.refs_2_.qa_ref), channel_id=1, source_target_pairs={{0,1},{1,0},{2,3},{3,2},{4,5},{5,4},{6,7},{7,6},{8,9},{9,8},{10,11... | collective-permute-start | bytes 1179656 | tf_op jit(solution)/shard_map/ppermute | solution.py:410
  49.6 4.3 %collective-permute-start.4 = (f32[8,2048]{1,0:T(8,128)S(1)}, f32[8,2048]{1,0:T(8,128)S(1)}, u32[]{:S(2)}, u32[]{:S(2)}) collective-permute-start(f32[8,2048]{1,0:T(8,128)S(1)} %stats.1.refs_5_), channel_id=1, source_target_pairs={{0,1},{1,0},{2,3},{3,2},{4,5},{5,4},{6,7},{7,6},{8,9},{9,8},{10,11... | collective-permute-start | bytes 196616 | tf_op jit(solution)/shard_map/ppermute | solution.py:410
  50.5 3.6 %collective-permute-start.5 = (f32[8,2048]{1,0:T(8,128)S(1)}, f32[8,2048]{1,0:T(8,128)S(1)}, u32[]{:S(2)}, u32[]{:S(2)}) collective-permute-start(f32[8,2048]{1,0:T(8,128)S(1)} %stats.1.refs_5_), channel_id=1, source_target_pairs={{0,32},{32,0},{64,96},{96,64},{1,33},{33,1},{65,97},{97,65},{2,34}... | collective-permute-start | bytes 196616 | tf_op jit(solution)/shard_map/ppermute | solution.py:406
  50.8 4.9 %collective-permute-start.6 = (f32[8,2048]{1,0:T(8,128)S(1)}, f32[8,2048]{1,0:T(8,128)S(1)}, u32[]{:S(2)}, u32[]{:S(2)}) collective-permute-start(f32[8,2048]{1,0:T(8,128)S(1)} %stats.1.refs_5_), channel_id=1, source_target_pairs={{0,33},{1,32},{32,1},{33,0},{64,97},{65,96},{96,65},{97,64},{2,35}... | collective-permute-start | bytes 196616 | tf_op jit(solution)/shard_map/ppermute | solution.py:416
  73.8 9.9 %collective-permute-start.9 = (bf16[16,16,384]{2,1,0:T(8,128)(2,1)S(1)}, bf16[16,16,384]{2,1,0:T(8,128)(2,1)S(1)}, u32[]{:S(2)}, u32[]{:S(2)}) collective-permute-start(bf16[16,16,384]{2,1,0:T(8,128)(2,1)S(1)} %get-tuple-element.40), channel_id=1, source_target_pairs={{0,1},{1,0},{2,3},{3,2},{4,5},{5,4},{6,7},{7,6},{8,9},{9,8},{10,11... | collective-permute-start | bytes 589832 | tf_op jit(solution)/shard_map/ppermute | solution.py:410
  74.0 16.3 %collective-permute-start.7 = (bf16[16,32,384]{2,1,0:T(8,128)(2,1)S(1)}, bf16[16,32,384]{2,1,0:T(8,128)(2,1)S(1)}, u32[]{:S(2)}, u32[]{:S(2)}) collective-permute-start(bf16[16,32,384]{2,1,0:T(8,128)(2,1)S(1)} %get-tuple-element.36), channel_id=1, source_target_pairs={{0,96},{96,0},{32,64},{64,32},{1,97},{97,1},{33,65},{65,33},{2,98}... | collective-permute-start | bytes 1179656 | tf_op jit(solution)/shard_map/ppermute | solution.py:402
  83.2 1.6 %collective-permute-start.8 = (bf16[16,16,384]{2,1,0:T(8,128)(2,1)S(1)}, bf16[16,16,384]{2,1,0:T(8,128)(2,1)S(1)}, u32[]{:S(2)}, u32[]{:S(2)}) collective-permute-start(bf16[16,16,384]{2,1,0:T(8,128)(2,1)S(1)} %get-tuple-element.38), channel_id=1, source_target_pairs={{0,1},{1,0},{2,3},{3,2},{4,5},{5,4},{6,7},{7,6},{8,9},{9,8},{10,11... | collective-permute-start | bytes 589832 | tf_op jit(solution)/shard_map/ppermute | solution.py:410
  83.8 6.5 %collective-permute-start.10 = (bf16[16,16,384]{2,1,0:T(8,128)(2,1)S(1)}, bf16[16,16,384]{2,1,0:T(8,128)(2,1)S(1)}, u32[]{:S(2)}, u32[]{:S(2)}) collective-permute-start(bf16[16,16,384]{2,1,0:T(8,128)(2,1)S(1)} %meet.1), channel_id=1, source_target_pairs={{0,32},{32,0},{64,96},{96,64},{1,33},{33,1},{65,97},{97,65},{2,34}... | collective-permute-start | bytes 589832 | tf_op jit(solution)/shard_map/ppermute | solution.py:406

commit v10 on v8

--- a/solution.py
+++ b/solution.py
@@ -298,7 +298,7 @@
         dv_s[pl.ds(j0, TK), :] = dv.astype(dv_s.dtype)
         return 0
 
-    lax.fori_loop(0, ROWS // TK, one_chunk, 0, unroll=len(blocks) == 1)
+    lax.fori_loop(0, ROWS // TK, one_chunk, 0, unroll=len(blocks) <= 2)
     place4 = [shift(HD, cols, 0, dst) for _, cols, dst in WINDOWS]
     half = ROWS // 2
     if gives_dkv:
@@ -432,11 +432,12 @@
     rows = rows_of(queries, keys)
     dq, keys_there = grads(1, (0, 1, 2, 3), rows, statistics, gives_dq=True)
     keys_got = over_a(keys_there)
-    core, beside, both, *dkv = grads(0, (1, 2, 3), rows, statistics, dq, gives_dkv=False)
-    core_got, both_got = over_core(core), over_core(both)
+    beside, both, *dkv = grads(0, (2, 3), rows, statistics, dq, gives_dkv=False)
+    both_got = over_core(both)
     send = meet(beside, both_got)
     beside_got = over_b(send)
-    own, keys_here = grads(0, (0,), rows, statistics, dq, dkv)
+    own, core, keys_here = grads(0, (0, 1), rows, statistics, dq, dkv)
+    core_got = over_core(core)
     total = combine([keys_here, keys_got, own, core_got, beside_got])
     total = to_heads(total)
     return tuple(finish(total))

time: 106 us -> 107 us (level)
  waiting for transfers between devices: 10.7 us -> 11.8 us
    ppermute x3, waiting for transfers between devices: 4.99 us -> 8.96 us  [over_b(): return lax.ppermute(x, Z, ((0, 1), (1, 0), (2, 3), (3, 2)))]
    ppermute x2, waiting for transfers between devices: 5.73 us -> 1.94 us  [over_a(): return lax.ppermute(x, Z, ((0, 3), (3, 0), (1, 2), (2, 1)))]
  transfers between devices with their start and end apart: 11 -> 11, of which waited for: 4 -> 6; matrix products, arithmetic and copies ran while one was open for 0% -> 0% of each run, Pallas kernels for 8% -> 11%
where the time goes in v10:
time: 107 us; the launch traced here: 106 us
  Pallas kernels  42 us (39%)
  blocking collectives  35.2 us (33%)
  starting transfers between devices  15.6 us (15%)
  waiting for transfers between devices  11.8 us (11%)
    all_to_all x2, blocking collectives, to_heads(): return lax.all_to_all(x, HEADS, 0, 0, tiled=True)  35.2 us
    pallas_call x3, Pallas kernels, grads(): pl.pallas_call(functools.partial(grads_kernel, key_block, blocks, dq is n...  23.4 us
    ppermute x3, waiting for transfers between devices, over_b(): return lax.ppermute(x, Z, ((0, 1), (1, 0), (2, 3), (3, 2)))  8.96 us
    pallas_call x1, Pallas kernels, stats(): pl.pallas_call(stats_kernel, out_shape=pltpu.VMEM((8, NQ // 2), F32), in_...  8.78 us
    ppermute x6, starting transfers between devices, over_core(): return lax.ppermute(x, CORE, ((0, 1), (1, 0)))  7.56 us
    ppermute x2, starting transfers between devices, over_a(): return lax.ppermute(x, Z, ((0, 3), (3, 0), (1, 2), (2, 1)))  5.08 us
    pallas_call x1, Pallas kernels, first_stats(): pl.pallas_call(first_stats_kernel, out_shape=[pltpu.VMEM((8, NQ // 2), F3...  3.43 us
    pallas_call x1, Pallas kernels, pack(): pl.pallas_call(pack_kernel, out_shape=jax.ShapeDtypeStruct((H, PD, WIDE),...  3.4 us
  transfers between devices with their start and end apart: 11, of which 6 were waited for; matrix products, arithmetic and copies ran while one was open for 0% of the time, Pallas kernels for 11%

profile of v10, /device:TPU:1, one launch (start us, length us, event | category | flops | bytes accessed | tf_op | source)
XLA Modules:
  0.0 105.6 jit_solution(14183147967718465419)
XLA Ops:
  0.7 3.4 %pack.1 = bf16[16,64,384]{2,1,0:T(8,128)(2,1)S(1)} custom-call(s32[512]{0:T(512)} %order_ref.1, s32[2]{0:T(128)S(1)} %pad_add_fusion.place_ref, bf16[64,1536]{1,0:T(8,128)(2,1)} %q_ref.1, bf16[64,1536]{1,0:T(8,128)(2,1)} %g_ref.1, bf16[512,1536]{1,0:T(8,128)(2,1)} %k_ref.1, bf16[512,1536]{1,0:T(8,128)(2,1)} %v_ref.1), custom_call_target="tpu_custom_call" | custom-call | tf_op jit(solution)/shard_map/pack/pallas_call | solution.py:108
  4.1 20.9 %all_to_all.10 = bf16[16,64,384]{2,1,0:T(8,128)(2,1)S(1)} all-to-all(bf16[16,64,384]{2,1,0:T(8,128)(2,1)S(1)} %pack.1), channel_id=1, replica_groups=mesh['blk_0'=4,'blk_1'=2,'grp_0'=2,'grp_1'=4,'grp_2'=2] {'blk_1','grp_0'..., dimensions={0} | all-to-all | bytes 1572864 | tf_op jit(solution)/shard_map/all_to_all | solution.py:414
  25.1 1.7 %collective-permute-start.1 = (bf16[16,32,384]{2,1,0:T(8,128)(2,1)S(1)}, bf16[16,32,384]{2,1,0:T(8,128)(2,1)S(1)}, u32[]{:S(2)}, u32[]{:S(2)}) collective-permute-start(bf16[16,32,384]{2,1,0:T(8,128)(2,1)S(1)} %get-tuple-element.42.refs_0_.qa_ref), channel_id=1, source_target_pairs={{0,32},{32,0},{64,96},{96,64},{1,33},{33,1},{65,97},{97,65},{2,34}... | collective-permute-start | bytes 1179656 | tf_op jit(solution)/shard_map/ppermute | solution.py:406
  26.8 2.1 %collective-permute-start = (bf16[16,32,384]{2,1,0:T(8,128)(2,1)S(1)}, bf16[16,32,384]{2,1,0:T(8,128)(2,1)S(1)}, u32[]{:S(2)}, u32[]{:S(2)}) collective-permute-start(bf16[16,32,384]{2,1,0:T(8,128)(2,1)S(1)} %get-tuple-element.42.refs_0_.qa_ref), channel_id=1, source_target_pairs={{0,1},{1,0},{2,3},{3,2},{4,5},{5,4},{6,7},{7,6},{8,9},{9,8},{10,11... | collective-permute-start | bytes 1179656 | tf_op jit(solution)/shard_map/ppermute | solution.py:410
  28.9 2.2 %collective-permute-start.3 = (bf16[16,32,384]{2,1,0:T(8,128)(2,1)S(1)}, bf16[16,32,384]{2,1,0:T(8,128)(2,1)S(1)}, u32[]{:S(2)}, u32[]{:S(2)}) collective-permute-start(bf16[16,32,384]{2,1,0:T(8,128)(2,1)S(1)} %get-tuple-element.41.refs_4_.kv_ref), channel_id=1, source_target_pairs={{0,96},{96,0},{32,64},{64,32},{1,97},{97,1},{33,65},{65,33},{2,98}... | collective-permute-start | bytes 1179656 | tf_op jit(solution)/shard_map/ppermute | solution.py:402
  31.1 3.3 %collective-permute-done.1.refs_2_.qa_ref = bf16[16,32,384]{2,1,0:T(8,128)(2,1)S(1)} collective-permute-done((bf16[16,32,384]{2,1,0:T(8,128)(2,1)S(1)}, bf16[16,32,384]{2,1,0:T(8,128)(2,1)S(1)}, u32[]{:S(2)}, u32[]{:S(2)}) %collective-permute-start.1) | collective-permute-done | bytes 393248 | tf_op jit(solution)/shard_map/ppermute | solution.py:406
  34.4 2.5 %collective-permute-start.2 = (bf16[16,32,384]{2,1,0:T(8,128)(2,1)S(1)}, bf16[16,32,384]{2,1,0:T(8,128)(2,1)S(1)}, u32[]{:S(2)}, u32[]{:S(2)}) collective-permute-start(bf16[16,32,384]{2,1,0:T(8,128)(2,1)S(1)} %collective-permute-done.1.refs_2_.qa_ref), channel_id=1, source_target_pairs={{0,1},{1,0},{2,3},{3,2},{4,5},{5,4},{6,7},{7,6},{8,9},{9,8},{10,11... | collective-permute-start | bytes 1179656 | tf_op jit(solution)/shard_map/ppermute | solution.py:410
  36.9 3.4 %first_stats.1 = (f32[8,2048]{1,0:T(8,128)S(1)}, bf16[128,2048]{1,0:T(8,128)(2,1)S(1)}, bf16[128,2048]{1,0:T(8,128)(2,1)S(1)}, bf16[1024,128]{1,0:T(8,128)(2,1)S(1)}, bf16[1024,128]{1,0:T(8,128)(2,1)S(1)}) custom-call(bf16[16,32,384]{2,1,0:T(8,128)(2,1)S(1)} %get-tuple-element.42.refs_0_.qa_ref, ...), custom_call_target="tpu_custom_call" | custom-call | flops 2147483648 | bytes 2097152 | tf_op jit(solution)/shard_map/first_stats/pallas_call | solution.py:173
  40.3 0.4 collective-permute-done.3.refs_5_.kv_ref
  40.8 8.8 %stats.1.refs_5_ = f32[8,2048]{1,0:T(8,128)S(1)} custom-call(bf16[16,32,384]{2,1,0:T(8,128)(2,1)S(1)} %collective-permute-done.1.refs_2_.qa_ref, bf16[16,32,384]{2,1,0:T(8,128)(2,1)S(1)} %collective-permute-done.2.refs_3_.qb_ref, bf16[16,32,384]{2,1,0:T(8,128)(2,1)S(1)} %collective-permute-done.3.refs_5_.kv_ref, f32[8,2048]{1,0:T(8,128)S(1)} %get-tuple-element.27.part_ref, ...), custom_call_target="tpu_custom_call" | custom-call | flops 6442450944 | bytes 4194304 | tf_op jit(solution)/shard_map/stats/pallas_call | solution.py:208
  49.6 1.1 %collective-permute-start.5 = (f32[8,2048]{1,0:T(8,128)S(1)}, f32[8,2048]{1,0:T(8,128)S(1)}, u32[]{:S(2)}, u32[]{:S(2)}) collective-permute-start(f32[8,2048]{1,0:T(8,128)S(1)} %stats.1.refs_5_), channel_id=1, source_target_pairs={{0,32},{32,0},{64,96},{96,64},{1,33},{33,1},{65,97},{97,65},{2,34}... | collective-permute-start | bytes 196616 | tf_op jit(solution)/shard_map/ppermute | solution.py:406
  51.1 1.7 %collective-permute-done.5.refs_7_ = f32[8,2048]{1,0:T(8,128)S(1)} collective-permute-done((f32[8,2048]{1,0:T(8,128)S(1)}, f32[8,2048]{1,0:T(8,128)S(1)}, u32[]{:S(2)}, u32[]{:S(2)}) %collective-permute-start.5) | collective-permute-done | bytes 65568 | tf_op jit(solution)/shard_map/ppermute | solution.py:406
  52.8 2.0 %collective-permute-start.6 = (f32[8,2048]{1,0:T(8,128)S(1)}, f32[8,2048]{1,0:T(8,128)S(1)}, u32[]{:S(2)}, u32[]{:S(2)}) collective-permute-start(f32[8,2048]{1,0:T(8,128)S(1)} %collective-permute-done.5.refs_7_), channel_id=1, source_target_pairs={{0,1},{1,0},{2,3},{3,2},{4,5},{5,4},{6,7},{7,6},{8,9},{9,8},{10,11... | collective-permute-start | bytes 196616 | tf_op jit(solution)/shard_map/ppermute | solution.py:410
  54.8 1.6 %rows_of.1 = (bf16[4096,128]{1,0:T(8,128)(2,1)S(1)}, bf16[4096,128]{1,0:T(8,128)(2,1)S(1)}, bf16[2048,128]{1,0:T(8,128)(2,1)S(1)}, bf16[2048,128]{1,0:T(8,128)(2,1)S(1)}, bf16[96,2048]{1,0:T(8,128)(2,1)S(1)}) custom-call(bf16[16,32,384]{2,1,0:T(8,128)(2,1)S(1)} %get-tuple-element.42.refs_0_.qa_ref, ...), custom_call_target="tpu_custom_call" | custom-call | tf_op jit(solution)/shard_map/rows_of/pallas_call | solution.py:231
  56.4 11.6 %shard_map.76 = (f32[96,4096]{1,0:T(8,128)S(1)}, bf16[16,32,384]{2,1,0:T(8,128)(2,1)S(1)}) custom-call(bf16[4096,128]{1,0:T(8,128)(2,1)S(1)} %get-tuple-element.22.refs_0_, bf16[4096,128]{1,0:T(8,128)(2,1)S(1)} %get-tuple-element.23.refs_1_, bf16[2048,128]{1,0:T(8,128)(2,1)S(1)} %get-tuple-element.24.refs_2_, ...), custom_call_target="tpu_custom_call" | custom-call | flops 10737418240 | bytes 1048576 | tf_op jit(solution)/shard_map/pallas_call | solution.py:325
  68.0 5.8 %shard_map.77 = (bf16[16,16,384]{2,1,0:T(8,128)(2,1)S(1)}, bf16[16,16,384]{2,1,0:T(8,128)(2,1)S(1)}, f32[1024,128]{1,0:T(8,128)S(1)}, f32[1024,128]{1,0:T(8,128)S(1)}) custom-call(bf16[4096,128]{1,0:T(8,128)(2,1)S(1)} %get-tuple-element.22.refs_0_, bf16[4096,128]{1,0:T(8,128)(2,1)S(1)} %get-tuple-element.23.refs_1_, ...), custom_call_target="tpu_custom_call" | custom-call | flops 5368709120 | bytes 1048576 | tf_op jit(solution)/shard_map/pallas_call | solution.py:325
  73.9 2.8 %collective-permute-start.7 = (bf16[16,32,384]{2,1,0:T(8,128)(2,1)S(1)}, bf16[16,32,384]{2,1,0:T(8,128)(2,1)S(1)}, u32[]{:S(2)}, u32[]{:S(2)}) collective-permute-start(bf16[16,32,384]{2,1,0:T(8,128)(2,1)S(1)} %get-tuple-element.36), channel_id=1, source_target_pairs={{0,96},{96,0},{32,64},{64,32},{1,97},{97,1},{33,65},{65,33},{2,98}... | collective-permute-start | bytes 1179656 | tf_op jit(solution)/shard_map/ppermute | solution.py:402
  76.8 6.0 %shard_map.78 = (bf16[16,16,384]{2,1,0:T(8,128)(2,1)S(1)}, bf16[16,16,384]{2,1,0:T(8,128)(2,1)S(1)}, bf16[16,32,384]{2,1,0:T(8,128)(2,1)S(1)}) custom-call(bf16[4096,128]{1,0:T(8,128)(2,1)S(1)} %get-tuple-element.22.refs_0_, bf16[4096,128]{1,0:T(8,128)(2,1)S(1)} %get-tuple-element.23.refs_1_, bf16[2048,128]{1,0:T(8,128)(2,1)S(1)} %get-tuple-element.24.refs_2_, ...), custom_call_target="tpu_custom_call" | custom-call | flops 5368709120 | bytes 1048576 | tf_op jit(solution)/shard_map/pallas_call | solution.py:325
  82.8 0.6 collective-permute-start.8
  83.5 0.9 collective-permute-done.8.refs_3_
  84.4 1.5 %collective-permute-done.7.refs_1_ = bf16[16,32,384]{2,1,0:T(8,128)(2,1)S(1)} collective-permute-done((bf16[16,32,384]{2,1,0:T(8,128)(2,1)S(1)}, bf16[16,32,384]{2,1,0:T(8,128)(2,1)S(1)}, u32[]{:S(2)}, u32[]{:S(2)}) %collective-permute-start.7) | collective-permute-done | bytes 393248 | tf_op jit(solution)/shard_map/ppermute | solution.py:402
  85.9 4.0 %collective-permute-done.10.refs_4_ = bf16[16,16,384]{2,1,0:T(8,128)(2,1)S(1)} collective-permute-done((bf16[16,16,384]{2,1,0:T(8,128)(2,1)S(1)}, bf16[16,16,384]{2,1,0:T(8,128)(2,1)S(1)}, u32[]{:S(2)}, u32[]{:S(2)}) %collective-permute-start.10) | collective-permute-done | bytes 196640 | tf_op jit(solution)/shard_map/ppermute | solution.py:406
  90.0 14.3 %all_to_all.11.got_ref = bf16[16,48,384]{2,1,0:T(8,128)(2,1)S(1)} all-to-all(bf16[16,48,384]{2,1,0:T(8,128)(2,1)S(1)} %combine.1), channel_id=1, replica_groups=mesh['blk_0'=4,'blk_1'=2,'grp_0'=2,'grp_1'=4,'grp_2'=2] {'blk_1','grp_0'..., dimensions={0} | all-to-all | bytes 1179648 | tf_op jit(solution)/shard_map/all_to_all | solution.py:414
  104.4 1.2 %finish.1 = (bf16[64,1536]{1,0:T(8,128)(2,1)}, bf16[64,1536]{1,0:T(8,128)(2,1)}, bf16[64,1536]{1,0:T(8,128)(2,1)}) custom-call(bf16[16,48,384]{2,1,0:T(8,128)(2,1)S(1)} %all_to_all.11.got_ref), custom_call_target="tpu_custom_call" | custom-call | tf_op jit(solution)/shard_map/finish/pallas_call | solution.py:391
  (12 shorter events, 1.0 us)
Async XLA Ops:
  25.1 9.3 %collective-permute-start.1 = (bf16[16,32,384]{2,1,0:T(8,128)(2,1)S(1)}, bf16[16,32,384]{2,1,0:T(8,128)(2,1)S(1)}, u32[]{:S(2)}, u32[]{:S(2)}) collective-permute-start(bf16[16,32,384]{2,1,0:T(8,128)(2,1)S(1)} %get-tuple-element.42.refs_0_.qa_ref), channel_id=1, source_target_pairs={{0,32},{32,0},{64,96},{96,64},{1,33},{33,1},{65,97},{97,65},{2,34}... | collective-permute-start | bytes 1179656 | tf_op jit(solution)/shard_map/ppermute | solution.py:406
  26.8 10.1 %collective-permute-start = (bf16[16,32,384]{2,1,0:T(8,128)(2,1)S(1)}, bf16[16,32,384]{2,1,0:T(8,128)(2,1)S(1)}, u32[]{:S(2)}, u32[]{:S(2)}) collective-permute-start(bf16[16,32,384]{2,1,0:T(8,128)(2,1)S(1)} %get-tuple-element.42.refs_0_.qa_ref), channel_id=1, source_target_pairs={{0,1},{1,0},{2,3},{3,2},{4,5},{5,4},{6,7},{7,6},{8,9},{9,8},{10,11... | collective-permute-start | bytes 1179656 | tf_op jit(solution)/shard_map/ppermute | solution.py:410
  28.9 11.9 %collective-permute-start.3 = (bf16[16,32,384]{2,1,0:T(8,128)(2,1)S(1)}, bf16[16,32,384]{2,1,0:T(8,128)(2,1)S(1)}, u32[]{:S(2)}, u32[]{:S(2)}) collective-permute-start(bf16[16,32,384]{2,1,0:T(8,128)(2,1)S(1)} %get-tuple-element.41.refs_4_.kv_ref), channel_id=1, source_target_pairs={{0,96},{96,0},{32,64},{64,32},{1,97},{97,1},{33,65},{65,33},{2,98}... | collective-permute-start | bytes 1179656 | tf_op jit(solution)/shard_map/ppermute | solution.py:402
  34.4 6.3 %collective-permute-start.2 = (bf16[16,32,384]{2,1,0:T(8,128)(2,1)S(1)}, bf16[16,32,384]{2,1,0:T(8,128)(2,1)S(1)}, u32[]{:S(2)}, u32[]{:S(2)}) collective-permute-start(bf16[16,32,384]{2,1,0:T(8,128)(2,1)S(1)} %collective-permute-done.1.refs_2_.qa_ref), channel_id=1, source_target_pairs={{0,1},{1,0},{2,3},{3,2},{4,5},{5,4},{6,7},{7,6},{8,9},{9,8},{10,11... | collective-permute-start | bytes 1179656 | tf_op jit(solution)/shard_map/ppermute | solution.py:410
  49.6 3.2 %collective-permute-start.5 = (f32[8,2048]{1,0:T(8,128)S(1)}, f32[8,2048]{1,0:T(8,128)S(1)}, u32[]{:S(2)}, u32[]{:S(2)}) collective-permute-start(f32[8,2048]{1,0:T(8,128)S(1)} %stats.1.refs_5_), channel_id=1, source_target_pairs={{0,32},{32,0},{64,96},{96,64},{1,33},{33,1},{65,97},{97,65},{2,34}... | collective-permute-start | bytes 196616 | tf_op jit(solution)/shard_map/ppermute | solution.py:406
  50.7 5.7 %collective-permute-start.4 = (f32[8,2048]{1,0:T(8,128)S(1)}, f32[8,2048]{1,0:T(8,128)S(1)}, u32[]{:S(2)}, u32[]{:S(2)}) collective-permute-start(f32[8,2048]{1,0:T(8,128)S(1)} %stats.1.refs_5_), channel_id=1, source_target_pairs={{0,1},{1,0},{2,3},{3,2},{4,5},{5,4},{6,7},{7,6},{8,9},{9,8},{10,11... | collective-permute-start | bytes 196616 | tf_op jit(solution)/shard_map/ppermute | solution.py:410
  52.8 3.7 %collective-permute-start.6 = (f32[8,2048]{1,0:T(8,128)S(1)}, f32[8,2048]{1,0:T(8,128)S(1)}, u32[]{:S(2)}, u32[]{:S(2)}) collective-permute-start(f32[8,2048]{1,0:T(8,128)S(1)} %collective-permute-done.5.refs_7_), channel_id=1, source_target_pairs={{0,1},{1,0},{2,3},{3,2},{4,5},{5,4},{6,7},{7,6},{8,9},{9,8},{10,11... | collective-permute-start | bytes 196616 | tf_op jit(solution)/shard_map/ppermute | solution.py:410
  73.8 9.5 %collective-permute-start.9 = (bf16[16,16,384]{2,1,0:T(8,128)(2,1)S(1)}, bf16[16,16,384]{2,1,0:T(8,128)(2,1)S(1)}, u32[]{:S(2)}, u32[]{:S(2)}) collective-permute-start(bf16[16,16,384]{2,1,0:T(8,128)(2,1)S(1)} %get-tuple-element.40), channel_id=1, source_target_pairs={{0,1},{1,0},{2,3},{3,2},{4,5},{5,4},{6,7},{7,6},{8,9},{9,8},{10,11... | collective-permute-start | bytes 589832 | tf_op jit(solution)/shard_map/ppermute | solution.py:410
  73.9 12.0 %collective-permute-start.7 = (bf16[16,32,384]{2,1,0:T(8,128)(2,1)S(1)}, bf16[16,32,384]{2,1,0:T(8,128)(2,1)S(1)}, u32[]{:S(2)}, u32[]{:S(2)}) collective-permute-start(bf16[16,32,384]{2,1,0:T(8,128)(2,1)S(1)} %get-tuple-element.36), channel_id=1, source_target_pairs={{0,96},{96,0},{32,64},{64,32},{1,97},{97,1},{33,65},{65,33},{2,98}... | collective-permute-start | bytes 1179656 | tf_op jit(solution)/shard_map/ppermute | solution.py:402
  82.8 1.6 %collective-permute-start.8 = (bf16[16,16,384]{2,1,0:T(8,128)(2,1)S(1)}, bf16[16,16,384]{2,1,0:T(8,128)(2,1)S(1)}, u32[]{:S(2)}, u32[]{:S(2)}) collective-permute-start(bf16[16,16,384]{2,1,0:T(8,128)(2,1)S(1)} %get-tuple-element.38), channel_id=1, source_target_pairs={{0,1},{1,0},{2,3},{3,2},{4,5},{5,4},{6,7},{7,6},{8,9},{9,8},{10,11... | collective-permute-start | bytes 589832 | tf_op jit(solution)/shard_map/ppermute | solution.py:410
  83.4 6.5 %collective-permute-start.10 = (bf16[16,16,384]{2,1,0:T(8,128)(2,1)S(1)}, bf16[16,16,384]{2,1,0:T(8,128)(2,1)S(1)}, u32[]{:S(2)}, u32[]{:S(2)}) collective-permute-start(bf16[16,16,384]{2,1,0:T(8,128)(2,1)S(1)} %meet.1), channel_id=1, source_target_pairs={{0,32},{32,0},{64,96},{96,64},{1,33},{33,1},{65,97},{97,65},{2,34}... | collective-permute-start | bytes 589832 | tf_op jit(solution)/shard_map/ppermute | solution.py:406
